TPU v7x, 32 devices: a whole 2x2x4 slice. The times are simulated.
32 devices in a mesh: seq: 8 (over y, x, core), head: 4 (over z).
Axes of the slice: x: 2, y: 2, z: 4, core: 2. Of those that a mesh axis runs over, the one named last changes fastest.
Arguments:
- query: bfloat16 [2048, 4096], P('seq', 'head'), may hold values from -6 to 6
- key_in: bfloat16 [2048, 4096], P('seq', 'head'), may hold values from -6 to 6
- value: bfloat16 [2048, 4096], P('seq', 'head'), may hold values from -6 to 6
- gates: bfloat16 [2048, 4096], P('seq', 'head'), may hold values from -1 to 0
- beta: float32 [2048, 32], P('seq', 'head'), may hold values from 0 to 1
- conv_query: bfloat16 [4, 4096], P(None, 'head'), may hold values from -3 to 3
- conv_key: bfloat16 [4, 4096], P(None, 'head'), may hold values from -3 to 3
- conv_value: bfloat16 [4, 4096], P(None, 'head'), may hold values from -3 to 3
- out_weight: bfloat16 [4096, 2304], P('head'), may hold values from -0.75 to 0.75
Outputs:
- mixed: bfloat16 [2048, 2304], P(('seq', 'head'))
All inputs are finite; a program needn't handle non-finite values.
Results may differ from a plain program's by a relative error of at most 0.0049.
Values may be sent and summed in bfloat16 or wider, within the bound.
No kernel may reach another device: no remote copies, remote signals or barrier semaphores. Data moves between devices by JAX's collectives and lax.ppermute only.
A program may use at most 128 MiB of HBM per device.

v0:
```python
import jax
import jax.numpy as jnp
from jax import lax
from jax.sharding import PartitionSpec as P

DK = 128
BLOCK = 64


def from_behind(block, axis, distance):
    devices = range(lax.axis_size(axis))
    route = [(i - distance, i) for i in devices if i - distance in devices]
    return lax.ppermute(block, axis, route)


def matmul(left, right):
    return jnp.einsum("...ij,...jk->...ik", left, right, precision=lax.Precision.HIGHEST)


def block_terms(query, keys, values, retention_decay, beta):
    length = query.shape[-2]
    width = query.shape[-1]
    cumul = jnp.cumsum(retention_decay, axis=-2)
    final = cumul[..., -1:, :]
    forward = keys * jnp.exp(-cumul)
    backward = keys * jnp.exp(cumul)
    queried = query * jnp.exp(cumul)
    trailing = keys * jnp.exp(final - cumul)
    strict = jnp.tril(jnp.ones((length, length), jnp.float32), -1)
    inclusive = jnp.tril(jnp.ones((length, length), jnp.float32))
    identity = jnp.eye(length, dtype=jnp.float32)
    coupling = matmul(backward, jnp.swapaxes(forward, -1, -2))
    system = identity + beta[..., :, None] * coupling * strict
    right_sides = jnp.concatenate([beta[..., None] * values, beta[..., None] * backward], axis=-1)
    solved = jax.scipy.linalg.solve_triangular(system, right_sides, lower=True)
    direct_values = solved[..., :width]
    weighted = solved[..., width:]
    scores = matmul(queried, jnp.swapaxes(forward, -1, -2)) * inclusive
    transition = jnp.eye(width, dtype=jnp.float32) * jnp.swapaxes(jnp.exp(final), -1, -2) - matmul(
        jnp.swapaxes(trailing, -1, -2), weighted
    )
    offset = matmul(jnp.swapaxes(trailing, -1, -2), direct_values)
    direct = matmul(scores, direct_values)
    coefficient = queried - matmul(scores, weighted)
    return (transition, offset, direct, coefficient)


def conv_silu(data, before, weight):
    taps = weight.shape[0]
    count = data.shape[0]
    padded = jnp.concatenate([before.astype(jnp.float32), data.astype(jnp.float32)], axis=0)
    total = jnp.zeros((count, data.shape[1]), jnp.float32)
    for offset_index in range(taps):
        total = (
            total
            + weight[offset_index].astype(jnp.float32) * padded[offset_index : offset_index + count]
        )
    return jax.nn.silu(total)


def normalize(data):
    return data * lax.rsqrt(jnp.sum(data * data, axis=-1, keepdims=True) + 1e-06)


def shards(query, key_in, value, gates, beta, conv_query, conv_key, conv_value, out_weight):
    margin = conv_query.shape[0] - 1
    length = query.shape[0]
    groups = beta.shape[1]
    blocks = length // BLOCK
    rims = jnp.stack(
        [query[length - margin :], key_in[length - margin :], value[length - margin :]]
    )
    rims = from_behind(rims, "seq", 1)

    def split_heads(data):
        return jnp.transpose(data.reshape(blocks, BLOCK, groups, DK), (2, 0, 1, 3))

    query_heads = normalize(split_heads(conv_silu(query, rims[0], conv_query))) * DK ** (-0.5)
    key_heads = normalize(split_heads(conv_silu(key_in, rims[1], conv_key)))
    value_heads = split_heads(conv_silu(value, rims[2], conv_value))
    gate_heads = split_heads(gates.astype(jnp.float32))
    beta_heads = jnp.transpose(beta.reshape(blocks, BLOCK, groups), (2, 0, 1))
    transition, offset, direct, coefficient = block_terms(
        query_heads, key_heads, value_heads, gate_heads, beta_heads
    )

    def advance(carry, item):
        state, product = carry
        step_transition, step_offset = item
        return (
            (matmul(step_transition, state) + step_offset, matmul(step_transition, product)),
            (state, product),
        )

    identity = jnp.broadcast_to(jnp.eye(DK, dtype=jnp.float32), (groups, DK, DK))
    zeros = jnp.zeros((groups, DK, DK), jnp.float32)
    (final_state, final_product), (starts, products) = lax.scan(
        advance,
        (zeros, identity),
        (jnp.transpose(transition, (1, 0, 2, 3)), jnp.transpose(offset, (1, 0, 2, 3))),
    )
    starts = jnp.transpose(starts, (1, 0, 2, 3))
    products = jnp.transpose(products, (1, 0, 2, 3))
    local_out = direct + matmul(coefficient, starts)
    carried_coef = matmul(coefficient, products)

    def relay(step_index, arriving):
        return from_behind(matmul(final_product, arriving) + final_state, "seq", 1)

    incoming = lax.fori_loop(0, lax.axis_size("seq") - 1, relay, zeros)
    outputs = local_out + jnp.einsum(
        "hnic,hcd->hnid", carried_coef, incoming, precision=lax.Precision.HIGHEST
    )
    flat = jnp.transpose(outputs, (1, 2, 0, 3)).reshape(length, groups * DK).astype(jnp.bfloat16)
    mixed = lax.psum_scatter(
        jnp.dot(flat, out_weight, preferred_element_type=jnp.float32),
        "head",
        scatter_dimension=0,
        tiled=True,
    )
    return mixed.astype(jnp.bfloat16)


def solution(mesh):
    in_specs = (
        P("seq", "head"),
        P("seq", "head"),
        P("seq", "head"),
        P("seq", "head"),
        P("seq", "head"),
        P(None, "head"),
        P(None, "head"),
        P(None, "head"),
        P("head", None),
    )
    out_specs = P(("seq", "head"), None)
    return jax.shard_map(shards, mesh=mesh, in_specs=in_specs, out_specs=out_specs, check_vma=False)
```

profile of v0, /device:TPU:0, one launch (start us, length us, event | category | flops | bytes accessed | tf_op | source)
XLA Modules:
  0.0 386.7 jit_solution(4107834376364706326)
XLA Ops:
  6.5 0.7 slice_bitcast_fusion.6
  7.3 0.7 slice_bitcast_fusion.4
  8.0 2.4 collective-permute-start.1
  10.5 1.1 convert_bitcast_fusion
  13.0 1.1 convert_element_type.83
  14.1 1.1 convert_element_type.90
  15.3 0.6 multiply_bitcast_fusion.1
  16.1 0.4 fusion.53
  16.5 0.6 copy-done.8
  17.2 0.6 multiply_bitcast_fusion.2
  18.0 1.0 copy-done
  19.0 0.4 fusion.56
  19.4 0.6 multiply_bitcast_fusion
  20.2 2.5 bitcast_multiply_fusion
  22.8 4.1 %fusion.25 = f32[8,4,1,64,64]{4,3,2,1,0:T(8,128)} fusion(f32[64,64]{1,0:T(8,128)S(1)} %fusion.72, f32[8,4,64]{2,1,0:T(4,128)S(1)} %bitcast.179, f32[64,64]{1,0:T(8,128)S(1)} %get-tuple-element.156, pred[64,64]{1,0:T(8,128)(4,1)S(1)} %get-tuple-element.155, f32[8,4,64,128]{3,0,1,2:T(8,128)S(1)} %fusion.54, f32[4,64,8,128]{3,2,1,0:T(8,128)S(1)} %bitcast.168, ...), kind=kOutput, calls=%fused_computation.39 | convolution fusion | flops 203161600 | bytes 2674688 | tf_op jit(solution)/shard_map/...ij,...jk->...ik/dot_general | solution.py:17
  26.9 158.7 %custom-call.4 = f32[8,4,1,64,64]{3,4,2,1,0:T(8,128)} custom-call(f32[8,4,1,64,64]{4,3,2,1,0:T(8,128)} %fusion.25), custom_call_target="InvertDiagBlocksLowerTriangular" | custom-call | tf_op jit(solution)/shard_map/jit(_solve_triangular)/vmap(vmap())/triangular_solve | solution.py:35
  185.6 4.8 %convolution_multiply_fusion.1 = f32[8,4,64,64]{3,2,1,0:T(8,128)S(1)} fusion(f32[64,64]{1,0:T(8,128)S(1)} %broadcast_select_fusion, f32[8,4,64,128]{3,0,1,2:T(8,128)S(1)} %fusion.54, f32[4,64,8,128]{3,2,1,0:T(8,128)S(1)} %bitcast.169, f32[8,4,64]{2,1,0:T(4,128)S(1)} %add_rsqrt_fusion, f32[4,64,8,128]{3,2,1,0:T(8,128)} %bitcast.173, ...), kind=kOutput, calls=%fused_computation.36 | convolution fusion | flops 203030528 | bytes 3702784 | tf_op jit(solution)/shard_map/...ij,...jk->...ik/dot_general | solution.py:17
  190.4 2.0 fusion.11
  192.4 2.3 fusion.63
  194.7 3.3 convolution_subtract_fusion
  198.0 5.6 %convolution_bitcast_fusion = f32[4,8,128,128]{3,2,0,1:T(8,128)} fusion(f32[8,4,64,256]{3,2,1,0:T(8,128)S(1)} %fusion.11, f32[8,4,64,128]{3,0,1,2:T(8,128)S(1)} %fusion.54, f32[4,64,8,128]{3,2,1,0:T(8,128)S(1)} %bitcast.170, f32[8,4,128]{2,1,0:T(4,128)S(1)} %copy.28, f32[8,4,64]{2,1,0:T(4,128)S(1)} %add_rsqrt_fusion), kind=kOutput, calls=%fused_computation.24 | convolution fusion | flops 403439616 | bytes 5275648 | tf_op jit(solution)/shard_map/...ij,...jk->...ik/dot_general | solution.py:17
  203.6 5.8 %bitcast_subtract_fusion = f32[4,8,128,128]{3,2,0,1:T(8,128)} fusion(f32[4,8,128]{2,0,1:T(4,128)S(1)} %copy.27, f32[128,128]{1,0:T(8,128)S(1)} %fusion.70, f32[8,4,64,256]{3,2,1,0:T(8,128)S(1)} %fusion.11, f32[8,4,64,128]{3,0,1,2:T(8,128)S(1)} %fusion.54, f32[4,64,8,128]{3,2,1,0:T(8,128)S(1)} %bitcast.171, f32[8,4,128]{2,1,0:T(4,128)S(1)} %copy.28, ...), kind=kOutput, calls=%fused_computation.19 | convolution fusion | flops 404488192 | bytes 5357568 | tf_op jit(solution)/shard_map/...ij,...jk->...ik/dot_general | solution.py:17
  209.4 18.9 %while.28 = (s32[]{:T(128)}, f32[8,128,128]{2,1,0:T(8,128)S(1)}, f32[8,128,128]{2,1,0:T(8,128)S(1)}, f32[4,8,128,128]{3,2,1,0:T(8,128)}, f32[4,8,128,128]{3,2,1,...) while((s32[]{:T(128)}, f32[8,128,128]{2,1,0:T(8,128)S(1)}, ...), condition=%wide.region_4.5_spmd.clone, body=%wide.region_3.4_spmd.clone.sunk | while | flops 403046400 | bytes 7865975 | solution.py:97
  209.6 1.1 bitcast_dynamic-update-slice_fusion.3
  210.6 1.8 convolution_add_fusion.6
  212.5 1.7 fusion.103
  214.3 1.0 bitcast_dynamic-update-slice_fusion.3
  215.3 1.8 convolution_add_fusion.6
  217.2 1.7 fusion.103
  219.0 1.1 bitcast_dynamic-update-slice_fusion.3
  220.0 1.8 convolution_add_fusion.6
  221.9 1.7 fusion.103
  223.7 1.1 bitcast_dynamic-update-slice_fusion.3
  224.8 1.8 convolution_add_fusion.6
  226.6 1.7 fusion.103
  228.4 4.7 %fusion.15 = f32[8,4,64,128]{3,2,1,0:T(8,128)} fusion(f32[8,4,64,128]{3,2,1,0:T(8,128)S(1)} %copy-done.2, f32[4,8,128,128]{3,2,1,0:T(8,128)} %get-tuple-element.68), kind=kOutput, calls=%fused_computation.20 | convolution fusion | flops 402653184 | bytes 4194304 | tf_op jit(solution)/shard_map/...ij,...jk->...ik/dot_general | solution.py:17
  233.1 3.1 fusion.19
  236.2 71.2 %while.27 = (s32[]{:T(128)}, f32[8,128,128]{2,1,0:T(8,128)S(1)}, f32[8,128,128]{2,1,0:T(8,128)S(1)}, f32[8,128,128]{2,1,0:T(8,128)S(1)}, s32[]{:T(128)}) while((s32[]{:T(128)}, f32[8,128,128]{2,1,0:T(8,128)S(1)}, f32[8,128,128]{2,1,0:T(8,128)S(1)}, f32[8,128,128]{2,1,0:T(8,128)S(1)}, s32[]{:T(128)}) %tuple.58), condition=%wide.region_6.7_spmd, body=%wide.region_5.6_spmd.sunk | while | flops 201457664 | bytes 4194405 | solution.py:110
  236.2 0.6 convolution_add_fusion.5
  236.9 4.5 %collective-permute-start = (f32[8,128,128]{2,1,0:T(8,128)S(1)}, f32[8,128,128]{2,1,0:T(8,128)S(1)}, u32[]{:S(2)}, u32[]{:S(2)}) collective-permute-start(f32[8,128,128]{2,1,0:T(8,128)S(1)} %convolution_add_fusion.5), channel_id=1, source_target_pairs={{0,4},{4,8},{8,12},{12,16},{16,20},{20,24},{24,28},{1,5},{5,9},{9,... | collective-permute-start | bytes 1572872 | tf_op jit(solution)/shard_map/while/body/eval_jaxpr/ppermute | solution.py:13
  241.4 1.5 collective-permute-done
  242.9 0.6 convolution_add_fusion.5
  243.6 6.5 %collective-permute-start = (f32[8,128,128]{2,1,0:T(8,128)S(1)}, f32[8,128,128]{2,1,0:T(8,128)S(1)}, u32[]{:S(2)}, u32[]{:S(2)}) collective-permute-start(f32[8,128,128]{2,1,0:T(8,128)S(1)} %convolution_add_fusion.5), channel_id=1, source_target_pairs={{0,4},{4,8},{8,12},{12,16},{16,20},{20,24},{24,28},{1,5},{5,9},{9,... | collective-permute-start | bytes 1572872 | tf_op jit(solution)/shard_map/while/body/eval_jaxpr/ppermute | solution.py:13
  250.1 1.5 collective-permute-done
  251.6 0.6 convolution_add_fusion.5
  252.3 9.0 %collective-permute-start = (f32[8,128,128]{2,1,0:T(8,128)S(1)}, f32[8,128,128]{2,1,0:T(8,128)S(1)}, u32[]{:S(2)}, u32[]{:S(2)}) collective-permute-start(f32[8,128,128]{2,1,0:T(8,128)S(1)} %convolution_add_fusion.5), channel_id=1, source_target_pairs={{0,4},{4,8},{8,12},{12,16},{16,20},{20,24},{24,28},{1,5},{5,9},{9,... | collective-permute-start | bytes 1572872 | tf_op jit(solution)/shard_map/while/body/eval_jaxpr/ppermute | solution.py:13
  261.3 1.5 collective-permute-done
  262.8 0.6 convolution_add_fusion.5
  263.4 9.0 %collective-permute-start = (f32[8,128,128]{2,1,0:T(8,128)S(1)}, f32[8,128,128]{2,1,0:T(8,128)S(1)}, u32[]{:S(2)}, u32[]{:S(2)}) collective-permute-start(f32[8,128,128]{2,1,0:T(8,128)S(1)} %convolution_add_fusion.5), channel_id=1, source_target_pairs={{0,4},{4,8},{8,12},{12,16},{16,20},{20,24},{24,28},{1,5},{5,9},{9,... | collective-permute-start | bytes 1572872 | tf_op jit(solution)/shard_map/while/body/eval_jaxpr/ppermute | solution.py:13
  272.4 1.5 collective-permute-done
  273.9 0.6 convolution_add_fusion.5
  274.6 9.0 %collective-permute-start = (f32[8,128,128]{2,1,0:T(8,128)S(1)}, f32[8,128,128]{2,1,0:T(8,128)S(1)}, u32[]{:S(2)}, u32[]{:S(2)}) collective-permute-start(f32[8,128,128]{2,1,0:T(8,128)S(1)} %convolution_add_fusion.5), channel_id=1, source_target_pairs={{0,4},{4,8},{8,12},{12,16},{16,20},{20,24},{24,28},{1,5},{5,9},{9,... | collective-permute-start | bytes 1572872 | tf_op jit(solution)/shard_map/while/body/eval_jaxpr/ppermute | solution.py:13
  283.6 1.5 collective-permute-done
  285.1 0.6 convolution_add_fusion.5
  285.7 9.0 %collective-permute-start = (f32[8,128,128]{2,1,0:T(8,128)S(1)}, f32[8,128,128]{2,1,0:T(8,128)S(1)}, u32[]{:S(2)}, u32[]{:S(2)}) collective-permute-start(f32[8,128,128]{2,1,0:T(8,128)S(1)} %convolution_add_fusion.5), channel_id=1, source_target_pairs={{0,4},{4,8},{8,12},{12,16},{16,20},{20,24},{24,28},{1,5},{5,9},{9,... | collective-permute-start | bytes 1572872 | tf_op jit(solution)/shard_map/while/body/eval_jaxpr/ppermute | solution.py:13
  294.7 1.5 collective-permute-done
  296.2 0.6 convolution_add_fusion.5
  296.9 9.0 %collective-permute-start = (f32[8,128,128]{2,1,0:T(8,128)S(1)}, f32[8,128,128]{2,1,0:T(8,128)S(1)}, u32[]{:S(2)}, u32[]{:S(2)}) collective-permute-start(f32[8,128,128]{2,1,0:T(8,128)S(1)} %convolution_add_fusion.5), channel_id=1, source_target_pairs={{0,4},{4,8},{8,12},{12,16},{16,20},{20,24},{24,28},{1,5},{5,9},{9,... | collective-permute-start | bytes 1572872 | tf_op jit(solution)/shard_map/while/body/eval_jaxpr/ppermute | solution.py:13
  305.9 1.5 collective-permute-done
  307.4 2.3 fusion.27
  309.7 0.3 copy.33
  310.0 5.2 %fusion.65 = f32[256,2304]{1,0:T(8,128)} fusion(bf16[1024,2304]{1,0:T(8,128)(2,1)} %param.21, bf16[32,8,8,128]{3,2,1,0:T(8,128)(2,1)S(1)} %bitcast.177), kind=kOutput, calls=%fused_computation.94 | convolution fusion | flops 1207959552 | bytes 7602176 | tf_op jit(solution)/shard_map/dot_general | solution.py:116
  315.2 62.8 %reduce-scatter.2.cloned.1.call-done = f32[64,2304]{1,0:T(8,128)} async-done(((f32[256,2304]{1,0:T(8,128)}), f32[64,2304]{1,0:T(8,128)}) %reduce-scatter.2.cloned.1.call-update) | async-done | bytes 589840 | tf_op jit(solution)/shard_map/reduce_scatter | solution.py:115
  378.0 1.8 convert_element_type.95
  (72 shorter events, 2.4 us)
Async XLA Ops:
  6.5 371.5 %reduce-scatter.2.cloned.1.call-start = ((), (), s32[]{:S(2)}) async-start(), calls=%async_computation.1 | async-start | bytes 2949120 | tf_op jit(solution)/shard_map/reduce_scatter | solution.py:115
  8.0 7.2 %collective-permute-start.1 = (bf16[3,3,1024]{2,1,0:T(4,128)(2,1)S(1)}, bf16[3,3,1024]{2,1,0:T(4,128)(2,1)S(1)}, u32[]{:S(2)}, u32[]{:S(2)}) collective-permute-start(bf16[3,3,1024]{2,1,0:T(4,128)(2,1)S(1)} %pad_maximum_fusion.3), channel_id=1, source_target_pairs={{0,4},{4,8},{8,12},{12,16},{16,20},{20,24},{24,28},{1,5},{5,9},{9,... | collective-permute-start | bytes 55304 | tf_op jit(solution)/shard_map/ppermute | solution.py:13
  11.6 0.7 copy-start.14
  11.6 0.7 copy-start.15
  11.6 0.7 copy-start.16
  11.6 1.1 copy-start.11
  11.9 1.1 copy-start.12
  12.3 1.8 copy-start.13
  12.7 2.5 copy-start.17
  15.9 1.2 copy-start.8
  17.8 1.6 copy-start.7
  18.0 1.0 copy-start
  185.6 4.8 %copy-start.5 = (f32[8,4,64,128]{3,2,1,0:T(8,128)S(1)}, f32[8,4,64,128]{3,2,1,0:T(8,128)}, u32[]{:S(2)}) copy-start(f32[8,4,64,128]{3,2,1,0:T(8,128)} %get-tuple-element.139) | copy-start | bytes 3145732
  185.6 4.8 %copy-start.6 = (f32[8,4,64,128]{3,2,1,0:T(8,128)S(1)}, f32[8,4,64,128]{3,2,1,0:T(8,128)}, u32[]{:S(2)}) copy-start(f32[8,4,64,128]{3,2,1,0:T(8,128)} %get-tuple-element.140) | copy-start | bytes 3145732
  185.6 4.8 %copy-start.10 = (f32[8,4,1,64,64]{3,4,2,1,0:T(8,128)S(1)}, f32[8,4,1,64,64]{3,4,2,1,0:T(8,128)}, u32[]{:S(2)}) copy-start(f32[8,4,1,64,64]{3,4,2,1,0:T(8,128)} %custom-call.4) | copy-start | bytes 1572868
  192.4 2.3 copy-start.1
  209.4 18.9 %copy-start.2 = (f32[8,4,64,128]{3,2,1,0:T(8,128)S(1)}, f32[8,4,64,128]{3,2,1,0:T(8,128)}, u32[]{:S(2)}) copy-start(f32[8,4,64,128]{3,2,1,0:T(8,128)} %convolution_subtract_fusion) | copy-start | bytes 3145732
  228.3 4.7 %copy-start.3 = (f32[8,4,64,128]{3,2,1,0:T(8,128)S(1)}, f32[8,4,64,128]{3,2,1,0:T(8,128)}, u32[]{:S(2)}) copy-start(f32[8,4,64,128]{3,2,1,0:T(8,128)} %fusion.63) | copy-start | bytes 3145732
  228.4 4.7 %copy-start.9 = (f32[4,8,128,128]{3,2,1,0:T(8,128)S(1)}, f32[4,8,128,128]{3,2,1,0:T(8,128)}, u32[]{:S(2)}) copy-start(f32[4,8,128,128]{3,2,1,0:T(8,128)} %get-tuple-element.67) | copy-start | bytes 6291460
  236.2 71.2 %copy-start.4 = (f32[8,4,64,128]{3,2,1,0:T(8,128)S(1)}, f32[8,4,64,128]{3,2,1,0:T(8,128)}, u32[]{:S(2)}) copy-start(f32[8,4,64,128]{3,2,1,0:T(8,128)} %fusion.19) | copy-start | bytes 3145732
  236.9 6.0 %collective-permute-start = (f32[8,128,128]{2,1,0:T(8,128)S(1)}, f32[8,128,128]{2,1,0:T(8,128)S(1)}, u32[]{:S(2)}, u32[]{:S(2)}) collective-permute-start(f32[8,128,128]{2,1,0:T(8,128)S(1)} %convolution_add_fusion.5), channel_id=1, source_target_pairs={{0,4},{4,8},{8,12},{12,16},{16,20},{20,24},{24,28},{1,5},{5,9},{9,... | collective-permute-start | bytes 1572872 | tf_op jit(solution)/shard_map/while/body/eval_jaxpr/ppermute | solution.py:13
  243.6 8.0 %collective-permute-start = (f32[8,128,128]{2,1,0:T(8,128)S(1)}, f32[8,128,128]{2,1,0:T(8,128)S(1)}, u32[]{:S(2)}, u32[]{:S(2)}) collective-permute-start(f32[8,128,128]{2,1,0:T(8,128)S(1)} %convolution_add_fusion.5), channel_id=1, source_target_pairs={{0,4},{4,8},{8,12},{12,16},{16,20},{20,24},{24,28},{1,5},{5,9},{9,... | collective-permute-start | bytes 1572872 | tf_op jit(solution)/shard_map/while/body/eval_jaxpr/ppermute | solution.py:13
  252.3 10.5 %collective-permute-start = (f32[8,128,128]{2,1,0:T(8,128)S(1)}, f32[8,128,128]{2,1,0:T(8,128)S(1)}, u32[]{:S(2)}, u32[]{:S(2)}) collective-permute-start(f32[8,128,128]{2,1,0:T(8,128)S(1)} %convolution_add_fusion.5), channel_id=1, source_target_pairs={{0,4},{4,8},{8,12},{12,16},{16,20},{20,24},{24,28},{1,5},{5,9},{9,... | collective-permute-start | bytes 1572872 | tf_op jit(solution)/shard_map/while/body/eval_jaxpr/ppermute | solution.py:13
  263.4 10.5 %collective-permute-start = (f32[8,128,128]{2,1,0:T(8,128)S(1)}, f32[8,128,128]{2,1,0:T(8,128)S(1)}, u32[]{:S(2)}, u32[]{:S(2)}) collective-permute-start(f32[8,128,128]{2,1,0:T(8,128)S(1)} %convolution_add_fusion.5), channel_id=1, source_target_pairs={{0,4},{4,8},{8,12},{12,16},{16,20},{20,24},{24,28},{1,5},{5,9},{9,... | collective-permute-start | bytes 1572872 | tf_op jit(solution)/shard_map/while/body/eval_jaxpr/ppermute | solution.py:13
  274.6 10.5 %collective-permute-start = (f32[8,128,128]{2,1,0:T(8,128)S(1)}, f32[8,128,128]{2,1,0:T(8,128)S(1)}, u32[]{:S(2)}, u32[]{:S(2)}) collective-permute-start(f32[8,128,128]{2,1,0:T(8,128)S(1)} %convolution_add_fusion.5), channel_id=1, source_target_pairs={{0,4},{4,8},{8,12},{12,16},{16,20},{20,24},{24,28},{1,5},{5,9},{9,... | collective-permute-start | bytes 1572872 | tf_op jit(solution)/shard_map/while/body/eval_jaxpr/ppermute | solution.py:13
  285.7 10.5 %collective-permute-start = (f32[8,128,128]{2,1,0:T(8,128)S(1)}, f32[8,128,128]{2,1,0:T(8,128)S(1)}, u32[]{:S(2)}, u32[]{:S(2)}) collective-permute-start(f32[8,128,128]{2,1,0:T(8,128)S(1)} %convolution_add_fusion.5), channel_id=1, source_target_pairs={{0,4},{4,8},{8,12},{12,16},{16,20},{20,24},{24,28},{1,5},{5,9},{9,... | collective-permute-start | bytes 1572872 | tf_op jit(solution)/shard_map/while/body/eval_jaxpr/ppermute | solution.py:13
  296.9 10.5 %collective-permute-start = (f32[8,128,128]{2,1,0:T(8,128)S(1)}, f32[8,128,128]{2,1,0:T(8,128)S(1)}, u32[]{:S(2)}, u32[]{:S(2)}) collective-permute-start(f32[8,128,128]{2,1,0:T(8,128)S(1)} %convolution_add_fusion.5), channel_id=1, source_target_pairs={{0,4},{4,8},{8,12},{12,16},{16,20},{20,24},{24,28},{1,5},{5,9},{9,... | collective-permute-start | bytes 1572872 | tf_op jit(solution)/shard_map/while/body/eval_jaxpr/ppermute | solution.py:13
Sparse Core Ops, SparseCore 0:
  315.4 62.5 reduce-scatter.1
where the time goes:
time: 388 us; the launch traced here: 387 us
  other arithmetic  174 us (45%)
  waiting for transfers between devices  73.1 us (19%)
  matrix products  61.8 us (16%)
  starting transfers between devices  58.5 us (15%)
  between operations  13.8 us (4%)
  local copies, waits for them, and re-layouts  5.22 us (1%)
    another operation x1, other arithmetic, block_terms(): solved = jax.scipy.linalg.solve_triangular(system, right_sides, lower=True)  159 us
    reduce_scatter x1, waiting for transfers between devices, shards(): lax.psum_scatter(jnp.dot(flat, out_weight, preferred_element_type=jnp.flo...  62.8 us
    ppermute x8, starting transfers between devices, from_behind(): return lax.ppermute(block, axis, route)  58.5 us
    dot_general x23, matrix products, matmul(): jnp.einsum('...ij,...jk->...ik', left, right, precision=lax.Precision.HIG...  52.3 us
    ppermute x8, waiting for transfers between devices, from_behind(): return lax.ppermute(block, axis, route)  10.4 us
  transfers between devices with their start and end apart: 9, of which 8 were waited for; matrix products, arithmetic and copies ran while one was open for 1% of the time, Pallas kernels for 0%

commit v1 on v0

v1 whole, which is shorter than its diff:
```python
import functools

import jax
import jax.numpy as jnp
from jax import lax
from jax.experimental import pallas as pl
from jax.experimental.pallas import tpu as pltpu
from jax.sharding import PartitionSpec as P

DK = 128
CHUNK = 128
MID = 63
HALO = 16
BASE = 32
F32 = jnp.float32
BF16 = jnp.bfloat16

PASS_A = 3
PASS_SOLVE = 3
PASS_UW = 3
PASS_PO = 3
PASS_COMP = 2
PASS_SCORES = 1
PASS_SU = 3

NN = (((1,), (0,)), ((), ()))
NT = (((1,), (1,)), ((), ()))
TN = (((0,), (0,)), ((), ()))


def dot(left, right, dims):
    return lax.dot_general(left, right, dims, preferred_element_type=F32)


def split(data):
    high = data.astype(BF16)
    return high, (data - high.astype(F32)).astype(BF16)


def mm(left, right, dims, passes):
    if passes == 1:
        return dot(left.astype(BF16), right.astype(BF16), dims)
    left_high, left_low = split(left)
    if passes == 2:
        right = right.astype(BF16)
        return dot(left_high, right, dims) + dot(left_low, right, dims)
    right_high, right_low = split(right)
    return dot(left_high, right_high, dims) + (
        dot(left_low, right_high, dims) + dot(left_high, right_low, dims)
    )


def conv_silu(scratch, data, before, taps):
    count, width = data.shape
    scratch[0:8, :] = before.astype(F32)
    scratch[8 : 8 + count, :] = data.astype(F32)
    number = taps.shape[0]
    total = taps[number - 1 : number, :].astype(F32) * scratch[8 : 8 + count, :]
    for tap in range(number - 1):
        first = 8 - (number - 1) + tap
        total = total + taps[tap : tap + 1, :].astype(F32) * scratch[first : first + count, :]
    return total / (1.0 + jnp.exp(-total))


def normalize(data):
    return data * lax.rsqrt(jnp.sum(data * data, axis=-1, keepdims=True) + 1e-06)


def iotas():
    rows = lax.broadcasted_iota(jnp.int32, (CHUNK, CHUNK), 0)
    columns = lax.broadcasted_iota(jnp.int32, (CHUNK, CHUNK), 1)
    return rows, columns


def cumulate(gates, rows, columns):
    ones = jnp.where(columns <= rows, 1.0, 0.0).astype(BF16)
    return dot(ones, gates, NN)


def inverse_blocks(matrices, rows, columns):
    lanes = lax.broadcasted_iota(jnp.int32, (8, CHUNK), 1)
    inner = lax.broadcasted_iota(jnp.int32, (8, CHUNK), 0)
    tiles = BASE // 8
    packed, solved = [], []
    for matrix in matrices:
        pack = []
        for t in range(tiles):
            total = jnp.zeros((8, CHUNK), F32)
            for b in range(CHUNK // BASE):
                first = b * BASE + t * 8
                total = jnp.where(lanes // BASE == b, matrix[first : first + 8, :], total)
            pack.append(total)
        packed.append(pack)
        solved.append([jnp.where(lanes % BASE == inner + 8 * t, 1.0, 0.0) for t in range(tiles)])
    for j in range(BASE - 1):
        pick = (lanes // BASE) * BASE + j
        for pack, block in zip(packed, solved):
            row = jnp.broadcast_to(block[j // 8][j % 8 : j % 8 + 1, :], (8, CHUNK))
            for t in range(j // 8, tiles):
                factor = jnp.take_along_axis(pack[t], pick, axis=1)
                block[t] = block[t] - factor * row
    results = []
    for block in solved:
        tall = jnp.concatenate(block * (CHUNK // BASE), axis=0)
        results.append(jnp.where(rows // BASE == columns // BASE, tall, 0.0))
    size = BASE
    while size < CHUNK:
        here = (rows // (2 * size) == columns // (2 * size)) & (rows // size != columns // size)
        moved = [
            mm(jnp.where(here, matrix, 0.0), result, NN, PASS_SOLVE)
            for matrix, result in zip(matrices, results)
        ]
        results = [
            result - mm(result, move, NN, PASS_SOLVE) for result, move in zip(results, moved)
        ]
        size *= 2
    return results


def column_of(table, head):
    lanes = lax.broadcasted_iota(jnp.int32, table.shape, 1)
    return jnp.sum(jnp.where(lanes == head, table, 0.0), axis=-1, keepdims=True)


def chunk_terms(keys, values, gates, betas, rows, columns):
    cumul = [cumulate(g, rows, columns) for g in gates]
    middle = [c[MID : MID + 1, :] for c in cumul]
    final = [c[CHUNK - 1 : CHUNK, :] for c in cumul]
    forward = [k * jnp.exp(m - c) for k, m, c in zip(keys, middle, cumul)]
    backward = [k * jnp.exp(c - m) for k, m, c in zip(keys, middle, cumul)]
    coupling = [mm(b, f, NT, PASS_A) for b, f in zip(backward, forward)]
    strict = [jnp.where(columns < rows, a * b, 0.0) for a, b in zip(coupling, betas)]
    solver = inverse_blocks(strict, rows, columns)
    sides = [
        jnp.concatenate([beta * b * jnp.exp(m), beta * v], axis=-1)
        for beta, b, m, v in zip(betas, backward, middle, values)
    ]
    solved = [mm(x, side, NN, PASS_UW) for x, side in zip(solver, sides)]
    trailing = [f * jnp.exp(e - m) for f, e, m in zip(forward, final, middle)]
    summary = [mm(u, t, TN, PASS_PO) for u, t in zip(solved, trailing)]
    return [jnp.exp(e) for e in final], summary, solved, forward


def chunk_of(step_heads, key, value, gate, beta, key_rim, value_rim, key_taps, value_taps, scratch):
    rows, columns = iotas()
    keys_all = conv_silu(scratch.at[0], key[...], key_rim[8:16, :], key_taps)
    values_all = conv_silu(scratch.at[1], value[...], value_rim[8:16, :], value_taps)
    heads = [pl.program_id(0) * step_heads + i for i in range(step_heads)]
    parts = [slice(i * DK, (i + 1) * DK) for i in range(step_heads)]
    terms = chunk_terms(
        [normalize(keys_all[:, at]) for at in parts],
        [values_all[:, at] for at in parts],
        [gate[:, at] for at in parts],
        [column_of(beta[...], head) for head in heads],
        rows,
        columns,
    )
    return heads, parts, rows, columns, terms


def later_kernel(
    step_heads, key, value, gate, beta, key_rim, value_rim, key_taps, value_taps,
    summary_out, decay_out, solved_out, forward_out, scratch,
):
    _, parts, _, _, terms = chunk_of(
        step_heads, key, value, gate, beta, key_rim, value_rim, key_taps, value_taps, scratch
    )
    for i, (at, decay, summary, solved, forward) in enumerate(zip(parts, *terms)):
        summary_out[i] = summary
        decay_out[i] = jnp.broadcast_to(decay, (8, DK))
        solved_out[i] = solved
        forward_out[:, at] = forward.astype(forward_out.dtype)


def first_kernel(
    step_heads, where, key, value, gate, beta, key_rim, value_rim, key_taps, value_taps,
    later_summary, later_decay,
    send_out, carry_out, solved_out, forward_out, scratch,
):
    heads, parts, rows, columns, terms = chunk_of(
        step_heads, key, value, gate, beta, key_rim, value_rim, key_taps, value_taps, scratch
    )
    carries, moves = [], []
    for i, (at, decay, summary, solved, forward) in enumerate(zip(parts, *terms)):
        solved_out[i] = solved
        forward_out[:, at] = forward.astype(forward_out.dtype)
        steady = jnp.where(rows == columns, decay, 0.0)
        carry = jnp.concatenate([steady - summary[:DK], summary[DK:]], axis=0)
        carry_out[i] = carry.astype(BF16)
        carries.append(carry)
    for i, carry in enumerate(carries):
        moves.append(mm(carry, later_summary[i, :DK, :], NN, PASS_COMP))
    for i, (head, decay, summary, moved) in enumerate(zip(heads, terms[0], terms[1], moves)):
        after = later_decay[i, 0:1, :]
        product = summary[:DK] * after + moved[:DK]
        offset = summary[DK:] * after - moved[DK:] + later_summary[i, DK:, :]
        both = decay * after
        high = both.astype(BF16)
        low = (both - high.astype(F32)).astype(BF16)
        slot = lax.bitwise_xor(head, where[0]) if where is not None else head
        send_out[slot, 0:DK, :] = product.astype(BF16)
        send_out[slot, DK : 2 * DK, :] = offset.astype(BF16)
        send_out[slot, 2 * DK : 2 * DK + 16, :] = jnp.concatenate(
            [jnp.broadcast_to(high, (8, DK)), jnp.broadcast_to(low, (8, DK))], axis=0
        )


def output_kernel(
    step_heads, query, gate, query_rim, query_taps,
    first_solved, later_solved, first_forward, later_forward, carry,
    direct_out, coefficient_out, scratch,
):
    rows, columns = iotas()
    queries_all = conv_silu(scratch, query[...], query_rim[8:16, :], query_taps)
    for i in range(step_heads):
        at = slice(i * DK, (i + 1) * DK)
        for c in range(2):
            tokens = slice(c * CHUNK, (c + 1) * CHUNK)
            queries = normalize(queries_all[tokens, at]) * DK ** (-0.5)
            solved = (first_solved, later_solved)[c][i]
            forward = (first_forward, later_forward)[c][:, at]
            cumul = cumulate(gate[tokens, at], rows, columns)
            middle = cumul[MID : MID + 1, :]
            queried = queries * jnp.exp(cumul - middle)
            scores = mm(queried, forward, NT, PASS_SCORES)
            scores = jnp.where(columns <= rows, scores, 0.0)
            moved = mm(scores, solved, NN, PASS_SU)
            coefficient = queried * jnp.exp(middle) - moved[:, :DK]
            direct = moved[:, DK:]
            if c == 1:
                weights = coefficient.astype(BF16)
                direct = direct + dot(weights, carry[i, DK:, :], NT)
                coefficient = dot(weights, carry[i, :DK, :], NT)
            direct_out[tokens, at] = direct
            coefficient_out[tokens, at] = coefficient.astype(BF16)


def scan_kernel(count, where, table, states_out):
    state = jnp.zeros((DK, DK), F32)
    for shard in range(count):
        slot = lax.bitwise_xor(where[0], shard)
        states_out[slot] = state.astype(BF16)
        if shard < count - 1:
            high = table[slot, 2 * DK : 2 * DK + 1, :].astype(F32)
            low = table[slot, 2 * DK + 8 : 2 * DK + 9, :].astype(F32)
            state = (
                state * (high + low)
                - dot(state.astype(BF16), table[slot, 0:DK, :], NN)
                + table[slot, DK : 2 * DK, :].astype(F32)
            )


def head_kernel(heads, parts, where, direct, coefficient, states, out):
    rows_each = direct.shape[0] // parts
    for head in range(heads):
        at = slice(head * DK, (head + 1) * DK)
        slot = lax.bitwise_xor(where[0], head)
        total = direct[:, at] + dot(coefficient[:, at], states[slot], NT)
        out[:, at] = total.astype(BF16)


def spec(shape, index):
    return pl.BlockSpec(shape, index)


def call(kernel, grid, in_specs, out_specs, out_shape, scratch, cost, limit, scalars, *args):
    return pl.pallas_call(
        kernel,
        grid_spec=pltpu.PrefetchScalarGridSpec(
            num_scalar_prefetch=scalars,
            grid=grid,
            in_specs=in_specs,
            out_specs=out_specs,
            scratch_shapes=scratch,
        ),
        out_shape=out_shape,
        compiler_params=pltpu.CompilerParams(
            dimension_semantics=("arbitrary",) * len(grid), vmem_limit_bytes=limit << 20
        ),
        cost_estimate=pl.CostEstimate(flops=cost[0], bytes_accessed=cost[1], transcendentals=0),
    )(*args)


def shards(query, key_in, value, gates, beta, conv_query, conv_key, conv_value, out_weight):
    length, width = query.shape
    groups = beta.shape[1]
    taps = conv_query.shape[0]
    ranks = lax.axis_size("seq")
    me = lax.axis_index("seq").astype(jnp.int32)
    spread = groups == ranks
    step_heads = 4
    steps = groups // step_heads
    wide = step_heads * DK
    shape = jax.ShapeDtypeStruct

    rims = jnp.stack([query[length - HALO :], key_in[length - HALO :], value[length - HALO :]])
    rims = lax.ppermute(rims, "seq", [(i, i + 1) for i in range(ranks - 1)])

    def chunk_spec(c):
        return spec((CHUNK, wide), lambda p, *_: (c, p))

    tap_spec = spec((taps, wide), lambda p, *_: (0, p))
    rim_spec = spec((HALO, wide), lambda p, *_: (CHUNK // HALO - 1, p))
    edge_spec = spec((HALO, wide), lambda p, *_: (0, p))
    solved_spec = spec((step_heads, CHUNK, 2 * DK), lambda p, *_: (p, 0, 0))
    summary_spec = spec((step_heads, 2 * DK, DK), lambda p, *_: (p, 0, 0))
    decay_spec = spec((step_heads, 8, DK), lambda p, *_: (p, 0, 0))
    block_spec = spec((CHUNK, wide), lambda p, *_: (0, p))
    whole_spec = spec((length, wide), lambda p, *_: (0, p))
    solved_shape = shape((groups, CHUNK, 2 * DK), F32)
    forward_shape = shape((CHUNK, width), BF16 if PASS_SCORES == 1 else F32)
    conv_scratch = pltpu.VMEM((2, 8 + CHUNK, wide), F32)

    later_summary, later_decay, later_solved, later_forward = call(
        functools.partial(later_kernel, step_heads),
        (steps,),
        [chunk_spec(1)] * 3
        + [spec((CHUNK, groups), lambda p, *_: (1, 0)), rim_spec, rim_spec, tap_spec, tap_spec],
        [summary_spec, decay_spec, solved_spec, block_spec],
        [shape((groups, 2 * DK, DK), F32), shape((groups, 8, DK), F32), solved_shape, forward_shape],
        [conv_scratch],
        (groups * 300_000_000, 4 << 20),
        60,
        0,
        key_in, value, gates, beta, key_in, value, conv_key, conv_value,
    )
    packed = 2 * DK + 16
    send, carry, first_solved, first_forward = call(
        functools.partial(first_kernel, step_heads) if spread
        else functools.partial(first_kernel, step_heads, None),
        (steps,),
        [chunk_spec(0)] * 3
        + [spec((CHUNK, groups), lambda p, *_: (0, 0)), edge_spec, edge_spec, tap_spec, tap_spec]
        + [summary_spec, decay_spec],
        [spec((groups, packed, DK), lambda p, *_: (0, 0, 0)), summary_spec, solved_spec, block_spec],
        [shape((groups, packed, DK), BF16), shape((groups, 2 * DK, DK), BF16), solved_shape, forward_shape],
        [conv_scratch],
        (groups * 300_000_000, 4 << 20),
        60,
        1 if spread else 0,
        *((me[None],) if spread else ()),
        key_in, value, gates, beta, rims[1], rims[2], conv_key, conv_value,
        later_summary, later_decay,
    )

    def exchange(blocks):
        return [blocks[0]] + [
            lax.ppermute(blocks[m], "seq", [(i, i ^ m) for i in range(ranks)])
            for m in range(1, ranks)
        ]

    direct, coefficient = call(
        functools.partial(output_kernel, step_heads),
        (steps,),
        [whole_spec, whole_spec, edge_spec, tap_spec, solved_spec, solved_spec, block_spec, block_spec, summary_spec],
        [whole_spec, whole_spec],
        [shape((length, width), F32), shape((length, width), BF16)],
        [pltpu.VMEM((8 + length, wide), F32)],
        (groups * 300_000_000, 4 << 20),
        60,
        0,
        query, gates, rims[0], conv_query,
        first_solved, later_solved, first_forward, later_forward, carry,
    )

    if spread:
        arrived = exchange(send)
        arrived, direct, coefficient = lax.optimization_barrier((arrived, direct, coefficient))
        table = jnp.stack(arrived)
        states = call(
            functools.partial(scan_kernel, ranks),
            (1,),
            [spec((ranks, packed, DK), lambda p, *_: (0, 0, 0))],
            spec((ranks, DK, DK), lambda p, *_: (0, 0, 0)),
            shape((ranks, DK, DK), BF16),
            [],
            (ranks * 4_000_000, 1 << 20),
            16,
            1,
            me[None], table,
        )
        states = jnp.stack(exchange(states))
        order = me
    else:
        every = lax.all_gather(send, "seq")
        product, offset = every[:, :, :DK].astype(F32), every[:, :, DK : 2 * DK].astype(F32)
        decay = every[:, :, 2 * DK : 2 * DK + 1].astype(F32) + every[:, :, 2 * DK + 8 : 2 * DK + 9].astype(F32)
        state = jnp.zeros((groups, DK, DK), F32)
        states = state
        for shard in range(ranks):
            states = jnp.where(me == shard, state, states)
            moved = jnp.einsum("hij,hjk->hik", state, product[shard], precision=lax.Precision.HIGHEST)
            state = state * decay[shard] - moved + offset[shard]
        states = states.astype(BF16)
        order = jnp.zeros((), jnp.int32)

    parts = lax.axis_size("head")
    mine = lax.axis_index("head")
    head_out = call(
        functools.partial(head_kernel, groups, parts),
        (1,),
        [
            spec((length, width), lambda p, *_: (0, 0)),
            spec((length, width), lambda p, *_: (0, 0)),
            spec((groups, DK, DK), lambda p, *_: (0, 0, 0)),
        ],
        spec((length, width), lambda p, *_: (0, 0)),
        shape((length, width), BF16),
        [],
        (groups * 8_000_000, 2 << 20),
        16,
        1,
        order[None], direct, coefficient, states,
    )
    share = length // parts

    def partial_sum(owner):
        rows = lax.dynamic_slice_in_dim(head_out, owner * share, share, 0)
        return jnp.dot(rows, out_weight, preferred_element_type=F32)

    arrived = []
    for distance in range(1, parts):
        part = partial_sum(lax.rem(mine + distance, parts)).astype(BF16)
        arrived.append(
            lax.ppermute(part, "head", [(i, (i + distance) % parts) for i in range(parts)])
        )
    total, arrived = lax.optimization_barrier((partial_sum(mine), arrived))
    for part in arrived:
        total = total + part.astype(F32)
    return total.astype(BF16)


def solution(mesh):
    in_specs = (
        P("seq", "head"),
        P("seq", "head"),
        P("seq", "head"),
        P("seq", "head"),
        P("seq", "head"),
        P(None, "head"),
        P(None, "head"),
        P(None, "head"),
        P("head", None),
    )
    out_specs = P(("seq", "head"), None)
    return jax.shard_map(shards, mesh=mesh, in_specs=in_specs, out_specs=out_specs, check_vma=False)
```

time: 388 us -> 87.4 us (0.23)
  the two profiles are of different devices: /device:TPU:0 before, /device:TPU:11 now
where the time goes in v1:
time: 87.4 us; the launch traced here: 86.8 us
  Pallas kernels  26.1 us (30%)
  waiting for transfers between devices  22.8 us (26%)
  starting transfers between devices  20.9 us (24%)
  matrix products  8.54 us (10%)
  local copies, waits for them, and re-layouts  7.31 us (8%)
    pallas_call x5, Pallas kernels, call(): pl.pallas_call(kernel, grid_spec=pltpu.PrefetchScalarGridSpec(num_scalar_...  26.1 us
    ppermute x3, waiting for transfers between devices, shards(): lax.ppermute(part, 'head', [(i, (i + distance) % parts) for i in range(pa...  19.7 us
    ppermute x14, starting transfers between devices, exchange(): lax.ppermute(blocks[m], 'seq', [(i, i ^ m) for i in range(ranks)])  13.3 us
    dot_general x4, matrix products, partial_sum(): return jnp.dot(rows, out_weight, preferred_element_type=F32)  8.54 us
    ppermute x3, starting transfers between devices, shards(): lax.ppermute(part, 'head', [(i, (i + distance) % parts) for i in range(pa...  3.95 us
    unnamed x22, local copies, waits for them, and re-layouts  3.91 us
    ppermute x1, starting transfers between devices, shards(): rims = lax.ppermute(rims, 'seq', [(i, i + 1) for i in range(ranks - 1)])  3.68 us
    ppermute x14, waiting for transfers between devices, exchange(): lax.ppermute(blocks[m], 'seq', [(i, i ^ m) for i in range(ranks)])  3.07 us
  transfers between devices with their start and end apart: 18, of which 4 were waited for; matrix products, arithmetic and copies ran while one was open for 8% of the time, Pallas kernels for 18%

profile of v1, /device:TPU:11, one launch (start us, length us, event | category | flops | bytes accessed | tf_op | source)
XLA Modules:
  0.0 86.8 jit_solution(17036115081825162567)
XLA Ops:
  0.0 0.8 slice_bitcast_fusion.20
  0.8 0.8 slice_bitcast_fusion.18
  1.6 3.7 %collective-permute-start = (bf16[3,16,1024]{2,1,0:T(8,128)(2,1)S(1)}, bf16[3,16,1024]{2,1,0:T(8,128)(2,1)S(1)}, u32[]{:S(2)}, u32[]{:S(2)}) collective-permute-start(bf16[3,16,1024]{2,1,0:T(8,128)(2,1)S(1)} %pad_maximum_fusion), channel_id=1, source_target_pairs={{0,4},{4,8},{8,12},{12,16},{16,20},{20,24},{24,28},{1,5},{5,9},{9,... | collective-permute-start | bytes 294920 | tf_op jit(solution)/shard_map/ppermute | solution.py:297
  5.2 1.5 %copy.11.beta = f32[256,8]{1,0:T(8,128)} copy(f32[256,8]{0,1:T(8,128)} %param.13) | data formatting | bytes 16384 | tf_op args[4]
  6.7 8.0 %shard_map.91 = (f32[8,256,128]{2,1,0:T(8,128)}, f32[8,8,128]{2,1,0:T(8,128)}, f32[8,128,256]{2,1,0:T(8,128)}, bf16[128,1024]{1,0:T(8,128)(2,1)}) custom-call(bf16[256,1024]{1,0:T(8,128)(2,1)} %key.3, bf16[256,1024]{1,0:T(8,128)(2,1)} %value.3, bf16[256,1024]{1,0:T(8,128)(2,1)} %gate.5, f32[256,8]{1,0:T(8,128)} %copy.11.beta, bf16[256,1024]{1,0:T(8,128)(2,1)} %key.3, ...), custom_call_target="tpu_custom_call" | custom-call | flops 2400000000 | bytes 4194304 | tf_op jit(solution)/shard_map/pallas_call | solution.py:267
  14.8 0.0 collective-permute-done
  14.8 0.7 slice_bitcast_fusion.15
  15.4 8.9 %shard_map.92 = (bf16[8,272,128]{2,1,0:T(8,128)(2,1)}, bf16[8,256,128]{2,1,0:T(8,128)(2,1)}, f32[8,128,256]{2,1,0:T(8,128)}, bf16[128,1024]{1,0:T(8,128)(2,1)}) custom-call(s32[1]{0:T(128)} %bitcast.where, bf16[256,1024]{1,0:T(8,128)(2,1)} %key.3, bf16[256,1024]{1,0:T(8,128)(2,1)} %value.3, bf16[256,1024]{1,0:T(8,128)(2,1)} %gate.5, f32[256,8]{1,0:T(8,128)} %copy.11.beta, ...), custom_call_target="tpu_custom_call" | custom-call | flops 2400000000 | bytes 4194304 | tf_op jit(solution)/shard_map/pallas_call | solution.py:267
  24.4 1.2 %slice_bitcast_fusion = (bf16[272,128]{1,0:T(8,128)(2,1)S(1)}, bf16[272,128]{1,0:T(8,128)(2,1)S(1)}, bf16[272,128]{1,0:T(8,128)(2,1)S(1)}, bf16[272,128]{1,0:T(8...) fusion(bf16[8,272,128]{2,1,0:T(8,128)(2,1)} %get-tuple-element.31), kind=kLoop, calls=%fused_computation.18 | loop fusion | bytes 1114112 | tf_op jit(solution)/shard_map/squeeze | solution.py:348
  25.6 0.1 collective-permute-start.1
  25.6 0.3 collective-permute-start.2
  26.0 1.8 %collective-permute-start.3 = (bf16[272,128]{1,0:T(8,128)(2,1)S(1)}, bf16[272,128]{1,0:T(8,128)(2,1)S(1)}, u32[]{:S(2)}, u32[]{:S(2)}) collective-permute-start(bf16[272,128]{1,0:T(8,128)(2,1)S(1)} %get-tuple-element.57), channel_id=1, source_target_pairs={{0,12},{4,8},{8,4},{12,0},{16,28},{20,24},{24,20},{28,16},{1,13},{... | collective-permute-start | bytes 208904 | tf_op jit(solution)/shard_map/ppermute | solution.py:348
  27.8 0.0 collective-permute-start.4
  27.8 1.4 %collective-permute-start.5 = (bf16[272,128]{1,0:T(8,128)(2,1)S(1)}, bf16[272,128]{1,0:T(8,128)(2,1)S(1)}, u32[]{:S(2)}, u32[]{:S(2)}) collective-permute-start(bf16[272,128]{1,0:T(8,128)(2,1)S(1)} %get-tuple-element.55), channel_id=1, source_target_pairs={{0,20},{4,16},{8,28},{12,24},{16,4},{20,0},{24,12},{28,8},{1,21},{... | collective-permute-start | bytes 208904 | tf_op jit(solution)/shard_map/ppermute | solution.py:348
  29.2 0.0 collective-permute-done.1
  29.2 1.2 %collective-permute-start.6 = (bf16[272,128]{1,0:T(8,128)(2,1)S(1)}, bf16[272,128]{1,0:T(8,128)(2,1)S(1)}, u32[]{:S(2)}, u32[]{:S(2)}) collective-permute-start(bf16[272,128]{1,0:T(8,128)(2,1)S(1)} %get-tuple-element.54), channel_id=1, source_target_pairs={{0,24},{4,28},{8,16},{12,20},{16,8},{20,12},{24,0},{28,4},{1,25},{... | collective-permute-start | bytes 208904 | tf_op jit(solution)/shard_map/ppermute | solution.py:348
  30.4 0.0 collective-permute-done.2
  30.4 1.8 %collective-permute-start.7 = (bf16[272,128]{1,0:T(8,128)(2,1)S(1)}, bf16[272,128]{1,0:T(8,128)(2,1)S(1)}, u32[]{:S(2)}, u32[]{:S(2)}) collective-permute-start(bf16[272,128]{1,0:T(8,128)(2,1)S(1)} %get-tuple-element.53), channel_id=1, source_target_pairs={{0,28},{4,24},{8,20},{12,16},{16,12},{20,8},{24,4},{28,0},{1,29},{... | collective-permute-start | bytes 208904 | tf_op jit(solution)/shard_map/ppermute | solution.py:348
  32.2 8.0 %shard_map.93 = (f32[256,1024]{1,0:T(8,128)}, bf16[256,1024]{1,0:T(8,128)(2,1)}) custom-call(bf16[256,1024]{1,0:T(8,128)(2,1)} %query.1, bf16[256,1024]{1,0:T(8,128)(2,1)} %gate.5, bf16[16,1024]{1,0:T(8,128)(2,1)} %get-tuple-element.69.query_rim, bf16[4,1024]{1,0:T(4,128)(2,1)} %query_taps.1, f32[8,128,256]{2,1,0:T(8,128)} %get-tuple-element.32.first_solved, ...), custom_call_target="tpu_custom_call" | custom-call | flops 2400000000 | bytes 4194304 | tf_op jit(solution)/shard_map/pallas_call | solution.py:267
  40.2 0.0 collective-permute-done.3
  40.2 0.0 collective-permute-done.4
  40.2 0.0 collective-permute-done.5
  40.2 0.0 collective-permute-done.6
  40.2 0.0 collective-permute-done.7
  40.4 0.9 shard_map.94
  41.3 0.1 collective-permute-start.8
  41.4 0.3 collective-permute-start.9
  41.7 1.8 %collective-permute-start.10 = (bf16[128,128]{1,0:T(8,128)(2,1)S(1)}, bf16[128,128]{1,0:T(8,128)(2,1)S(1)}, u32[]{:S(2)}, u32[]{:S(2)}) collective-permute-start(bf16[128,128]{1,0:T(8,128)(2,1)S(1)} %get-tuple-element.65), channel_id=1, source_target_pairs={{0,12},{4,8},{8,4},{12,0},{16,28},{20,24},{24,20},{28,16},{1,13},{... | collective-permute-start | bytes 98312 | tf_op jit(solution)/shard_map/ppermute | solution.py:348
  43.5 0.1 collective-permute-start.11
  43.6 1.4 %collective-permute-start.12 = (bf16[128,128]{1,0:T(8,128)(2,1)S(1)}, bf16[128,128]{1,0:T(8,128)(2,1)S(1)}, u32[]{:S(2)}, u32[]{:S(2)}) collective-permute-start(bf16[128,128]{1,0:T(8,128)(2,1)S(1)} %get-tuple-element.63), channel_id=1, source_target_pairs={{0,20},{4,16},{8,28},{12,24},{16,4},{20,0},{24,12},{28,8},{1,21},{... | collective-permute-start | bytes 98312 | tf_op jit(solution)/shard_map/ppermute | solution.py:348
  44.9 0.0 collective-permute-done.8
  44.9 1.2 %collective-permute-start.13 = (bf16[128,128]{1,0:T(8,128)(2,1)S(1)}, bf16[128,128]{1,0:T(8,128)(2,1)S(1)}, u32[]{:S(2)}, u32[]{:S(2)}) collective-permute-start(bf16[128,128]{1,0:T(8,128)(2,1)S(1)} %get-tuple-element.62), channel_id=1, source_target_pairs={{0,24},{4,28},{8,16},{12,20},{16,8},{20,12},{24,0},{28,4},{1,25},{... | collective-permute-start | bytes 98312 | tf_op jit(solution)/shard_map/ppermute | solution.py:348
  46.2 0.0 collective-permute-done.9
  46.2 1.8 %collective-permute-start.14 = (bf16[128,128]{1,0:T(8,128)(2,1)S(1)}, bf16[128,128]{1,0:T(8,128)(2,1)S(1)}, u32[]{:S(2)}, u32[]{:S(2)}) collective-permute-start(bf16[128,128]{1,0:T(8,128)(2,1)S(1)} %get-tuple-element.61), channel_id=1, source_target_pairs={{0,28},{4,24},{8,20},{12,16},{16,12},{20,8},{24,4},{28,0},{1,29},{... | collective-permute-start | bytes 98312 | tf_op jit(solution)/shard_map/ppermute | solution.py:348
  48.0 0.0 collective-permute-done.10
  48.0 0.0 collective-permute-done.11
  48.0 0.0 collective-permute-done.12
  48.0 0.5 collective-permute-done.13
  48.6 2.5 %collective-permute-done.14 = bf16[128,128]{1,0:T(8,128)(2,1)S(1)} collective-permute-done((bf16[128,128]{1,0:T(8,128)(2,1)S(1)}, bf16[128,128]{1,0:T(8,128)(2,1)S(1)}, u32[]{:S(2)}, u32[]{:S(2)}) %collective-permute-start.14) | collective-permute-done | bytes 32800 | tf_op jit(solution)/shard_map/ppermute | solution.py:348
  51.1 0.0 copy-start
  51.1 1.2 %copy-done = f32[256,1024]{1,0:T(8,128)S(1)} copy-done((f32[256,1024]{1,0:T(8,128)S(1)}, f32[256,1024]{1,0:T(8,128)}, u32[]{:S(2)}) %copy-start) | copy-done | bytes 1048600
  52.3 0.0 copy-start.1
  52.3 1.0 %copy-done.1 = bf16[256,1024]{1,0:T(8,128)(2,1)S(1)} copy-done((bf16[256,1024]{1,0:T(8,128)(2,1)S(1)}, bf16[256,1024]{1,0:T(8,128)(2,1)}, u32[]{:S(2)}) %copy-start.1) | copy-done | bytes 524312
  53.4 0.0 slice-start
  53.4 0.3 shard_map.95
  53.7 0.0 slice-start.1
  53.7 3.4 %convolution_convert_fusion.2 = bf16[64,2304]{1,0:T(8,128)(2,1)S(1)} fusion(bf16[1024,2304]{1,0:T(8,128)(2,1)} %param.17, bf16[256,1024]{1,0:T(8,128)(2,1)S(1)} %shard_map.95, s32[]{:T(128)S(6)} %select_n.13), kind=kOutput, calls=%fused_computation.2 | convolution fusion | flops 302137344 | bytes 5144580 | tf_op jit(solution)/shard_map/dot_general | solution.py:419
  57.1 1.4 %collective-permute-start.15 = (bf16[64,2304]{1,0:T(8,128)(2,1)S(1)}, bf16[64,2304]{1,0:T(8,128)(2,1)S(1)}, u32[]{:S(2)}, u32[]{:S(2)}) collective-permute-start(bf16[64,2304]{1,0:T(8,128)(2,1)S(1)} %convolution_convert_fusion.2), channel_id=1, source_target_pairs={{0,1},{1,2},{2,3},{3,0},{4,5},{5,6},{6,7},{7,4},{8,9},{9,10},{10,1... | collective-permute-start | bytes 884744 | tf_op jit(solution)/shard_map/ppermute | solution.py:425
  58.5 3.3 %convolution_convert_fusion.1 = bf16[64,2304]{1,0:T(8,128)(2,1)S(1)} fusion(bf16[1024,2304]{1,0:T(8,128)(2,1)} %param.17, bf16[256,1024]{1,0:T(8,128)(2,1)S(1)} %shard_map.95, s32[]{:T(128)S(6)} %select_n.14), kind=kOutput, calls=%fused_computation.1 | convolution fusion | flops 302137344 | bytes 5144580 | tf_op jit(solution)/shard_map/dot_general | solution.py:419
  61.8 1.1 %collective-permute-start.16 = (bf16[64,2304]{1,0:T(8,128)(2,1)S(1)}, bf16[64,2304]{1,0:T(8,128)(2,1)S(1)}, u32[]{:S(2)}, u32[]{:S(2)}) collective-permute-start(bf16[64,2304]{1,0:T(8,128)(2,1)S(1)} %convolution_convert_fusion.1), channel_id=1, source_target_pairs={{0,2},{1,3},{2,0},{3,1},{4,6},{5,7},{6,4},{7,5},{8,10},{9,11},{10,... | collective-permute-start | bytes 884744 | tf_op jit(solution)/shard_map/ppermute | solution.py:425
  62.9 0.0 slice-done
  62.9 0.0 slice-done.1
  62.9 0.9 %convolution_convert_fusion = bf16[64,2304]{1,0:T(8,128)(2,1)S(1)} fusion(bf16[1024,2304]{1,0:T(8,128)(2,1)S(1)} %bitcast.78, bf16[256,1024]{1,0:T(8,128)(2,1)S(1)} %shard_map.95, s32[]{:T(128)S(6)} %select_n.15), kind=kOutput, calls=%fused_computation | convolution fusion | flops 302137344 | bytes 5144580 | tf_op jit(solution)/shard_map/dot_general | solution.py:419
  63.8 1.5 %collective-permute-start.17 = (bf16[64,2304]{1,0:T(8,128)(2,1)S(1)}, bf16[64,2304]{1,0:T(8,128)(2,1)S(1)}, u32[]{:S(2)}, u32[]{:S(2)}) collective-permute-start(bf16[64,2304]{1,0:T(8,128)(2,1)S(1)} %convolution_convert_fusion), channel_id=1, source_target_pairs={{0,3},{1,0},{2,1},{3,2},{4,7},{5,4},{6,5},{7,6},{8,11},{9,8},{10,9... | collective-permute-start | bytes 884744 | tf_op jit(solution)/shard_map/ppermute | solution.py:425
  65.3 0.9 %fusion.3 = f32[64,2304]{1,0:T(8,128)S(1)} fusion(bf16[1024,2304]{1,0:T(8,128)(2,1)S(1)} %bitcast.78, bf16[256,1024]{1,0:T(8,128)(2,1)S(1)} %shard_map.95, s32[]{:T(128)S(6)} %select_n.12), kind=kOutput, calls=%fused_computation.7 | convolution fusion | flops 301989888 | bytes 5439492 | tf_op jit(solution)/shard_map/dot_general | solution.py:419
  66.2 0.0 collective-permute-done.15
  66.2 17.2 %collective-permute-done.16 = bf16[64,2304]{1,0:T(8,128)(2,1)S(1)} collective-permute-done((bf16[64,2304]{1,0:T(8,128)(2,1)S(1)}, bf16[64,2304]{1,0:T(8,128)(2,1)S(1)}, u32[]{:S(2)}, u32[]{:S(2)}) %collective-permute-start.16) | collective-permute-done | bytes 294944 | tf_op jit(solution)/shard_map/ppermute | solution.py:425
  83.4 2.6 %collective-permute-done.17 = bf16[64,2304]{1,0:T(8,128)(2,1)S(1)} collective-permute-done((bf16[64,2304]{1,0:T(8,128)(2,1)S(1)}, bf16[64,2304]{1,0:T(8,128)(2,1)S(1)}, u32[]{:S(2)}, u32[]{:S(2)}) %collective-permute-start.17) | collective-permute-done | bytes 294944 | tf_op jit(solution)/shard_map/ppermute | solution.py:425
  86.0 0.8 add_convert_fusion
  (18 shorter events, 0.2 us)
Async XLA Ops:
  1.6 13.2 %collective-permute-start = (bf16[3,16,1024]{2,1,0:T(8,128)(2,1)S(1)}, bf16[3,16,1024]{2,1,0:T(8,128)(2,1)S(1)}, u32[]{:S(2)}, u32[]{:S(2)}) collective-permute-start(bf16[3,16,1024]{2,1,0:T(8,128)(2,1)S(1)} %pad_maximum_fusion), channel_id=1, source_target_pairs={{0,4},{4,8},{8,12},{12,16},{16,20},{20,24},{24,28},{1,5},{5,9},{9,... | collective-permute-start | bytes 294920 | tf_op jit(solution)/shard_map/ppermute | solution.py:297
  25.6 3.6 %collective-permute-start.1 = (bf16[272,128]{1,0:T(8,128)(2,1)S(1)}, bf16[272,128]{1,0:T(8,128)(2,1)S(1)}, u32[]{:S(2)}, u32[]{:S(2)}) collective-permute-start(bf16[272,128]{1,0:T(8,128)(2,1)S(1)} %get-tuple-element.59), channel_id=1, source_target_pairs={{0,4},{4,0},{8,12},{12,8},{16,20},{20,16},{24,28},{28,24},{1,5},{5... | collective-permute-start | bytes 208904 | tf_op jit(solution)/shard_map/ppermute | solution.py:348
  25.6 4.8 %collective-permute-start.2 = (bf16[272,128]{1,0:T(8,128)(2,1)S(1)}, bf16[272,128]{1,0:T(8,128)(2,1)S(1)}, u32[]{:S(2)}, u32[]{:S(2)}) collective-permute-start(bf16[272,128]{1,0:T(8,128)(2,1)S(1)} %get-tuple-element.58), channel_id=1, source_target_pairs={{0,8},{4,12},{8,0},{12,4},{16,24},{20,28},{24,16},{28,20},{1,9},{5... | collective-permute-start | bytes 208904 | tf_op jit(solution)/shard_map/ppermute | solution.py:348
  26.0 14.2 %collective-permute-start.3 = (bf16[272,128]{1,0:T(8,128)(2,1)S(1)}, bf16[272,128]{1,0:T(8,128)(2,1)S(1)}, u32[]{:S(2)}, u32[]{:S(2)}) collective-permute-start(bf16[272,128]{1,0:T(8,128)(2,1)S(1)} %get-tuple-element.57), channel_id=1, source_target_pairs={{0,12},{4,8},{8,4},{12,0},{16,28},{20,24},{24,20},{28,16},{1,13},{... | collective-permute-start | bytes 208904 | tf_op jit(solution)/shard_map/ppermute | solution.py:348
  27.8 12.4 %collective-permute-start.4 = (bf16[272,128]{1,0:T(8,128)(2,1)S(1)}, bf16[272,128]{1,0:T(8,128)(2,1)S(1)}, u32[]{:S(2)}, u32[]{:S(2)}) collective-permute-start(bf16[272,128]{1,0:T(8,128)(2,1)S(1)} %get-tuple-element.56), channel_id=1, source_target_pairs={{0,16},{4,20},{8,24},{12,28},{16,0},{20,4},{24,8},{28,12},{1,17},{... | collective-permute-start | bytes 208904 | tf_op jit(solution)/shard_map/ppermute | solution.py:348
  27.8 12.4 %collective-permute-start.5 = (bf16[272,128]{1,0:T(8,128)(2,1)S(1)}, bf16[272,128]{1,0:T(8,128)(2,1)S(1)}, u32[]{:S(2)}, u32[]{:S(2)}) collective-permute-start(bf16[272,128]{1,0:T(8,128)(2,1)S(1)} %get-tuple-element.55), channel_id=1, source_target_pairs={{0,20},{4,16},{8,28},{12,24},{16,4},{20,0},{24,12},{28,8},{1,21},{... | collective-permute-start | bytes 208904 | tf_op jit(solution)/shard_map/ppermute | solution.py:348
  29.2 11.0 %collective-permute-start.6 = (bf16[272,128]{1,0:T(8,128)(2,1)S(1)}, bf16[272,128]{1,0:T(8,128)(2,1)S(1)}, u32[]{:S(2)}, u32[]{:S(2)}) collective-permute-start(bf16[272,128]{1,0:T(8,128)(2,1)S(1)} %get-tuple-element.54), channel_id=1, source_target_pairs={{0,24},{4,28},{8,16},{12,20},{16,8},{20,12},{24,0},{28,4},{1,25},{... | collective-permute-start | bytes 208904 | tf_op jit(solution)/shard_map/ppermute | solution.py:348
  30.4 9.8 %collective-permute-start.7 = (bf16[272,128]{1,0:T(8,128)(2,1)S(1)}, bf16[272,128]{1,0:T(8,128)(2,1)S(1)}, u32[]{:S(2)}, u32[]{:S(2)}) collective-permute-start(bf16[272,128]{1,0:T(8,128)(2,1)S(1)} %get-tuple-element.53), channel_id=1, source_target_pairs={{0,28},{4,24},{8,20},{12,16},{16,12},{20,8},{24,4},{28,0},{1,29},{... | collective-permute-start | bytes 208904 | tf_op jit(solution)/shard_map/ppermute | solution.py:348
  41.3 3.7 %collective-permute-start.8 = (bf16[128,128]{1,0:T(8,128)(2,1)S(1)}, bf16[128,128]{1,0:T(8,128)(2,1)S(1)}, u32[]{:S(2)}, u32[]{:S(2)}) collective-permute-start(bf16[128,128]{1,0:T(8,128)(2,1)S(1)} %get-tuple-element.67), channel_id=1, source_target_pairs={{0,4},{4,0},{8,12},{12,8},{16,20},{20,16},{24,28},{28,24},{1,5},{5... | collective-permute-start | bytes 98312 | tf_op jit(solution)/shard_map/ppermute | solution.py:348
  41.4 4.8 %collective-permute-start.9 = (bf16[128,128]{1,0:T(8,128)(2,1)S(1)}, bf16[128,128]{1,0:T(8,128)(2,1)S(1)}, u32[]{:S(2)}, u32[]{:S(2)}) collective-permute-start(bf16[128,128]{1,0:T(8,128)(2,1)S(1)} %get-tuple-element.66), channel_id=1, source_target_pairs={{0,8},{4,12},{8,0},{12,4},{16,24},{20,28},{24,16},{28,20},{1,9},{5... | collective-permute-start | bytes 98312 | tf_op jit(solution)/shard_map/ppermute | solution.py:348
  41.7 6.3 %collective-permute-start.10 = (bf16[128,128]{1,0:T(8,128)(2,1)S(1)}, bf16[128,128]{1,0:T(8,128)(2,1)S(1)}, u32[]{:S(2)}, u32[]{:S(2)}) collective-permute-start(bf16[128,128]{1,0:T(8,128)(2,1)S(1)} %get-tuple-element.65), channel_id=1, source_target_pairs={{0,12},{4,8},{8,4},{12,0},{16,28},{20,24},{24,20},{28,16},{1,13},{... | collective-permute-start | bytes 98312 | tf_op jit(solution)/shard_map/ppermute | solution.py:348
  43.5 4.5 %collective-permute-start.11 = (bf16[128,128]{1,0:T(8,128)(2,1)S(1)}, bf16[128,128]{1,0:T(8,128)(2,1)S(1)}, u32[]{:S(2)}, u32[]{:S(2)}) collective-permute-start(bf16[128,128]{1,0:T(8,128)(2,1)S(1)} %get-tuple-element.64), channel_id=1, source_target_pairs={{0,16},{4,20},{8,24},{12,28},{16,0},{20,4},{24,8},{28,12},{1,17},{... | collective-permute-start | bytes 98312 | tf_op jit(solution)/shard_map/ppermute | solution.py:348
  43.6 4.5 %collective-permute-start.12 = (bf16[128,128]{1,0:T(8,128)(2,1)S(1)}, bf16[128,128]{1,0:T(8,128)(2,1)S(1)}, u32[]{:S(2)}, u32[]{:S(2)}) collective-permute-start(bf16[128,128]{1,0:T(8,128)(2,1)S(1)} %get-tuple-element.63), channel_id=1, source_target_pairs={{0,20},{4,16},{8,28},{12,24},{16,4},{20,0},{24,12},{28,8},{1,21},{... | collective-permute-start | bytes 98312 | tf_op jit(solution)/shard_map/ppermute | solution.py:348
  44.9 3.7 %collective-permute-start.13 = (bf16[128,128]{1,0:T(8,128)(2,1)S(1)}, bf16[128,128]{1,0:T(8,128)(2,1)S(1)}, u32[]{:S(2)}, u32[]{:S(2)}) collective-permute-start(bf16[128,128]{1,0:T(8,128)(2,1)S(1)} %get-tuple-element.62), channel_id=1, source_target_pairs={{0,24},{4,28},{8,16},{12,20},{16,8},{20,12},{24,0},{28,4},{1,25},{... | collective-permute-start | bytes 98312 | tf_op jit(solution)/shard_map/ppermute | solution.py:348
  46.2 4.9 %collective-permute-start.14 = (bf16[128,128]{1,0:T(8,128)(2,1)S(1)}, bf16[128,128]{1,0:T(8,128)(2,1)S(1)}, u32[]{:S(2)}, u32[]{:S(2)}) collective-permute-start(bf16[128,128]{1,0:T(8,128)(2,1)S(1)} %get-tuple-element.61), channel_id=1, source_target_pairs={{0,28},{4,24},{8,20},{12,16},{16,12},{20,8},{24,4},{28,0},{1,29},{... | collective-permute-start | bytes 98312 | tf_op jit(solution)/shard_map/ppermute | solution.py:348
  51.1 1.2 %copy-start = (f32[256,1024]{1,0:T(8,128)S(1)}, f32[256,1024]{1,0:T(8,128)}, u32[]{:S(2)}) copy-start(f32[256,1024]{1,0:T(8,128)} %get-tuple-element.39.direct) | copy-start | bytes 3145732
  52.3 1.0 %copy-start.1 = (bf16[256,1024]{1,0:T(8,128)(2,1)S(1)}, bf16[256,1024]{1,0:T(8,128)(2,1)}, u32[]{:S(2)}) copy-start(bf16[256,1024]{1,0:T(8,128)(2,1)} %get-tuple-element.40.coefficient) | copy-start | bytes 1572868
  53.4 9.5 %slice-start = ((s8[4718592]{0:T(1024)(128)(4,1)}), s8[524288]{0:T(1024)(128)(4,1)S(1)}, s32[]{:S(2)}) async-start(s8[4718592]{0:T(1024)(128)(4,1)} %bitcast.77), calls=%async_computation | async-start | bytes 1048576
  53.7 9.2 %slice-start.1 = ((s8[4718592]{0:T(1024)(128)(4,1)}), s8[4194304]{0:T(1024)(128)(4,1)S(1)}, s32[]{:S(2)}) async-start(s8[4718592]{0:T(1024)(128)(4,1)} %bitcast.77), calls=%async_computation.1 | async-start | bytes 8388608
  57.1 9.1 %collective-permute-start.15 = (bf16[64,2304]{1,0:T(8,128)(2,1)S(1)}, bf16[64,2304]{1,0:T(8,128)(2,1)S(1)}, u32[]{:S(2)}, u32[]{:S(2)}) collective-permute-start(bf16[64,2304]{1,0:T(8,128)(2,1)S(1)} %convolution_convert_fusion.2), channel_id=1, source_target_pairs={{0,1},{1,2},{2,3},{3,0},{4,5},{5,6},{6,7},{7,4},{8,9},{9,10},{10,1... | collective-permute-start | bytes 884744 | tf_op jit(solution)/shard_map/ppermute | solution.py:425
  61.8 21.7 %collective-permute-start.16 = (bf16[64,2304]{1,0:T(8,128)(2,1)S(1)}, bf16[64,2304]{1,0:T(8,128)(2,1)S(1)}, u32[]{:S(2)}, u32[]{:S(2)}) collective-permute-start(bf16[64,2304]{1,0:T(8,128)(2,1)S(1)} %convolution_convert_fusion.1), channel_id=1, source_target_pairs={{0,2},{1,3},{2,0},{3,1},{4,6},{5,7},{6,4},{7,5},{8,10},{9,11},{10,... | collective-permute-start | bytes 884744 | tf_op jit(solution)/shard_map/ppermute | solution.py:425
  63.8 22.2 %collective-permute-start.17 = (bf16[64,2304]{1,0:T(8,128)(2,1)S(1)}, bf16[64,2304]{1,0:T(8,128)(2,1)S(1)}, u32[]{:S(2)}, u32[]{:S(2)}) collective-permute-start(bf16[64,2304]{1,0:T(8,128)(2,1)S(1)} %convolution_convert_fusion), channel_id=1, source_target_pairs={{0,3},{1,0},{2,1},{3,2},{4,7},{5,4},{6,5},{7,6},{8,11},{9,8},{10,9... | collective-permute-start | bytes 884744 | tf_op jit(solution)/shard_map/ppermute | solution.py:425

commit v2 on v1

v2 whole, which is shorter than its diff:
```python
import functools

import jax
import jax.numpy as jnp
from jax import lax
from jax.experimental import pallas as pl
from jax.experimental.pallas import tpu as pltpu
from jax.sharding import PartitionSpec as P

DK = 128
CHUNK = 128
MID = 63
HALO = 16
BASE = 16
LIMIT = 32
F32 = jnp.float32
BF16 = jnp.bfloat16

PASS_A = 3
PASS_SOLVE = 3
PASS_UW = 3
PASS_PO = 3
PASS_COMP = 2
PASS_SCORES = 1
PASS_SU = 3

NN = (((1,), (0,)), ((), ()))
NT = (((1,), (1,)), ((), ()))
TN = (((0,), (0,)), ((), ()))


def dot(left, right, dims):
    return lax.dot_general(left, right, dims, preferred_element_type=F32)


def split(data):
    high = data.astype(BF16)
    return high, (data - high.astype(F32)).astype(BF16)


def mm(left, right, dims, passes):
    if passes == 1:
        return dot(left.astype(BF16), right.astype(BF16), dims)
    left_high, left_low = split(left)
    if passes == 2:
        right = right.astype(BF16)
        return dot(left_high, right, dims) + dot(left_low, right, dims)
    right_high, right_low = split(right)
    return dot(left_high, right_high, dims) + (
        dot(left_low, right_high, dims) + dot(left_high, right_low, dims)
    )


def conv_silu(scratch, data, before, taps):
    count, width = data.shape
    scratch[0:8, :] = before.astype(F32)
    scratch[8 : 8 + count, :] = data.astype(F32)
    number = taps.shape[0]
    total = taps[number - 1 : number, :].astype(F32) * scratch[8 : 8 + count, :]
    for tap in range(number - 1):
        first = 8 - (number - 1) + tap
        total = total + taps[tap : tap + 1, :].astype(F32) * scratch[first : first + count, :]
    return total / (1.0 + jnp.exp(-total))


def normalize(data):
    return data * lax.rsqrt(jnp.sum(data * data, axis=-1, keepdims=True) + 1e-06)


def iotas():
    rows = lax.broadcasted_iota(jnp.int32, (CHUNK, CHUNK), 0)
    columns = lax.broadcasted_iota(jnp.int32, (CHUNK, CHUNK), 1)
    return rows, columns


def cumulate(gates, rows, columns):
    ones = jnp.where(columns <= rows, 1.0, 0.0).astype(BF16)
    return dot(ones, gates, NN)


def inverse_blocks(matrices, rows, columns):
    lanes = lax.broadcasted_iota(jnp.int32, (8, CHUNK), 1)
    inner = lax.broadcasted_iota(jnp.int32, (8, CHUNK), 0)
    tiles = BASE // 8
    packed, solved = [], []
    for matrix in matrices:
        pack = []
        for t in range(tiles):
            total = jnp.zeros((8, CHUNK), F32)
            for b in range(CHUNK // BASE):
                first = b * BASE + t * 8
                total = jnp.where(lanes // BASE == b, matrix[first : first + 8, :], total)
            pack.append(total)
        packed.append(pack)
        solved.append([jnp.where(lanes % BASE == inner + 8 * t, 1.0, 0.0) for t in range(tiles)])
    for j in range(BASE - 1):
        pick = (lanes // BASE) * BASE + j
        for pack, block in zip(packed, solved):
            row = jnp.broadcast_to(block[j // 8][j % 8 : j % 8 + 1, :], (8, CHUNK))
            for t in range(j // 8, tiles):
                factor = jnp.take_along_axis(pack[t], pick, axis=1)
                block[t] = block[t] - factor * row
    results = []
    for block in solved:
        tall = jnp.concatenate(block * (CHUNK // BASE), axis=0)
        results.append(jnp.where(rows // BASE == columns // BASE, tall, 0.0))
    size = BASE
    while size < CHUNK:
        here = (rows // (2 * size) == columns // (2 * size)) & (rows // size != columns // size)
        moved = [
            mm(jnp.where(here, matrix, 0.0), result, NN, PASS_SOLVE)
            for matrix, result in zip(matrices, results)
        ]
        results = [
            result - mm(result, move, NN, PASS_SOLVE) for result, move in zip(results, moved)
        ]
        size *= 2
    return results


def column_of(row, rows, columns):
    return jnp.sum(jnp.where(rows == columns, row, 0.0), axis=-1, keepdims=True)


def chunk_terms(keys, values, gates, betas, rows, columns):
    cumul = [cumulate(g, rows, columns) for g in gates]
    middle = [c[MID : MID + 1, :] for c in cumul]
    final = [c[CHUNK - 1 : CHUNK, :] for c in cumul]
    forward = [k * jnp.exp(m - c) for k, m, c in zip(keys, middle, cumul)]
    backward = [k * jnp.exp(c - m) for k, m, c in zip(keys, middle, cumul)]
    coupling = [mm(b, f, NT, PASS_A) for b, f in zip(backward, forward)]
    strict = [jnp.where(columns < rows, a * b, 0.0) for a, b in zip(coupling, betas)]
    solver = inverse_blocks(strict, rows, columns)
    sides = [
        jnp.concatenate([beta * b * jnp.exp(m), beta * v], axis=-1)
        for beta, b, m, v in zip(betas, backward, middle, values)
    ]
    solved = [mm(x, side, NN, PASS_UW) for x, side in zip(solver, sides)]
    trailing = [f * jnp.exp(e - m) for f, e, m in zip(forward, final, middle)]
    summary = [mm(u, t, TN, PASS_PO) for u, t in zip(solved, trailing)]
    return [jnp.exp(e) for e in final], summary, solved, forward


def chunk_of(key, value, gate, beta, key_rim, value_rim, key_taps, value_taps, scratch):
    rows, columns = iotas()
    keys_all = conv_silu(scratch.at[0], key[...], key_rim[8:16, :], key_taps)
    values_all = conv_silu(scratch.at[1], value[...], value_rim[8:16, :], value_taps)
    heads = range(beta.shape[0])
    parts = [slice(i * DK, (i + 1) * DK) for i in heads]
    terms = chunk_terms(
        [normalize(keys_all[:, at]) for at in parts],
        [values_all[:, at] for at in parts],
        [gate[:, at] for at in parts],
        [column_of(beta[i : i + 1, :], rows, columns) for i in heads],
        rows,
        columns,
    )
    return heads, parts, rows, columns, terms


def later_kernel(
    key, value, gate, beta, key_rim, value_rim, key_taps, value_taps,
    summary_out, decay_out, solved_out, forward_out, scratch,
):
    _, parts, _, _, terms = chunk_of(
        key, value, gate, beta, key_rim, value_rim, key_taps, value_taps, scratch
    )
    for i, (at, decay, summary, solved, forward) in enumerate(zip(parts, *terms)):
        summary_out[i] = summary
        decay_out[i] = jnp.broadcast_to(decay, (8, DK))
        solved_out[i] = solved
        forward_out[:, at] = forward.astype(forward_out.dtype)


def first_kernel(
    where, key, value, gate, beta, rims, key_taps, value_taps, later_summary, later_decay,
    carry_out, solved_out, forward_out, *rest,
):
    *send_outs, send, scratch = rest
    heads, parts, rows, columns, terms = chunk_of(
        key, value, gate, beta, rims.at[1], rims.at[2], key_taps, value_taps, scratch
    )
    carries, moves = [], []
    for i, (at, decay, summary, solved, forward) in enumerate(zip(parts, *terms)):
        solved_out[i] = solved
        forward_out[:, at] = forward.astype(forward_out.dtype)
        steady = jnp.where(rows == columns, decay, 0.0)
        carry = jnp.concatenate([steady - summary[:DK], summary[DK:]], axis=0)
        carry_out[i] = carry.astype(BF16)
        carries.append(carry)
    for i, carry in enumerate(carries):
        moves.append(mm(carry, later_summary[i, :DK, :], NN, PASS_COMP))
    for head, decay, summary, moved in zip(heads, terms[0], terms[1], moves):
        after = later_decay[head, 0:1, :]
        product = summary[:DK] * after + moved[:DK]
        offset = summary[DK:] * after - moved[DK:] + later_summary[head, DK:, :]
        both = decay * after
        high = both.astype(BF16)
        low = (both - high.astype(F32)).astype(BF16)
        slot = lax.bitwise_xor(head, where[0])
        send[slot, 0:DK, :] = product.astype(BF16)
        send[slot, DK : 2 * DK, :] = offset.astype(BF16)
        send[slot, 2 * DK : 2 * DK + 16, :] = jnp.concatenate(
            [jnp.broadcast_to(high, (8, DK)), jnp.broadcast_to(low, (8, DK))], axis=0
        )
    for slot, out in enumerate(send_outs):
        out[...] = send[slot]


def output_kernel(
    first_head, query, gate, rims, query_taps,
    first_solved, later_solved, first_forward, later_forward, carry, matrix,
    direct_out, coefficient_out, *rest,
):
    *kept, scratch = rest
    if kept:
        matrix_out, arrived = kept
        fetch = pltpu.make_async_copy(matrix, matrix_out, arrived)
        fetch.start()
    step_heads = query.shape[1] // DK
    query_rim = rims[0, :, first_head * DK : first_head * DK + query.shape[1]]
    rows, columns = iotas()
    queries_all = conv_silu(scratch, query[...], query_rim[8:16, :], query_taps)
    units = [(i, c) for i in range(step_heads) for c in range(2)]
    wide = [slice(i * DK, (i + 1) * DK) for i, _ in units]
    tall = [slice(c * CHUNK, (c + 1) * CHUNK) for _, c in units]
    solved = [(first_solved, later_solved)[c][first_head + i] for i, c in units]
    forward = [
        (first_forward, later_forward)[c][:, (first_head + i) * DK : (first_head + i + 1) * DK]
        for i, c in units
    ]
    cumul = [cumulate(gate[t, w], rows, columns) for t, w in zip(tall, wide)]
    middle = [c[MID : MID + 1, :] for c in cumul]
    queries = [normalize(queries_all[t, w]) * DK ** (-0.5) for t, w in zip(tall, wide)]
    queried = [q * jnp.exp(c - m) for q, c, m in zip(queries, cumul, middle)]
    scores = [mm(q, f, NT, PASS_SCORES) for q, f in zip(queried, forward)]
    scores = [jnp.where(columns <= rows, x, 0.0) for x in scores]
    moved = [mm(x, u, NN, PASS_SU) for x, u in zip(scores, solved)]
    weights = [
        (q * jnp.exp(m) - x[:, :DK]).astype(BF16) for q, m, x in zip(queried, middle, moved)
    ]
    later = [
        dot(w, carry[first_head + i], NT) if c == 1 else None for (i, c), w in zip(units, weights)
    ]
    for (i, c), t, w, weight, x, extra in zip(units, tall, wide, weights, moved, later):
        direct = x[:, DK:]
        if c == 1:
            direct = direct + extra[:, DK:]
            weight = extra[:, :DK].astype(BF16)
        direct_out[t, w] = direct
        coefficient_out[t, w] = weight
    if kept:
        fetch.wait()


def scan_kernel(count, where, *refs):
    tables, (states_out, table) = refs[:count], refs[count:]
    for slot in range(count):
        table[slot] = tables[slot][...]
    state = jnp.zeros((DK, DK), F32)
    for shard in range(count):
        slot = lax.bitwise_xor(where[0], shard)
        states_out[slot] = state.astype(BF16)
        if shard < count - 1:
            high = table[slot, 2 * DK : 2 * DK + 1, :].astype(F32)
            low = table[slot, 2 * DK + 8 : 2 * DK + 9, :].astype(F32)
            state = (
                state * (high + low)
                - dot(state.astype(BF16), table[slot, 0:DK, :], NN)
                + table[slot, DK : 2 * DK, :].astype(F32)
            )


def tail_kernel(query, key, value, out):
    out[0] = query[...]
    out[1] = key[...]
    out[2] = value[...]


def project_kernel(heads, owners, where, mine, direct_one, direct_two, weight_one, weight_two, matrix, states, *rest):
    *outs, head_out, ordered = rest
    parts = len(owners)
    share = head_out.shape[0] // parts

    @pl.when(pl.program_id(0) == 0)
    def _():
        for head in range(heads):
            at = slice(head * DK, (head + 1) * DK)
            half, inner = divmod(head, heads // 2)
            near = slice(inner * DK, (inner + 1) * DK)
            slot = lax.bitwise_xor(where[0], head)
            total = (direct_one, direct_two)[half][:, near] + dot(
                (weight_one, weight_two)[half][:, near], states[slot], NT
            )
            head_out[:, at] = total.astype(BF16)
        for distance in range(parts):
            owner = owners[distance](mine[0])
            ordered[distance * share : (distance + 1) * share, :] = head_out[
                pl.ds(pl.multiple_of(owner * share, share), share), :
            ]

    total = dot(ordered[...], matrix[...], NN)
    for distance in range(parts):
        outs[distance][...] = total[distance * share : (distance + 1) * share, :].astype(
            outs[distance].dtype
        )


def spec(shape, index):
    return pl.BlockSpec(shape, index)


def call(kernel, grid, in_specs, out_specs, out_shape, scratch, cost, limit, scalars, *args):
    return pl.pallas_call(
        kernel,
        grid_spec=pltpu.PrefetchScalarGridSpec(
            num_scalar_prefetch=scalars,
            grid=grid,
            in_specs=in_specs,
            out_specs=out_specs,
            scratch_shapes=scratch,
        ),
        out_shape=out_shape,
        compiler_params=pltpu.CompilerParams(
            dimension_semantics=("arbitrary",) * len(grid), vmem_limit_bytes=limit << 20
        ),
        cost_estimate=pl.CostEstimate(flops=cost[0], bytes_accessed=cost[1], transcendentals=0),
    )(*args)


def shards(query, key_in, value, gates, beta, conv_query, conv_key, conv_value, out_weight):
    length, width = query.shape
    groups = beta.shape[1]
    taps = conv_query.shape[0]
    ranks = lax.axis_size("seq")
    me = lax.axis_index("seq").astype(jnp.int32)
    spread = groups == ranks
    order = me if spread else jnp.zeros((), jnp.int32)
    shape = jax.ShapeDtypeStruct
    kept = pltpu.VMEM
    here = pl.BlockSpec(memory_space=pltpu.VMEM)
    query, key_in, value, gates, beta_rows, conv_query, conv_key, conv_value, out_weight = (
        pltpu.with_memory_space_constraint(data, pltpu.HBM)
        for data in (
            query, key_in, value, gates, beta.T, conv_query, conv_key, conv_value, out_weight
        )
    )
    tail_spec = spec((HALO, width), lambda p: (length // HALO - 1, 0))
    rims = call(
        tail_kernel, (1,), [tail_spec] * 3,
        spec((3, HALO, width), lambda p: (0, 0, 0)), shape((3, HALO, width), BF16),
        [], (0, 3 * HALO * width * 4), LIMIT, 0, query, key_in, value,
    )
    rims = lax.ppermute(rims, "seq", [(i, i + 1) for i in range(ranks - 1)])

    def chunk_specs(c):
        return [spec((CHUNK, width), lambda p, *_: (c, 0))] * 3 + [
            spec((groups, CHUNK), lambda p, *_: (0, c))
        ]

    tap_spec = spec((taps, width), lambda p, *_: (0, 0))
    rim_spec = spec((HALO, width), lambda p, *_: (CHUNK // HALO - 1, 0))
    solved_shape = kept((groups, CHUNK, 2 * DK), F32)
    forward_shape = kept((CHUNK, width), BF16 if PASS_SCORES == 1 else F32)
    conv_scratch = pltpu.VMEM((2, 8 + CHUNK, width), F32)
    cost = (groups * 100_000_000, 4 << 20)

    later_summary, later_decay, later_solved, later_forward = call(
        later_kernel,
        (1,),
        chunk_specs(1) + [rim_spec, rim_spec, tap_spec, tap_spec],
        [here] * 4,
        [kept((groups, 2 * DK, DK), F32), kept((groups, 8, DK), F32), solved_shape, forward_shape],
        [conv_scratch],
        cost,
        LIMIT,
        0,
        key_in, value, gates, beta_rows, key_in, value, conv_key, conv_value,
    )
    packed = 2 * DK + 16
    carry, first_solved, first_forward, *send = call(
        first_kernel,
        (1,),
        chunk_specs(0) + [here, tap_spec, tap_spec, here, here],
        [here] * (3 + groups),
        [kept((groups, 2 * DK, DK), BF16), solved_shape, forward_shape]
        + [kept((packed, DK), BF16)] * groups,
        [pltpu.VMEM((groups, packed, DK), BF16), conv_scratch],
        cost,
        LIMIT,
        1,
        order[None], key_in, value, gates, beta_rows, rims, conv_key, conv_value,
        later_summary, later_decay,
    )

    def exchange(blocks):
        return [blocks[0]] + [
            lax.ppermute(blocks[m], "seq", [(i, i ^ m) for i in range(ranks)])
            for m in range(1, ranks)
        ]

    def outputs(half, later_solved, fetch):
        half_spec = spec((length, width // 2), lambda p: (0, half))
        extra_shape = [kept(out_weight.shape, BF16)] if fetch else []
        return call(
            functools.partial(output_kernel, half * groups // 2),
            (1,),
            [half_spec, half_spec, here, spec((taps, width // 2), lambda p: (0, half))]
            + [here] * 5
            + [pl.BlockSpec(memory_space=pl.ANY)],
            [here] * (3 if fetch else 2),
            [kept((length, width // 2), F32), kept((length, width // 2), BF16)] + extra_shape,
            ([pltpu.SemaphoreType.DMA] if fetch else [])
            + [pltpu.VMEM((8 + length, width // 2), F32)],
            (groups * 50_000_000, 2 << 20),
            LIMIT,
            0,
            query, gates, rims, conv_query,
            first_solved, later_solved, first_forward, later_forward, carry, out_weight,
        )

    direct_one, weight_one, matrix = outputs(0, later_solved, True)
    if spread:
        arrived = exchange(send)
        arrived, direct_one, weight_one, matrix = lax.optimization_barrier((arrived, direct_one, weight_one, matrix))
        states = call(
            functools.partial(scan_kernel, ranks),
            (1,),
            [here] * ranks,
            spec((ranks, DK, DK), lambda p, *_: (0, 0, 0)),
            shape((ranks, DK, DK), BF16),
            [pltpu.VMEM((ranks, packed, DK), BF16)],
            (ranks * 4_000_000, 1 << 20),
            LIMIT,
            1,
            me[None], *arrived,
        )
        states, later_solved = lax.optimization_barrier((states, later_solved))
        direct_two, weight_two = outputs(1, later_solved, False)
        states = jnp.stack(exchange(states))
        states, direct_two, weight_two, matrix = lax.optimization_barrier(
            (states, direct_two, weight_two, matrix)
        )
    else:
        direct_two, weight_two = outputs(1, later_solved, False)
        every = lax.all_gather(jnp.stack(send), "seq")
        product, offset = every[:, :, :DK].astype(F32), every[:, :, DK : 2 * DK].astype(F32)
        decay = every[:, :, 2 * DK : 2 * DK + 1].astype(F32) + every[:, :, 2 * DK + 8 : 2 * DK + 9].astype(F32)
        state = jnp.zeros((groups, DK, DK), F32)
        states = state
        for shard in range(ranks):
            states = jnp.where(me == shard, state, states)
            moved = jnp.einsum("hij,hjk->hik", state, product[shard], precision=lax.Precision.HIGHEST)
            state = state * decay[shard] - moved + offset[shard]
        states = states.astype(BF16)

    parts = lax.axis_size("head")
    mine = lax.axis_index("head").astype(jnp.int32)
    share = length // parts
    model = out_weight.shape[1]
    if parts == 4:
        owners = (
            lambda z: z,
            lambda z: jnp.where(lax.rem(z, 2) == 0, 3, 0),
            lambda z: jnp.where(z < 2, 2, 1),
            lambda z: lax.rem(2 * z + 1, 5),
        )
    else:
        owners = [lambda z, d=d: lax.rem(z + d, parts) for d in range(parts)]
    own, *leaving = call(
        functools.partial(project_kernel, groups, owners),
        (1,),
        [here] * 5 + [spec((groups, DK, DK), lambda p, *_: (0, 0, 0))],
        [here] * parts,
        [kept((share, model), F32)] + [kept((share, model), BF16)] * (parts - 1),
        [pltpu.VMEM((length, width), BF16)] * 2,
        (2 * length * width * model, width * model * 2),
        LIMIT,
        2,
        order[None], mine[None], direct_one, direct_two, weight_one, weight_two, matrix, states,
    )
    if parts == 4:
        near, inward, last = leaving
        middle = (mine == 1) | (mine == 2)
        near = lax.ppermute(near, "head", [(0, 1), (1, 0), (2, 3), (3, 2)]).astype(F32)
        skipped = lax.ppermute(inward, "head", [(0, 2), (3, 1)])
        crossed = lax.ppermute(inward, "head", [(1, 2), (2, 1)])
        joined = (last.astype(F32) + jnp.where(middle, near, 0.0)).astype(BF16)
        joined = lax.ppermute(joined, "head", [(0, 1), (3, 2), (1, 3), (2, 0)])
        arrived = [jnp.where(middle, 0.0, near), skipped, crossed, joined]
    else:
        arrived = [
            lax.ppermute(part, "head", [(i, (i + d) % parts) for i in range(parts)])
            for d, part in enumerate(leaving, 1)
        ]
    total = own
    for part in arrived:
        total = total + part.astype(F32)
    return total.astype(BF16)


def solution(mesh):
    in_specs = (
        P("seq", "head"),
        P("seq", "head"),
        P("seq", "head"),
        P("seq", "head"),
        P("seq", "head"),
        P(None, "head"),
        P(None, "head"),
        P(None, "head"),
        P("head", None),
    )
    out_specs = P(("seq", "head"), None)
    return jax.shard_map(shards, mesh=mesh, in_specs=in_specs, out_specs=out_specs, check_vma=False)
```

time: 87.4 us -> 70.3 us (0.80)
  the two profiles are of different devices: /device:TPU:11 before, /device:TPU:0 now
where the time goes in v2:
time: 70.3 us; the launch traced here: 69.9 us
  starting transfers between devices  27.2 us (39%)
  Pallas kernels  21.4 us (30%)
  waiting for transfers between devices  20.1 us (29%)
  other arithmetic  0.99 us (1%)
    pallas_call x7, Pallas kernels, call(): pl.pallas_call(kernel, grid_spec=pltpu.PrefetchScalarGridSpec(num_scalar_...  21.4 us
    ppermute x14, starting transfers between devices, exchange(): lax.ppermute(blocks[m], 'seq', [(i, i ^ m) for i in range(ranks)])  14.9 us
    ppermute x1, waiting for transfers between devices, shards(): joined = lax.ppermute(joined, 'head', [(0, 1), (3, 2), (1, 3), (2, 0)])  10.3 us
    ppermute x1, starting transfers between devices, shards(): skipped = lax.ppermute(inward, 'head', [(0, 2), (3, 1)])  5.74 us
    ppermute x1, waiting for transfers between devices, shards(): skipped = lax.ppermute(inward, 'head', [(0, 2), (3, 1)])  4.48 us
    ppermute x14, waiting for transfers between devices, exchange(): lax.ppermute(blocks[m], 'seq', [(i, i ^ m) for i in range(ranks)])  4.29 us
    ppermute x1, starting transfers between devices, shards(): rims = lax.ppermute(rims, 'seq', [(i, i + 1) for i in range(ranks - 1)])  2.35 us
    ppermute x1, starting transfers between devices, shards(): joined = lax.ppermute(joined, 'head', [(0, 1), (3, 2), (1, 3), (2, 0)])  1.8 us
  transfers between devices with their start and end apart: 19, of which 6 were waited for; matrix products, arithmetic and copies ran while one was open for 0% of the time, Pallas kernels for 16%

profile of v2, /device:TPU:0, one launch (start us, length us, event | category | flops | bytes accessed | tf_op | source)
XLA Modules:
  0.0 69.9 jit_solution(2112979706285048574)
XLA Ops:
  0.0 0.8 %shard_map.91 = bf16[3,16,1024]{2,1,0:T(8,128)(2,1)S(1)} custom-call(bf16[256,1024]{1,0:T(8,128)(2,1)} %query.5, bf16[256,1024]{1,0:T(8,128)(2,1)} %key.5, bf16[256,1024]{1,0:T(8,128)(2,1)} %value.5), custom_call_target="tpu_custom_call" | custom-call | bytes 196608 | tf_op jit(solution)/shard_map/pallas_call | solution.py:314
  0.8 2.4 %collective-permute-start = (bf16[3,16,1024]{2,1,0:T(8,128)(2,1)S(1)}, bf16[3,16,1024]{2,1,0:T(8,128)(2,1)S(1)}, u32[]{:S(2)}, u32[]{:S(2)}) collective-permute-start(bf16[3,16,1024]{2,1,0:T(8,128)(2,1)S(1)} %shard_map.91), channel_id=1, source_target_pairs={{0,4},{4,8},{8,12},{12,16},{16,20},{20,24},{24,28},{1,5},{5,9},{9,... | collective-permute-start | bytes 294920 | tf_op jit(solution)/shard_map/ppermute | solution.py:354
  3.2 5.2 %shard_map.92 = (f32[8,256,128]{2,1,0:T(8,128)S(1)}, f32[8,8,128]{2,1,0:T(8,128)S(1)}, f32[8,128,256]{2,1,0:T(8,128)S(1)}, bf16[128,1024]{1,0:T(8,128)(2,1)S(1)}) custom-call(bf16[256,1024]{1,0:T(8,128)(2,1)} %key.5, bf16[256,1024]{1,0:T(8,128)(2,1)} %value.5, bf16[256,1024]{1,0:T(8,128)(2,1)} %gate.7, f32[8,256]{1,0:T(8,128)} %bitcast.31, ...), custom_call_target="tpu_custom_call" | custom-call | flops 800000000 | bytes 4194304 | tf_op jit(solution)/shard_map/pallas_call | solution.py:314
  8.3 0.0 collective-permute-done.rims
  8.3 6.2 %shard_map.93 = (bf16[8,256,128]{2,1,0:T(8,128)(2,1)S(1)}, f32[8,128,256]{2,1,0:T(8,128)S(1)}, bf16[128,1024]{1,0:T(8,128)(2,1)S(1)}, bf16[272,128]{1,0:T(8,128)...) custom-call(s32[1]{0:T(128)} %bitcast.where, ...), custom_call_target="tpu_custom_call" | custom-call | flops 800000000 | bytes 4194304 | tf_op jit(solution)/shard_map/pallas_call | solution.py:314
  14.5 2.6 %collective-permute-start.1 = (bf16[272,128]{1,0:T(8,128)(2,1)S(1)}, bf16[272,128]{1,0:T(8,128)(2,1)S(1)}, u32[]{:S(2)}, u32[]{:S(2)}) collective-permute-start(bf16[272,128]{1,0:T(8,128)(2,1)S(1)} %get-tuple-element.49), channel_id=1, source_target_pairs={{0,4},{4,0},{8,12},{12,8},{16,20},{20,16},{24,28},{28,24},{1,5},{5... | collective-permute-start | bytes 208904 | tf_op jit(solution)/shard_map/ppermute | solution.py:398
  17.1 1.5 %collective-permute-start.2 = (bf16[272,128]{1,0:T(8,128)(2,1)S(1)}, bf16[272,128]{1,0:T(8,128)(2,1)S(1)}, u32[]{:S(2)}, u32[]{:S(2)}) collective-permute-start(bf16[272,128]{1,0:T(8,128)(2,1)S(1)} %get-tuple-element.50), channel_id=1, source_target_pairs={{0,8},{4,12},{8,0},{12,4},{16,24},{20,28},{24,16},{28,20},{1,9},{5... | collective-permute-start | bytes 208904 | tf_op jit(solution)/shard_map/ppermute | solution.py:398
  18.6 0.0 collective-permute-start.3
  18.6 1.4 %collective-permute-start.4 = (bf16[272,128]{1,0:T(8,128)(2,1)}, bf16[272,128]{1,0:T(8,128)(2,1)}, u32[]{:S(2)}, u32[]{:S(2)}) collective-permute-start(bf16[272,128]{1,0:T(8,128)(2,1)} %get-tuple-element.52), channel_id=1, source_target_pairs={{0,16},{4,20},{8,24},{12,28},{16,0},{20,4},{24,8},{28,12},{1,17},{... | collective-permute-start | bytes 208904 | tf_op jit(solution)/shard_map/ppermute | solution.py:398
  20.0 0.6 collective-permute-start.5
  20.6 0.0 collective-permute-done.1.refs_1_
  20.6 1.3 %collective-permute-start.6 = (bf16[272,128]{1,0:T(8,128)(2,1)}, bf16[272,128]{1,0:T(8,128)(2,1)}, u32[]{:S(2)}, u32[]{:S(2)}) collective-permute-start(bf16[272,128]{1,0:T(8,128)(2,1)} %get-tuple-element.54), channel_id=1, source_target_pairs={{0,24},{4,28},{8,16},{12,20},{16,8},{20,12},{24,0},{28,4},{1,25},{... | collective-permute-start | bytes 208904 | tf_op jit(solution)/shard_map/ppermute | solution.py:398
  21.9 0.0 collective-permute-done.2.refs_2_
  21.9 1.1 %collective-permute-start.7 = (bf16[272,128]{1,0:T(8,128)(2,1)}, bf16[272,128]{1,0:T(8,128)(2,1)}, u32[]{:S(2)}, u32[]{:S(2)}) collective-permute-start(bf16[272,128]{1,0:T(8,128)(2,1)} %get-tuple-element.55), channel_id=1, source_target_pairs={{0,28},{4,24},{8,20},{12,16},{16,12},{20,8},{24,4},{28,0},{1,29},{... | collective-permute-start | bytes 208904 | tf_op jit(solution)/shard_map/ppermute | solution.py:398
  23.0 3.4 %shard_map.94 = (f32[256,512]{1,0:T(8,128)S(1)}, bf16[256,512]{1,0:T(8,128)(2,1)S(1)}, bf16[1024,2304]{1,0:T(8,128)(2,1)S(1)}) custom-call(bf16[256,1024]{1,0:T(8,128)(2,1)} %query.5, bf16[256,1024]{1,0:T(8,128)(2,1)} %gate.7, bf16[3,16,1024]{2,1,0:T(8,128)(2,1)S(1)} %collective-permute-done.rims, bf16[4,1024]{1,0:T(4,128)(2,1)} %query_taps.3, ...), custom_call_target="tpu_custom_call" | custom-call | flops 400000000 | bytes 2097152 | tf_op jit(solution)/shard_map/pallas_call | solution.py:314
  26.4 0.0 collective-permute-done.3.refs_3_
  26.4 0.0 collective-permute-done.4.refs_4_
  26.4 1.3 %collective-permute-done.5.refs_5_ = bf16[272,128]{1,0:T(8,128)(2,1)} collective-permute-done((bf16[272,128]{1,0:T(8,128)(2,1)}, bf16[272,128]{1,0:T(8,128)(2,1)}, u32[]{:S(2)}, u32[]{:S(2)}) %collective-permute-start.5) | collective-permute-done | bytes 69664 | tf_op jit(solution)/shard_map/ppermute | solution.py:398
  27.7 0.0 collective-permute-done.6.refs_6_
  27.8 0.0 collective-permute-done.7.refs_7_
  27.8 1.9 %shard_map.95 = bf16[8,128,128]{2,1,0:T(8,128)(2,1)S(1)} custom-call(s32[1]{0:T(128)} %bitcast.where, bf16[272,128]{1,0:T(8,128)(2,1)S(1)} %get-tuple-element.65.refs_0_, bf16[272,128]{1,0:T(8,128)(2,1)S(1)} %collective-permute-done.1.refs_1_, bf16[272,128]{1,0:T(8,128)(2,1)S(1)} %collective-permute-done.2.refs_2_, ...), custom_call_target="tpu_custom_call" | custom-call | flops 32000000 | bytes 1048576 | tf_op jit(solution)/shard_map/pallas_call | solution.py:314
  29.7 0.3 collective-permute-start.8
  29.9 1.6 %collective-permute-start.9 = (bf16[128,128]{1,0:T(8,128)(2,1)S(1)}, bf16[128,128]{1,0:T(8,128)(2,1)S(1)}, u32[]{:S(2)}, u32[]{:S(2)}) collective-permute-start(bf16[128,128]{1,0:T(8,128)(2,1)S(1)} %get-tuple-element.92), channel_id=1, source_target_pairs={{0,8},{4,12},{8,0},{12,4},{16,24},{20,28},{24,16},{28,20},{1,9},{5... | collective-permute-start | bytes 98312 | tf_op jit(solution)/shard_map/ppermute | solution.py:398
  31.5 0.1 collective-permute-start.10
  31.6 1.7 %collective-permute-start.11 = (bf16[128,128]{1,0:T(8,128)(2,1)S(1)}, bf16[128,128]{1,0:T(8,128)(2,1)S(1)}, u32[]{:S(2)}, u32[]{:S(2)}) collective-permute-start(bf16[128,128]{1,0:T(8,128)(2,1)S(1)} %get-tuple-element.90), channel_id=1, source_target_pairs={{0,16},{4,20},{8,24},{12,28},{16,0},{20,4},{24,8},{28,12},{1,17},{... | collective-permute-start | bytes 98312 | tf_op jit(solution)/shard_map/ppermute | solution.py:398
  33.3 0.2 collective-permute-start.12
  33.4 2.3 %shard_map.96 = (f32[256,512]{1,0:T(8,128)S(1)}, bf16[256,512]{1,0:T(8,128)(2,1)S(1)}) custom-call(bf16[256,1024]{1,0:T(8,128)(2,1)} %query.5, bf16[256,1024]{1,0:T(8,128)(2,1)} %gate.7, bf16[3,16,1024]{2,1,0:T(8,128)(2,1)S(1)} %collective-permute-done.rims, bf16[4,1024]{1,0:T(4,128)(2,1)} %query_taps.3, f32[8,128,256]{2,1,0:T(8,128)S(1)} %get-tuple-element.56.first_solved, ...), custom_call_target="tpu_custom_call" | custom-call | flops 400000000 | bytes 2097152 | tf_op jit(solution)/shard_map/pallas_call | solution.py:314
  35.8 0.0 collective-permute-done.8
  35.8 1.4 %collective-permute-start.13 = (bf16[128,128]{1,0:T(8,128)(2,1)S(1)}, bf16[128,128]{1,0:T(8,128)(2,1)S(1)}, u32[]{:S(2)}, u32[]{:S(2)}) collective-permute-start(bf16[128,128]{1,0:T(8,128)(2,1)S(1)} %get-tuple-element.88), channel_id=1, source_target_pairs={{0,24},{4,28},{8,16},{12,20},{16,8},{20,12},{24,0},{28,4},{1,25},{... | collective-permute-start | bytes 98312 | tf_op jit(solution)/shard_map/ppermute | solution.py:398
  37.2 0.0 collective-permute-done.9
  37.2 1.3 %collective-permute-start.14 = (bf16[128,128]{1,0:T(8,128)(2,1)S(1)}, bf16[128,128]{1,0:T(8,128)(2,1)S(1)}, u32[]{:S(2)}, u32[]{:S(2)}) collective-permute-start(bf16[128,128]{1,0:T(8,128)(2,1)S(1)} %get-tuple-element.87), channel_id=1, source_target_pairs={{0,28},{4,24},{8,20},{12,16},{16,12},{20,8},{24,4},{28,0},{1,29},{... | collective-permute-start | bytes 98312 | tf_op jit(solution)/shard_map/ppermute | solution.py:398
  38.5 0.0 collective-permute-done.10
  38.5 0.0 collective-permute-done.11
  38.5 0.0 collective-permute-done.12
  38.6 2.1 %collective-permute-done.13 = bf16[128,128]{1,0:T(8,128)(2,1)S(1)} collective-permute-done((bf16[128,128]{1,0:T(8,128)(2,1)S(1)}, bf16[128,128]{1,0:T(8,128)(2,1)S(1)}, u32[]{:S(2)}, u32[]{:S(2)}) %collective-permute-start.13) | collective-permute-done | bytes 32800 | tf_op jit(solution)/shard_map/ppermute | solution.py:398
  40.7 0.8 %collective-permute-done.14 = bf16[128,128]{1,0:T(8,128)(2,1)S(1)} collective-permute-done((bf16[128,128]{1,0:T(8,128)(2,1)S(1)}, bf16[128,128]{1,0:T(8,128)(2,1)S(1)}, u32[]{:S(2)}, u32[]{:S(2)}) %collective-permute-start.14) | collective-permute-done | bytes 32800 | tf_op jit(solution)/shard_map/ppermute | solution.py:398
  41.5 1.7 %shard_map.97 = (f32[64,2304]{1,0:T(8,128)S(1)}, bf16[64,2304]{1,0:T(8,128)(2,1)S(1)}, bf16[64,2304]{1,0:T(8,128)(2,1)S(1)}, bf16[64,2304]{1,0:T(8,128)(2,1)S(1)}) custom-call(s32[1]{0:T(128)} %bitcast.where, s32[1]{0:T(128)} %bitcast.1.mine, f32[256,512]{1,0:T(8,128)S(1)} %get-tuple-element.64.direct_one, f32[256,512]{1,0:T(8,128)S(1)} %get-tuple-element.78.direct_two, ...), custom_call_target="tpu_custom_call" | custom-call | flops 1207959552 | bytes 4718592 | tf_op jit(solution)/shard_map/pallas_call | solution.py:314
  43.2 1.7 %collective-permute-start.15 = (bf16[64,2304]{1,0:T(8,128)(2,1)S(1)}, bf16[64,2304]{1,0:T(8,128)(2,1)S(1)}, u32[]{:S(2)}, u32[]{:S(2)}) collective-permute-start(bf16[64,2304]{1,0:T(8,128)(2,1)S(1)} %get-tuple-element.84), channel_id=1, source_target_pairs={{0,1},{1,0},{2,3},{3,2},{4,5},{5,4},{6,7},{7,6},{8,9},{9,8},{10,11... | collective-permute-start | bytes 884744 | tf_op jit(solution)/shard_map/ppermute | solution.py:485
  44.9 0.7 collective-permute-start.17
  45.6 5.7 %collective-permute-start.16 = (bf16[64,2304]{1,0:T(8,128)(2,1)S(1)}, bf16[64,2304]{1,0:T(8,128)(2,1)S(1)}, u32[]{:S(2)}, u32[]{:S(2)}) collective-permute-start(bf16[64,2304]{1,0:T(8,128)(2,1)S(1)} %get-tuple-element.85), channel_id=1, source_target_pairs={{0,2},{3,1},{4,6},{7,5},{8,10},{11,9},{12,14},{15,13},{16,18},{19,... | collective-permute-start | bytes 884744 | tf_op jit(solution)/shard_map/ppermute | solution.py:486
  51.3 1.1 %collective-permute-done.15 = bf16[64,2304]{1,0:T(8,128)(2,1)S(1)} collective-permute-done((bf16[64,2304]{1,0:T(8,128)(2,1)S(1)}, bf16[64,2304]{1,0:T(8,128)(2,1)S(1)}, u32[]{:S(2)}, u32[]{:S(2)}) %collective-permute-start.15) | collective-permute-done | bytes 294944 | tf_op jit(solution)/shard_map/ppermute | solution.py:485
  52.4 0.1 fusion.6
  52.5 1.8 %collective-permute-start.18 = (bf16[64,2304]{1,0:T(8,128)(2,1)S(1)}, bf16[64,2304]{1,0:T(8,128)(2,1)S(1)}, u32[]{:S(2)}, u32[]{:S(2)}) collective-permute-start(bf16[64,2304]{1,0:T(8,128)(2,1)S(1)} %fusion.6), channel_id=1, source_target_pairs={{0,1},{3,2},{1,3},{2,0},{4,5},{7,6},{5,7},{6,4},{8,9},{11,10},{9,1... | collective-permute-start | bytes 884744 | tf_op jit(solution)/shard_map/ppermute | solution.py:489
  54.3 0.0 collective-permute-done.17
  54.3 4.5 %collective-permute-done.16 = bf16[64,2304]{1,0:T(8,128)(2,1)S(1)} collective-permute-done((bf16[64,2304]{1,0:T(8,128)(2,1)S(1)}, bf16[64,2304]{1,0:T(8,128)(2,1)S(1)}, u32[]{:S(2)}, u32[]{:S(2)}) %collective-permute-start.16) | collective-permute-done | bytes 294944 | tf_op jit(solution)/shard_map/ppermute | solution.py:486
  58.7 10.3 %collective-permute-done.18 = bf16[64,2304]{1,0:T(8,128)(2,1)S(1)} collective-permute-done((bf16[64,2304]{1,0:T(8,128)(2,1)S(1)}, bf16[64,2304]{1,0:T(8,128)(2,1)S(1)}, u32[]{:S(2)}, u32[]{:S(2)}) %collective-permute-start.18) | collective-permute-done | bytes 294944 | tf_op jit(solution)/shard_map/ppermute | solution.py:489
  69.0 0.9 %fusion.4 = bf16[64,2304]{1,0:T(8,128)(2,1)} fusion(f32[64,2304]{1,0:T(8,128)S(1)} %get-tuple-element.83, bf16[64,2304]{1,0:T(8,128)(2,1)S(1)} %collective-permute-done.15, bf16[64,2304]{1,0:T(8,128)(2,1)S(1)} %collective-permute-done.18, bf16[64,2304]{1,0:T(8,128)(2,1)S(1)} %collective-permute-done.17, bf16[64,2304]{1,0:T(8,128)(2,1)S(1)} %collective-permute-done.16, ...), kind=kLoop, calls=%fused_computation.6 | loop fusion | flops 1474560 | bytes 2064385 | tf_op jit(solution)/shard_map/convert_element_type | solution.py:499
  (8 shorter events, 0.1 us)
Async XLA Ops:
  0.8 7.5 %collective-permute-start = (bf16[3,16,1024]{2,1,0:T(8,128)(2,1)S(1)}, bf16[3,16,1024]{2,1,0:T(8,128)(2,1)S(1)}, u32[]{:S(2)}, u32[]{:S(2)}) collective-permute-start(bf16[3,16,1024]{2,1,0:T(8,128)(2,1)S(1)} %shard_map.91), channel_id=1, source_target_pairs={{0,4},{4,8},{8,12},{12,16},{16,20},{20,24},{24,28},{1,5},{5,9},{9,... | collective-permute-start | bytes 294920 | tf_op jit(solution)/shard_map/ppermute | solution.py:354
  14.5 6.1 %collective-permute-start.1 = (bf16[272,128]{1,0:T(8,128)(2,1)S(1)}, bf16[272,128]{1,0:T(8,128)(2,1)S(1)}, u32[]{:S(2)}, u32[]{:S(2)}) collective-permute-start(bf16[272,128]{1,0:T(8,128)(2,1)S(1)} %get-tuple-element.49), channel_id=1, source_target_pairs={{0,4},{4,0},{8,12},{12,8},{16,20},{20,16},{24,28},{28,24},{1,5},{5... | collective-permute-start | bytes 208904 | tf_op jit(solution)/shard_map/ppermute | solution.py:398
  17.1 4.8 %collective-permute-start.2 = (bf16[272,128]{1,0:T(8,128)(2,1)S(1)}, bf16[272,128]{1,0:T(8,128)(2,1)S(1)}, u32[]{:S(2)}, u32[]{:S(2)}) collective-permute-start(bf16[272,128]{1,0:T(8,128)(2,1)S(1)} %get-tuple-element.50), channel_id=1, source_target_pairs={{0,8},{4,12},{8,0},{12,4},{16,24},{20,28},{24,16},{28,20},{1,9},{5... | collective-permute-start | bytes 208904 | tf_op jit(solution)/shard_map/ppermute | solution.py:398
  18.6 7.8 %collective-permute-start.3 = (bf16[272,128]{1,0:T(8,128)(2,1)}, bf16[272,128]{1,0:T(8,128)(2,1)S(1)}, u32[]{:S(2)}, u32[]{:S(2)}) collective-permute-start(bf16[272,128]{1,0:T(8,128)(2,1)} %get-tuple-element.51), channel_id=1, source_target_pairs={{0,12},{4,8},{8,4},{12,0},{16,28},{20,24},{24,20},{28,16},{1,13},{... | collective-permute-start | bytes 208904 | tf_op jit(solution)/shard_map/ppermute | solution.py:398
  18.6 7.8 %collective-permute-start.4 = (bf16[272,128]{1,0:T(8,128)(2,1)}, bf16[272,128]{1,0:T(8,128)(2,1)}, u32[]{:S(2)}, u32[]{:S(2)}) collective-permute-start(bf16[272,128]{1,0:T(8,128)(2,1)} %get-tuple-element.52), channel_id=1, source_target_pairs={{0,16},{4,20},{8,24},{12,28},{16,0},{20,4},{24,8},{28,12},{1,17},{... | collective-permute-start | bytes 208904 | tf_op jit(solution)/shard_map/ppermute | solution.py:398
  20.0 7.7 %collective-permute-start.5 = (bf16[272,128]{1,0:T(8,128)(2,1)}, bf16[272,128]{1,0:T(8,128)(2,1)}, u32[]{:S(2)}, u32[]{:S(2)}) collective-permute-start(bf16[272,128]{1,0:T(8,128)(2,1)} %get-tuple-element.53), channel_id=1, source_target_pairs={{0,20},{4,16},{8,28},{12,24},{16,4},{20,0},{24,12},{28,8},{1,21},{... | collective-permute-start | bytes 208904 | tf_op jit(solution)/shard_map/ppermute | solution.py:398
  20.6 7.1 %collective-permute-start.6 = (bf16[272,128]{1,0:T(8,128)(2,1)}, bf16[272,128]{1,0:T(8,128)(2,1)}, u32[]{:S(2)}, u32[]{:S(2)}) collective-permute-start(bf16[272,128]{1,0:T(8,128)(2,1)} %get-tuple-element.54), channel_id=1, source_target_pairs={{0,24},{4,28},{8,16},{12,20},{16,8},{20,12},{24,0},{28,4},{1,25},{... | collective-permute-start | bytes 208904 | tf_op jit(solution)/shard_map/ppermute | solution.py:398
  21.9 5.9 %collective-permute-start.7 = (bf16[272,128]{1,0:T(8,128)(2,1)}, bf16[272,128]{1,0:T(8,128)(2,1)}, u32[]{:S(2)}, u32[]{:S(2)}) collective-permute-start(bf16[272,128]{1,0:T(8,128)(2,1)} %get-tuple-element.55), channel_id=1, source_target_pairs={{0,28},{4,24},{8,20},{12,16},{16,12},{20,8},{24,4},{28,0},{1,29},{... | collective-permute-start | bytes 208904 | tf_op jit(solution)/shard_map/ppermute | solution.py:398
  29.7 6.1 %collective-permute-start.8 = (bf16[128,128]{1,0:T(8,128)(2,1)S(1)}, bf16[128,128]{1,0:T(8,128)(2,1)S(1)}, u32[]{:S(2)}, u32[]{:S(2)}) collective-permute-start(bf16[128,128]{1,0:T(8,128)(2,1)S(1)} %get-tuple-element.93), channel_id=1, source_target_pairs={{0,4},{4,0},{8,12},{12,8},{16,20},{20,16},{24,28},{28,24},{1,5},{5... | collective-permute-start | bytes 98312 | tf_op jit(solution)/shard_map/ppermute | solution.py:398
  29.9 7.3 %collective-permute-start.9 = (bf16[128,128]{1,0:T(8,128)(2,1)S(1)}, bf16[128,128]{1,0:T(8,128)(2,1)S(1)}, u32[]{:S(2)}, u32[]{:S(2)}) collective-permute-start(bf16[128,128]{1,0:T(8,128)(2,1)S(1)} %get-tuple-element.92), channel_id=1, source_target_pairs={{0,8},{4,12},{8,0},{12,4},{16,24},{20,28},{24,16},{28,20},{1,9},{5... | collective-permute-start | bytes 98312 | tf_op jit(solution)/shard_map/ppermute | solution.py:398
  31.5 7.0 %collective-permute-start.10 = (bf16[128,128]{1,0:T(8,128)(2,1)S(1)}, bf16[128,128]{1,0:T(8,128)(2,1)S(1)}, u32[]{:S(2)}, u32[]{:S(2)}) collective-permute-start(bf16[128,128]{1,0:T(8,128)(2,1)S(1)} %get-tuple-element.91), channel_id=1, source_target_pairs={{0,12},{4,8},{8,4},{12,0},{16,28},{20,24},{24,20},{28,16},{1,13},{... | collective-permute-start | bytes 98312 | tf_op jit(solution)/shard_map/ppermute | solution.py:398
  31.6 6.9 %collective-permute-start.11 = (bf16[128,128]{1,0:T(8,128)(2,1)S(1)}, bf16[128,128]{1,0:T(8,128)(2,1)S(1)}, u32[]{:S(2)}, u32[]{:S(2)}) collective-permute-start(bf16[128,128]{1,0:T(8,128)(2,1)S(1)} %get-tuple-element.90), channel_id=1, source_target_pairs={{0,16},{4,20},{8,24},{12,28},{16,0},{20,4},{24,8},{28,12},{1,17},{... | collective-permute-start | bytes 98312 | tf_op jit(solution)/shard_map/ppermute | solution.py:398
  33.3 5.3 %collective-permute-start.12 = (bf16[128,128]{1,0:T(8,128)(2,1)S(1)}, bf16[128,128]{1,0:T(8,128)(2,1)S(1)}, u32[]{:S(2)}, u32[]{:S(2)}) collective-permute-start(bf16[128,128]{1,0:T(8,128)(2,1)S(1)} %get-tuple-element.89), channel_id=1, source_target_pairs={{0,20},{4,16},{8,28},{12,24},{16,4},{20,0},{24,12},{28,8},{1,21},{... | collective-permute-start | bytes 98312 | tf_op jit(solution)/shard_map/ppermute | solution.py:398
  35.8 4.9 %collective-permute-start.13 = (bf16[128,128]{1,0:T(8,128)(2,1)S(1)}, bf16[128,128]{1,0:T(8,128)(2,1)S(1)}, u32[]{:S(2)}, u32[]{:S(2)}) collective-permute-start(bf16[128,128]{1,0:T(8,128)(2,1)S(1)} %get-tuple-element.88), channel_id=1, source_target_pairs={{0,24},{4,28},{8,16},{12,20},{16,8},{20,12},{24,0},{28,4},{1,25},{... | collective-permute-start | bytes 98312 | tf_op jit(solution)/shard_map/ppermute | solution.py:398
  37.2 4.3 %collective-permute-start.14 = (bf16[128,128]{1,0:T(8,128)(2,1)S(1)}, bf16[128,128]{1,0:T(8,128)(2,1)S(1)}, u32[]{:S(2)}, u32[]{:S(2)}) collective-permute-start(bf16[128,128]{1,0:T(8,128)(2,1)S(1)} %get-tuple-element.87), channel_id=1, source_target_pairs={{0,28},{4,24},{8,20},{12,16},{16,12},{20,8},{24,4},{28,0},{1,29},{... | collective-permute-start | bytes 98312 | tf_op jit(solution)/shard_map/ppermute | solution.py:398
  43.2 9.1 %collective-permute-start.15 = (bf16[64,2304]{1,0:T(8,128)(2,1)S(1)}, bf16[64,2304]{1,0:T(8,128)(2,1)S(1)}, u32[]{:S(2)}, u32[]{:S(2)}) collective-permute-start(bf16[64,2304]{1,0:T(8,128)(2,1)S(1)} %get-tuple-element.84), channel_id=1, source_target_pairs={{0,1},{1,0},{2,3},{3,2},{4,5},{5,4},{6,7},{7,6},{8,9},{9,8},{10,11... | collective-permute-start | bytes 884744 | tf_op jit(solution)/shard_map/ppermute | solution.py:485
  44.9 9.4 %collective-permute-start.17 = (bf16[64,2304]{1,0:T(8,128)(2,1)S(1)}, bf16[64,2304]{1,0:T(8,128)(2,1)S(1)}, u32[]{:S(2)}, u32[]{:S(2)}) collective-permute-start(bf16[64,2304]{1,0:T(8,128)(2,1)S(1)} %get-tuple-element.85), channel_id=1, source_target_pairs={{1,2},{2,1},{5,6},{6,5},{9,10},{10,9},{13,14},{14,13},{17,18},{18,... | collective-permute-start | bytes 884744 | tf_op jit(solution)/shard_map/ppermute | solution.py:487
  45.6 13.2 %collective-permute-start.16 = (bf16[64,2304]{1,0:T(8,128)(2,1)S(1)}, bf16[64,2304]{1,0:T(8,128)(2,1)S(1)}, u32[]{:S(2)}, u32[]{:S(2)}) collective-permute-start(bf16[64,2304]{1,0:T(8,128)(2,1)S(1)} %get-tuple-element.85), channel_id=1, source_target_pairs={{0,2},{3,1},{4,6},{7,5},{8,10},{11,9},{12,14},{15,13},{16,18},{19,... | collective-permute-start | bytes 884744 | tf_op jit(solution)/shard_map/ppermute | solution.py:486
  52.5 16.6 %collective-permute-start.18 = (bf16[64,2304]{1,0:T(8,128)(2,1)S(1)}, bf16[64,2304]{1,0:T(8,128)(2,1)S(1)}, u32[]{:S(2)}, u32[]{:S(2)}) collective-permute-start(bf16[64,2304]{1,0:T(8,128)(2,1)S(1)} %fusion.6), channel_id=1, source_target_pairs={{0,1},{3,2},{1,3},{2,0},{4,5},{7,6},{5,7},{6,4},{8,9},{11,10},{9,1... | collective-permute-start | bytes 884744 | tf_op jit(solution)/shard_map/ppermute | solution.py:489

commit v3 on v2

--- a/solution.py
+++ b/solution.py
@@ -254,13 +254,13 @@
 
 
 def scan_kernel(count, where, *refs):
-    tables, (states_out, table) = refs[:count], refs[count:]
+    tables, outs, (states, table) = refs[:count], refs[count:-2], refs[-2:]
     for slot in range(count):
         table[slot] = tables[slot][...]
     state = jnp.zeros((DK, DK), F32)
     for shard in range(count):
         slot = lax.bitwise_xor(where[0], shard)
-        states_out[slot] = state.astype(BF16)
+        states[slot] = state.astype(BF16)
         if shard < count - 1:
             high = table[slot, 2 * DK : 2 * DK + 1, :].astype(F32)
             low = table[slot, 2 * DK + 8 : 2 * DK + 9, :].astype(F32)
@@ -269,6 +269,20 @@
                 - dot(state.astype(BF16), table[slot, 0:DK, :], NN)
                 + table[slot, DK : 2 * DK, :].astype(F32)
             )
+    for pair, out in enumerate(outs):
+        out[...] = states[2 * pair : 2 * pair + 2]
+
+
+def fetch_kernel(source, out, arrived):
+    copy = pltpu.make_async_copy(source.at[:, 0 : out.shape[1]], out, arrived)
+    copy.start()
+    copy.wait()
+
+
+def gather_kernel(*refs):
+    *pairs, out = refs
+    for i, pair in enumerate(pairs):
+        out[i] = pair[1]
 
 
 def tail_kernel(query, key, value, out):
@@ -277,8 +291,15 @@
     out[2] = value[...]
 
 
-def project_kernel(heads, owners, where, mine, direct_one, direct_two, weight_one, weight_two, matrix, states, *rest):
-    *outs, head_out, ordered = rest
+def project_kernel(heads, owners, where, mine, direct_one, direct_two, weight_one, weight_two, early, matrix, *rest):
+    arrived, rest = rest[: heads // 2 + 1], rest[heads // 2 + 1 :]
+    *outs, head_out, ordered, states, late, landed = rest
+    half_width = early.shape[1]
+    copy = pltpu.make_async_copy(matrix.at[:, half_width:], late, landed)
+    copy.start()
+    for pair in range(heads // 2):
+        states[2 * pair] = arrived[pair][0]
+        states[2 * pair + 1] = arrived[-1][pair]
     parts = len(owners)
     share = head_out.shape[0] // parts
 
@@ -299,11 +320,15 @@
                 pl.ds(pl.multiple_of(owner * share, share), share), :
             ]
 
-    total = dot(ordered[...], matrix[...], NN)
-    for distance in range(parts):
-        outs[distance][...] = total[distance * share : (distance + 1) * share, :].astype(
-            outs[distance].dtype
-        )
+    for side in range(2):
+        if side == 1:
+            copy.wait()
+        total = dot(ordered[...], (early, late)[side][...], NN)
+        at = slice(side * half_width, side * half_width + total.shape[1])
+        for distance in range(parts):
+            outs[distance][:, at] = total[distance * share : (distance + 1) * share, :].astype(
+                outs[distance].dtype
+            )
 
 
 def spec(shape, index):
@@ -339,6 +364,7 @@
     shape = jax.ShapeDtypeStruct
     kept = pltpu.VMEM
     here = pl.BlockSpec(memory_space=pltpu.VMEM)
+    anywhere = pl.BlockSpec(memory_space=pl.ANY)
     query, key_in, value, gates, beta_rows, conv_query, conv_key, conv_value, out_weight = (
         pltpu.with_memory_space_constraint(data, pltpu.HBM)
         for data in (
@@ -419,17 +445,17 @@
             first_solved, later_solved, first_forward, later_forward, carry, out_weight,
         )
 
-    direct_one, weight_one, matrix = outputs(0, later_solved, True)
+    direct_one, weight_one = outputs(0, later_solved, False)
     if spread:
         arrived = exchange(send)
-        arrived, direct_one, weight_one, matrix = lax.optimization_barrier((arrived, direct_one, weight_one, matrix))
+        arrived, direct_one, weight_one = lax.optimization_barrier((arrived, direct_one, weight_one))
         states = call(
             functools.partial(scan_kernel, ranks),
             (1,),
             [here] * ranks,
-            spec((ranks, DK, DK), lambda p, *_: (0, 0, 0)),
-            shape((ranks, DK, DK), BF16),
-            [pltpu.VMEM((ranks, packed, DK), BF16)],
+            [here] * (ranks // 2),
+            [shape((2, DK, DK), BF16)] * (ranks // 2),
+            [pltpu.VMEM((ranks, DK, DK), BF16), pltpu.VMEM((ranks, packed, DK), BF16)],
             (ranks * 4_000_000, 1 << 20),
             LIMIT,
             1,
@@ -437,10 +463,17 @@
         )
         states, later_solved = lax.optimization_barrier((states, later_solved))
         direct_two, weight_two = outputs(1, later_solved, False)
-        states = jnp.stack(exchange(states))
-        states, direct_two, weight_two, matrix = lax.optimization_barrier(
-            (states, direct_two, weight_two, matrix)
+        states = [states[0]] + [
+            lax.ppermute(states[d], "seq", [(i, i ^ (2 * d)) for i in range(ranks)])
+            for d in range(1, ranks // 2)
+        ]
+        states, direct_two, weight_two = lax.optimization_barrier((states, direct_two, weight_two))
+        aside = call(
+            gather_kernel, (1,), [here] * (ranks // 2), here,
+            shape((ranks // 2, DK, DK), BF16), [], (0, 1 << 18), LIMIT, 0, *states,
         )
+        aside, source = lax.optimization_barrier((aside, out_weight))
+        states = states + [lax.ppermute(aside, "seq", [(i, i ^ 1) for i in range(ranks)])]
     else:
         direct_two, weight_two = outputs(1, later_solved, False)
         every = lax.all_gather(jnp.stack(send), "seq")
@@ -453,6 +486,8 @@
             moved = jnp.einsum("hij,hjk->hik", state, product[shard], precision=lax.Precision.HIGHEST)
             state = state * decay[shard] - moved + offset[shard]
         states = states.astype(BF16)
+        source = out_weight
+        states = [states[i : i + 2] for i in range(0, groups, 2)] + [states[1::2]]
 
     parts = lax.axis_size("head")
     mine = lax.axis_index("head").astype(jnp.int32)
@@ -467,27 +502,37 @@
         )
     else:
         owners = [lambda z, d=d: lax.rem(z + d, parts) for d in range(parts)]
+    half = model // 2
+    early = call(
+        fetch_kernel, (1,), [anywhere], here, kept((width, half), BF16),
+        [pltpu.SemaphoreType.DMA], (0, width * model * 2), LIMIT, 0, source,
+    )
     own, *leaving = call(
         functools.partial(project_kernel, groups, owners),
         (1,),
-        [here] * 5 + [spec((groups, DK, DK), lambda p, *_: (0, 0, 0))],
+        [here] * 5 + [anywhere] + [here] * (groups // 2 + 1),
         [here] * parts,
         [kept((share, model), F32)] + [kept((share, model), BF16)] * (parts - 1),
-        [pltpu.VMEM((length, width), BF16)] * 2,
+        [pltpu.VMEM((length, width), BF16)] * 2
+        + [
+            pltpu.VMEM((groups, DK, DK), BF16),
+            pltpu.VMEM((width, model - half), BF16),
+            pltpu.SemaphoreType.DMA,
+        ],
         (2 * length * width * model, width * model * 2),
         LIMIT,
         2,
-        order[None], mine[None], direct_one, direct_two, weight_one, weight_two, matrix, states,
+        order[None], mine[None], direct_one, direct_two, weight_one, weight_two, early, source, *states,
     )
     if parts == 4:
         near, inward, last = leaving
         middle = (mine == 1) | (mine == 2)
         near = lax.ppermute(near, "head", [(0, 1), (1, 0), (2, 3), (3, 2)]).astype(F32)
+        crossed = lax.ppermute(inward, "head", [(1, 2), (2, 1)])
         skipped = lax.ppermute(inward, "head", [(0, 2), (3, 1)])
-        crossed = lax.ppermute(inward, "head", [(1, 2), (2, 1)])
         joined = (last.astype(F32) + jnp.where(middle, near, 0.0)).astype(BF16)
         joined = lax.ppermute(joined, "head", [(0, 1), (3, 2), (1, 3), (2, 0)])
-        arrived = [jnp.where(middle, 0.0, near), skipped, crossed, joined]
+        arrived = [jnp.where(middle, 0.0, near), crossed, skipped, joined]
     else:
         arrived = [
             lax.ppermute(part, "head", [(i, (i + d) % parts) for i in range(parts)])

time: 70.3 us -> 67.5 us (0.960)
  starting transfers between devices: 27.2 us -> 24.3 us
    ppermute x14 -> x7, starting transfers between devices: 14.9 us -> 8.56 us  [exchange(): lax.ppermute(blocks[m], 'seq', [(i, i ^ m) for i in range(ranks)])]
    ppermute x0 -> x4, starting transfers between devices: none -> 3.62 us  [the longest x3 3.55 us: shards(): lax.ppermute(states[d], 'seq', [(i, i ^ 2 * d) for i in range(ranks)])]
    ppermute x14 -> x7, waiting for transfers between devices: 4.29 us -> 2.16 us  [exchange(): lax.ppermute(blocks[m], 'seq', [(i, i ^ m) for i in range(ranks)])]
    ppermute x0 -> x4, waiting for transfers between devices: none -> 1.46 us  [the longest x3 1.46 us: shards(): lax.ppermute(states[d], 'seq', [(i, i ^ 2 * d) for i in range(ranks)])]
    pallas_call x7 -> x9, Pallas kernels: 21.4 us -> 21.8 us  [call(): pl.pallas_call(kernel, grid_spec=pltpu.PrefetchScalarGridSpec(num_scalar_...]
  transfers between devices with their start and end apart: 19 -> 16, of which waited for: 6 -> 6; matrix products, arithmetic and copies ran while one was open for 0% -> 0% of each run, Pallas kernels for 16% -> 17%
where the time goes in v3:
time: 67.5 us; the launch traced here: 67.1 us
  starting transfers between devices  24.3 us (36%)
  Pallas kernels  21.8 us (32%)
  waiting for transfers between devices  19.8 us (29%)
  other arithmetic  0.99 us (1%)
    pallas_call x9, Pallas kernels, call(): pl.pallas_call(kernel, grid_spec=pltpu.PrefetchScalarGridSpec(num_scalar_...  21.8 us
    ppermute x1, waiting for transfers between devices, shards(): joined = lax.ppermute(joined, 'head', [(0, 1), (3, 2), (1, 3), (2, 0)])  10.7 us
    ppermute x7, starting transfers between devices, exchange(): lax.ppermute(blocks[m], 'seq', [(i, i ^ m) for i in range(ranks)])  8.56 us
    ppermute x1, starting transfers between devices, shards(): skipped = lax.ppermute(inward, 'head', [(0, 2), (3, 1)])  5.75 us
    ppermute x1, waiting for transfers between devices, shards(): skipped = lax.ppermute(inward, 'head', [(0, 2), (3, 1)])  4.14 us
    ppermute x3, starting transfers between devices, shards(): lax.ppermute(states[d], 'seq', [(i, i ^ 2 * d) for i in range(ranks)])  3.55 us
    ppermute x1, starting transfers between devices, shards(): rims = lax.ppermute(rims, 'seq', [(i, i + 1) for i in range(ranks - 1)])  2.35 us
    ppermute x7, waiting for transfers between devices, exchange(): lax.ppermute(blocks[m], 'seq', [(i, i ^ m) for i in range(ranks)])  2.16 us
  transfers between devices with their start and end apart: 16, of which 6 were waited for; matrix products, arithmetic and copies ran while one was open for 0% of the time, Pallas kernels for 17%

profile of v3, /device:TPU:0, one launch (start us, length us, event | category | flops | bytes accessed | tf_op | source)
XLA Modules:
  0.0 67.1 jit_solution(8640736879982134467)
XLA Ops:
  0.0 0.8 %shard_map.91 = bf16[3,16,1024]{2,1,0:T(8,128)(2,1)S(1)} custom-call(bf16[256,1024]{1,0:T(8,128)(2,1)} %query.5, bf16[256,1024]{1,0:T(8,128)(2,1)} %key.5, bf16[256,1024]{1,0:T(8,128)(2,1)} %value.5), custom_call_target="tpu_custom_call" | custom-call | bytes 196608 | tf_op jit(solution)/shard_map/pallas_call | solution.py:339
  0.8 2.4 %collective-permute-start = (bf16[3,16,1024]{2,1,0:T(8,128)(2,1)S(1)}, bf16[3,16,1024]{2,1,0:T(8,128)(2,1)S(1)}, u32[]{:S(2)}, u32[]{:S(2)}) collective-permute-start(bf16[3,16,1024]{2,1,0:T(8,128)(2,1)S(1)} %shard_map.91), channel_id=1, source_target_pairs={{0,4},{4,8},{8,12},{12,16},{16,20},{20,24},{24,28},{1,5},{5,9},{9,... | collective-permute-start | bytes 294920 | tf_op jit(solution)/shard_map/ppermute | solution.py:380
  3.2 5.2 %shard_map.92 = (f32[8,256,128]{2,1,0:T(8,128)S(1)}, f32[8,8,128]{2,1,0:T(8,128)S(1)}, f32[8,128,256]{2,1,0:T(8,128)S(1)}, bf16[128,1024]{1,0:T(8,128)(2,1)S(1)}) custom-call(bf16[256,1024]{1,0:T(8,128)(2,1)} %key.5, bf16[256,1024]{1,0:T(8,128)(2,1)} %value.5, bf16[256,1024]{1,0:T(8,128)(2,1)} %gate.7, f32[8,256]{1,0:T(8,128)} %bitcast.3, ...), custom_call_target="tpu_custom_call" | custom-call | flops 800000000 | bytes 4194304 | tf_op jit(solution)/shard_map/pallas_call | solution.py:339
  8.3 0.0 collective-permute-done.rims
  8.3 5.5 %shard_map.93 = (bf16[8,256,128]{2,1,0:T(8,128)(2,1)S(1)}, f32[8,128,256]{2,1,0:T(8,128)S(1)}, bf16[128,1024]{1,0:T(8,128)(2,1)S(1)}, bf16[272,128]{1,0:T(8,128)...) custom-call(s32[1]{0:T(128)} %bitcast.where, ...), custom_call_target="tpu_custom_call" | custom-call | flops 800000000 | bytes 4194304 | tf_op jit(solution)/shard_map/pallas_call | solution.py:339
  13.8 2.7 %collective-permute-start.1 = (bf16[272,128]{1,0:T(8,128)(2,1)S(1)}, bf16[272,128]{1,0:T(8,128)(2,1)S(1)}, u32[]{:S(2)}, u32[]{:S(2)}) collective-permute-start(bf16[272,128]{1,0:T(8,128)(2,1)S(1)} %get-tuple-element.58), channel_id=1, source_target_pairs={{0,4},{4,0},{8,12},{12,8},{16,20},{20,16},{24,28},{28,24},{1,5},{5... | collective-permute-start | bytes 208904 | tf_op jit(solution)/shard_map/ppermute | solution.py:424
  16.5 1.5 %collective-permute-start.2 = (bf16[272,128]{1,0:T(8,128)(2,1)S(1)}, bf16[272,128]{1,0:T(8,128)(2,1)S(1)}, u32[]{:S(2)}, u32[]{:S(2)}) collective-permute-start(bf16[272,128]{1,0:T(8,128)(2,1)S(1)} %get-tuple-element.59), channel_id=1, source_target_pairs={{0,8},{4,12},{8,0},{12,4},{16,24},{20,28},{24,16},{28,20},{1,9},{5... | collective-permute-start | bytes 208904 | tf_op jit(solution)/shard_map/ppermute | solution.py:424
  18.0 0.0 collective-permute-start.3
  18.0 1.5 %collective-permute-start.4 = (bf16[272,128]{1,0:T(8,128)(2,1)S(1)}, bf16[272,128]{1,0:T(8,128)(2,1)S(1)}, u32[]{:S(2)}, u32[]{:S(2)}) collective-permute-start(bf16[272,128]{1,0:T(8,128)(2,1)S(1)} %get-tuple-element.61), channel_id=1, source_target_pairs={{0,16},{4,20},{8,24},{12,28},{16,0},{20,4},{24,8},{28,12},{1,17},{... | collective-permute-start | bytes 208904 | tf_op jit(solution)/shard_map/ppermute | solution.py:424
  19.5 0.5 collective-permute-start.5
  20.0 0.0 collective-permute-done.1.refs_1_
  20.0 1.3 %collective-permute-start.6 = (bf16[272,128]{1,0:T(8,128)(2,1)S(1)}, bf16[272,128]{1,0:T(8,128)(2,1)S(1)}, u32[]{:S(2)}, u32[]{:S(2)}) collective-permute-start(bf16[272,128]{1,0:T(8,128)(2,1)S(1)} %get-tuple-element.63), channel_id=1, source_target_pairs={{0,24},{4,28},{8,16},{12,20},{16,8},{20,12},{24,0},{28,4},{1,25},{... | collective-permute-start | bytes 208904 | tf_op jit(solution)/shard_map/ppermute | solution.py:424
  21.3 0.0 collective-permute-done.2.refs_2_
  21.3 1.1 %collective-permute-start.7 = (bf16[272,128]{1,0:T(8,128)(2,1)S(1)}, bf16[272,128]{1,0:T(8,128)(2,1)S(1)}, u32[]{:S(2)}, u32[]{:S(2)}) collective-permute-start(bf16[272,128]{1,0:T(8,128)(2,1)S(1)} %get-tuple-element.64), channel_id=1, source_target_pairs={{0,28},{4,24},{8,20},{12,16},{16,12},{20,8},{24,4},{28,0},{1,29},{... | collective-permute-start | bytes 208904 | tf_op jit(solution)/shard_map/ppermute | solution.py:424
  22.4 2.3 %shard_map.94 = (f32[256,512]{1,0:T(8,128)S(1)}, bf16[256,512]{1,0:T(8,128)(2,1)S(1)}) custom-call(bf16[256,1024]{1,0:T(8,128)(2,1)} %query.5, bf16[256,1024]{1,0:T(8,128)(2,1)} %gate.7, bf16[3,16,1024]{2,1,0:T(8,128)(2,1)S(1)} %collective-permute-done.rims, bf16[4,1024]{1,0:T(4,128)(2,1)} %query_taps.3, f32[8,128,256]{2,1,0:T(8,128)S(1)} %get-tuple-element.65.first_solved, ...), custom_call_target="tpu_custom_call" | custom-call | flops 400000000 | bytes 2097152 | tf_op jit(solution)/shard_map/pallas_call | solution.py:339
  24.7 0.0 collective-permute-done.3.refs_3_
  24.7 0.0 collective-permute-done.4.refs_4_
  24.8 2.1 %collective-permute-done.5.refs_5_ = bf16[272,128]{1,0:T(8,128)(2,1)S(1)} collective-permute-done((bf16[272,128]{1,0:T(8,128)(2,1)S(1)}, bf16[272,128]{1,0:T(8,128)(2,1)S(1)}, u32[]{:S(2)}, u32[]{:S(2)}) %collective-permute-start.5) | collective-permute-done | bytes 69664 | tf_op jit(solution)/shard_map/ppermute | solution.py:424
  26.9 0.0 collective-permute-done.6.refs_6_
  26.9 0.0 collective-permute-done.7.refs_7_
  26.9 0.9 %shard_map.95 = (bf16[2,128,128]{2,1,0:T(8,128)(2,1)S(1)}, bf16[2,128,128]{2,1,0:T(8,128)(2,1)S(1)}, bf16[2,128,128]{2,1,0:T(8,128)(2,1)S(1)}, bf16[2,128,128]{2,1,0:T(8,128)(2,1)S(1)}) custom-call(s32[1]{0:T(128)} %bitcast.where, bf16[272,128]{1,0:T(8,128)(2,1)S(1)} %get-tuple-element.73.refs_0_, bf16[272,128]{1,0:T(8,128)(2,1)S(1)} %collective-permute-done.1.refs_1_, ...), custom_call_target="tpu_custom_call" | custom-call | flops 32000000 | bytes 1048576 | tf_op jit(solution)/shard_map/pallas_call | solution.py:339
  27.8 1.4 %collective-permute-start.10 = (bf16[2,128,128]{2,1,0:T(8,128)(2,1)S(1)}, bf16[2,128,128]{2,1,0:T(8,128)(2,1)S(1)}, u32[]{:S(2)}, u32[]{:S(2)}) collective-permute-start(bf16[2,128,128]{2,1,0:T(8,128)(2,1)S(1)} %get-tuple-element.88), channel_id=1, source_target_pairs={{0,24},{4,28},{8,16},{12,20},{16,8},{20,12},{24,0},{28,4},{1,25},{... | collective-permute-start | bytes 196616 | tf_op jit(solution)/shard_map/ppermute | solution.py:467
  29.3 1.6 %collective-permute-start.8 = (bf16[2,128,128]{2,1,0:T(8,128)(2,1)S(1)}, bf16[2,128,128]{2,1,0:T(8,128)(2,1)S(1)}, u32[]{:S(2)}, u32[]{:S(2)}) collective-permute-start(bf16[2,128,128]{2,1,0:T(8,128)(2,1)S(1)} %get-tuple-element.86), channel_id=1, source_target_pairs={{0,8},{4,12},{8,0},{12,4},{16,24},{20,28},{24,16},{28,20},{1,9},{5... | collective-permute-start | bytes 196616 | tf_op jit(solution)/shard_map/ppermute | solution.py:467
  30.9 0.5 collective-permute-start.9
  31.4 2.3 %shard_map.96 = (f32[256,512]{1,0:T(8,128)S(1)}, bf16[256,512]{1,0:T(8,128)(2,1)S(1)}) custom-call(bf16[256,1024]{1,0:T(8,128)(2,1)} %query.5, bf16[256,1024]{1,0:T(8,128)(2,1)} %gate.7, bf16[3,16,1024]{2,1,0:T(8,128)(2,1)S(1)} %collective-permute-done.rims, bf16[4,1024]{1,0:T(4,128)(2,1)} %query_taps.3, f32[8,128,256]{2,1,0:T(8,128)S(1)} %get-tuple-element.65.first_solved, ...), custom_call_target="tpu_custom_call" | custom-call | flops 400000000 | bytes 2097152 | tf_op jit(solution)/shard_map/pallas_call | solution.py:339
  33.7 0.0 collective-permute-done.10.refs_3_.rest_3_
  33.7 0.7 %collective-permute-done.8.refs_1_.rest_1_ = bf16[2,128,128]{2,1,0:T(8,128)(2,1)S(1)} collective-permute-done((bf16[2,128,128]{2,1,0:T(8,128)(2,1)S(1)}, bf16[2,128,128]{2,1,0:T(8,128)(2,1)S(1)}, u32[]{:S(2)}, u32[]{:S(2)}) %collective-permute-start.8) | collective-permute-done | bytes 65568 | tf_op jit(solution)/shard_map/ppermute | solution.py:467
  34.4 0.8 %collective-permute-done.9.refs_2_.rest_2_ = bf16[2,128,128]{2,1,0:T(8,128)(2,1)S(1)} collective-permute-done((bf16[2,128,128]{2,1,0:T(8,128)(2,1)S(1)}, bf16[2,128,128]{2,1,0:T(8,128)(2,1)S(1)}, u32[]{:S(2)}, u32[]{:S(2)}) %collective-permute-start.9) | collective-permute-done | bytes 65568 | tf_op jit(solution)/shard_map/ppermute | solution.py:467
  35.2 0.1 collective-permute-start.11
  35.3 1.7 %shard_map.98.early = bf16[1024,1152]{1,0:T(8,128)(2,1)S(1)} custom-call(bf16[1024,2304]{1,0:T(8,128)(2,1)} %matrix.4), custom_call_target="tpu_custom_call" | custom-call | bytes 4718592 | tf_op jit(solution)/shard_map/pallas_call | solution.py:339
  37.0 0.0 collective-permute-done.11.rest_4_
  37.0 3.1 %shard_map.99 = (f32[64,2304]{1,0:T(8,128)S(1)}, bf16[64,2304]{1,0:T(8,128)(2,1)S(1)}, bf16[64,2304]{1,0:T(8,128)(2,1)S(1)}, bf16[64,2304]{1,0:T(8,128)(2,1)S(1)}) custom-call(s32[1]{0:T(128)} %bitcast.where, s32[1]{0:T(128)} %bitcast.1.mine, f32[256,512]{1,0:T(8,128)S(1)} %get-tuple-element.72.direct_one, f32[256,512]{1,0:T(8,128)S(1)} %get-tuple-element.92.direct_two, ...), custom_call_target="tpu_custom_call" | custom-call | flops 1207959552 | bytes 4718592 | tf_op jit(solution)/shard_map/pallas_call | solution.py:339
  40.1 1.6 %collective-permute-start.12 = (bf16[64,2304]{1,0:T(8,128)(2,1)S(1)}, bf16[64,2304]{1,0:T(8,128)(2,1)S(1)}, u32[]{:S(2)}, u32[]{:S(2)}) collective-permute-start(bf16[64,2304]{1,0:T(8,128)(2,1)S(1)} %get-tuple-element.102), channel_id=1, source_target_pairs={{0,1},{1,0},{2,3},{3,2},{4,5},{5,4},{6,7},{7,6},{8,9},{9,8},{10,11... | collective-permute-start | bytes 884744 | tf_op jit(solution)/shard_map/ppermute | solution.py:530
  41.7 0.7 collective-permute-start.13
  42.4 5.8 %collective-permute-start.14 = (bf16[64,2304]{1,0:T(8,128)(2,1)S(1)}, bf16[64,2304]{1,0:T(8,128)(2,1)S(1)}, u32[]{:S(2)}, u32[]{:S(2)}) collective-permute-start(bf16[64,2304]{1,0:T(8,128)(2,1)S(1)} %get-tuple-element.103), channel_id=1, source_target_pairs={{0,2},{3,1},{4,6},{7,5},{8,10},{11,9},{12,14},{15,13},{16,18},{19,... | collective-permute-start | bytes 884744 | tf_op jit(solution)/shard_map/ppermute | solution.py:532
  48.2 1.4 %collective-permute-done.12 = bf16[64,2304]{1,0:T(8,128)(2,1)S(1)} collective-permute-done((bf16[64,2304]{1,0:T(8,128)(2,1)S(1)}, bf16[64,2304]{1,0:T(8,128)(2,1)S(1)}, u32[]{:S(2)}, u32[]{:S(2)}) %collective-permute-start.12) | collective-permute-done | bytes 294944 | tf_op jit(solution)/shard_map/ppermute | solution.py:530
  49.6 0.1 fusion.6
  49.7 1.7 %collective-permute-start.15 = (bf16[64,2304]{1,0:T(8,128)(2,1)S(1)}, bf16[64,2304]{1,0:T(8,128)(2,1)S(1)}, u32[]{:S(2)}, u32[]{:S(2)}) collective-permute-start(bf16[64,2304]{1,0:T(8,128)(2,1)S(1)} %fusion.6), channel_id=1, source_target_pairs={{0,1},{3,2},{1,3},{2,0},{4,5},{7,6},{5,7},{6,4},{8,9},{11,10},{9,1... | collective-permute-start | bytes 884744 | tf_op jit(solution)/shard_map/ppermute | solution.py:534
  51.4 0.0 collective-permute-done.13
  51.4 4.1 %collective-permute-done.14 = bf16[64,2304]{1,0:T(8,128)(2,1)S(1)} collective-permute-done((bf16[64,2304]{1,0:T(8,128)(2,1)S(1)}, bf16[64,2304]{1,0:T(8,128)(2,1)S(1)}, u32[]{:S(2)}, u32[]{:S(2)}) %collective-permute-start.14) | collective-permute-done | bytes 294944 | tf_op jit(solution)/shard_map/ppermute | solution.py:532
  55.6 10.7 %collective-permute-done.15 = bf16[64,2304]{1,0:T(8,128)(2,1)S(1)} collective-permute-done((bf16[64,2304]{1,0:T(8,128)(2,1)S(1)}, bf16[64,2304]{1,0:T(8,128)(2,1)S(1)}, u32[]{:S(2)}, u32[]{:S(2)}) %collective-permute-start.15) | collective-permute-done | bytes 294944 | tf_op jit(solution)/shard_map/ppermute | solution.py:534
  66.2 0.9 %fusion.4 = bf16[64,2304]{1,0:T(8,128)(2,1)} fusion(f32[64,2304]{1,0:T(8,128)S(1)} %get-tuple-element.101, bf16[64,2304]{1,0:T(8,128)(2,1)S(1)} %collective-permute-done.12, bf16[64,2304]{1,0:T(8,128)(2,1)S(1)} %collective-permute-done.15, bf16[64,2304]{1,0:T(8,128)(2,1)S(1)} %collective-permute-done.14, bf16[64,2304]{1,0:T(8,128)(2,1)S(1)} %collective-permute-done.13, ...), kind=kLoop, calls=%fused_computation.6 | loop fusion | flops 1474560 | bytes 2064385 | tf_op jit(solution)/shard_map/convert_element_type | solution.py:544
  (1 shorter events, 0.0 us)
Async XLA Ops:
  0.8 7.5 %collective-permute-start = (bf16[3,16,1024]{2,1,0:T(8,128)(2,1)S(1)}, bf16[3,16,1024]{2,1,0:T(8,128)(2,1)S(1)}, u32[]{:S(2)}, u32[]{:S(2)}) collective-permute-start(bf16[3,16,1024]{2,1,0:T(8,128)(2,1)S(1)} %shard_map.91), channel_id=1, source_target_pairs={{0,4},{4,8},{8,12},{12,16},{16,20},{20,24},{24,28},{1,5},{5,9},{9,... | collective-permute-start | bytes 294920 | tf_op jit(solution)/shard_map/ppermute | solution.py:380
  13.8 6.2 %collective-permute-start.1 = (bf16[272,128]{1,0:T(8,128)(2,1)S(1)}, bf16[272,128]{1,0:T(8,128)(2,1)S(1)}, u32[]{:S(2)}, u32[]{:S(2)}) collective-permute-start(bf16[272,128]{1,0:T(8,128)(2,1)S(1)} %get-tuple-element.58), channel_id=1, source_target_pairs={{0,4},{4,0},{8,12},{12,8},{16,20},{20,16},{24,28},{28,24},{1,5},{5... | collective-permute-start | bytes 208904 | tf_op jit(solution)/shard_map/ppermute | solution.py:424
  16.5 4.8 %collective-permute-start.2 = (bf16[272,128]{1,0:T(8,128)(2,1)S(1)}, bf16[272,128]{1,0:T(8,128)(2,1)S(1)}, u32[]{:S(2)}, u32[]{:S(2)}) collective-permute-start(bf16[272,128]{1,0:T(8,128)(2,1)S(1)} %get-tuple-element.59), channel_id=1, source_target_pairs={{0,8},{4,12},{8,0},{12,4},{16,24},{20,28},{24,16},{28,20},{1,9},{5... | collective-permute-start | bytes 208904 | tf_op jit(solution)/shard_map/ppermute | solution.py:424
  18.0 6.7 %collective-permute-start.3 = (bf16[272,128]{1,0:T(8,128)(2,1)S(1)}, bf16[272,128]{1,0:T(8,128)(2,1)S(1)}, u32[]{:S(2)}, u32[]{:S(2)}) collective-permute-start(bf16[272,128]{1,0:T(8,128)(2,1)S(1)} %get-tuple-element.60), channel_id=1, source_target_pairs={{0,12},{4,8},{8,4},{12,0},{16,28},{20,24},{24,20},{28,16},{1,13},{... | collective-permute-start | bytes 208904 | tf_op jit(solution)/shard_map/ppermute | solution.py:424
  18.0 6.8 %collective-permute-start.4 = (bf16[272,128]{1,0:T(8,128)(2,1)S(1)}, bf16[272,128]{1,0:T(8,128)(2,1)S(1)}, u32[]{:S(2)}, u32[]{:S(2)}) collective-permute-start(bf16[272,128]{1,0:T(8,128)(2,1)S(1)} %get-tuple-element.61), channel_id=1, source_target_pairs={{0,16},{4,20},{8,24},{12,28},{16,0},{20,4},{24,8},{28,12},{1,17},{... | collective-permute-start | bytes 208904 | tf_op jit(solution)/shard_map/ppermute | solution.py:424
  19.5 7.4 %collective-permute-start.5 = (bf16[272,128]{1,0:T(8,128)(2,1)S(1)}, bf16[272,128]{1,0:T(8,128)(2,1)S(1)}, u32[]{:S(2)}, u32[]{:S(2)}) collective-permute-start(bf16[272,128]{1,0:T(8,128)(2,1)S(1)} %get-tuple-element.62), channel_id=1, source_target_pairs={{0,20},{4,16},{8,28},{12,24},{16,4},{20,0},{24,12},{28,8},{1,21},{... | collective-permute-start | bytes 208904 | tf_op jit(solution)/shard_map/ppermute | solution.py:424
  20.0 6.9 %collective-permute-start.6 = (bf16[272,128]{1,0:T(8,128)(2,1)S(1)}, bf16[272,128]{1,0:T(8,128)(2,1)S(1)}, u32[]{:S(2)}, u32[]{:S(2)}) collective-permute-start(bf16[272,128]{1,0:T(8,128)(2,1)S(1)} %get-tuple-element.63), channel_id=1, source_target_pairs={{0,24},{4,28},{8,16},{12,20},{16,8},{20,12},{24,0},{28,4},{1,25},{... | collective-permute-start | bytes 208904 | tf_op jit(solution)/shard_map/ppermute | solution.py:424
  21.3 5.6 %collective-permute-start.7 = (bf16[272,128]{1,0:T(8,128)(2,1)S(1)}, bf16[272,128]{1,0:T(8,128)(2,1)S(1)}, u32[]{:S(2)}, u32[]{:S(2)}) collective-permute-start(bf16[272,128]{1,0:T(8,128)(2,1)S(1)} %get-tuple-element.64), channel_id=1, source_target_pairs={{0,28},{4,24},{8,20},{12,16},{16,12},{20,8},{24,4},{28,0},{1,29},{... | collective-permute-start | bytes 208904 | tf_op jit(solution)/shard_map/ppermute | solution.py:424
  27.8 5.9 %collective-permute-start.10 = (bf16[2,128,128]{2,1,0:T(8,128)(2,1)S(1)}, bf16[2,128,128]{2,1,0:T(8,128)(2,1)S(1)}, u32[]{:S(2)}, u32[]{:S(2)}) collective-permute-start(bf16[2,128,128]{2,1,0:T(8,128)(2,1)S(1)} %get-tuple-element.88), channel_id=1, source_target_pairs={{0,24},{4,28},{8,16},{12,20},{16,8},{20,12},{24,0},{28,4},{1,25},{... | collective-permute-start | bytes 196616 | tf_op jit(solution)/shard_map/ppermute | solution.py:467
  29.3 5.1 %collective-permute-start.8 = (bf16[2,128,128]{2,1,0:T(8,128)(2,1)S(1)}, bf16[2,128,128]{2,1,0:T(8,128)(2,1)S(1)}, u32[]{:S(2)}, u32[]{:S(2)}) collective-permute-start(bf16[2,128,128]{2,1,0:T(8,128)(2,1)S(1)} %get-tuple-element.86), channel_id=1, source_target_pairs={{0,8},{4,12},{8,0},{12,4},{16,24},{20,28},{24,16},{28,20},{1,9},{5... | collective-permute-start | bytes 196616 | tf_op jit(solution)/shard_map/ppermute | solution.py:467
  30.9 4.3 %collective-permute-start.9 = (bf16[2,128,128]{2,1,0:T(8,128)(2,1)S(1)}, bf16[2,128,128]{2,1,0:T(8,128)(2,1)S(1)}, u32[]{:S(2)}, u32[]{:S(2)}) collective-permute-start(bf16[2,128,128]{2,1,0:T(8,128)(2,1)S(1)} %get-tuple-element.87), channel_id=1, source_target_pairs={{0,16},{4,20},{8,24},{12,28},{16,0},{20,4},{24,8},{28,12},{1,17},{... | collective-permute-start | bytes 196616 | tf_op jit(solution)/shard_map/ppermute | solution.py:467
  35.2 1.8 %collective-permute-start.11 = (bf16[4,128,128]{2,1,0:T(8,128)(2,1)S(1)}, bf16[4,128,128]{2,1,0:T(8,128)(2,1)S(1)}, u32[]{:S(2)}, u32[]{:S(2)}) collective-permute-start(bf16[4,128,128]{2,1,0:T(8,128)(2,1)S(1)} %shard_map.97), channel_id=1, source_target_pairs={{0,4},{4,0},{8,12},{12,8},{16,20},{20,16},{24,28},{28,24},{1,5},{5... | collective-permute-start | bytes 393224 | tf_op jit(solution)/shard_map/ppermute | solution.py:476
  40.1 9.5 %collective-permute-start.12 = (bf16[64,2304]{1,0:T(8,128)(2,1)S(1)}, bf16[64,2304]{1,0:T(8,128)(2,1)S(1)}, u32[]{:S(2)}, u32[]{:S(2)}) collective-permute-start(bf16[64,2304]{1,0:T(8,128)(2,1)S(1)} %get-tuple-element.102), channel_id=1, source_target_pairs={{0,1},{1,0},{2,3},{3,2},{4,5},{5,4},{6,7},{7,6},{8,9},{9,8},{10,11... | collective-permute-start | bytes 884744 | tf_op jit(solution)/shard_map/ppermute | solution.py:530
  41.7 9.7 %collective-permute-start.13 = (bf16[64,2304]{1,0:T(8,128)(2,1)S(1)}, bf16[64,2304]{1,0:T(8,128)(2,1)S(1)}, u32[]{:S(2)}, u32[]{:S(2)}) collective-permute-start(bf16[64,2304]{1,0:T(8,128)(2,1)S(1)} %get-tuple-element.103), channel_id=1, source_target_pairs={{1,2},{2,1},{5,6},{6,5},{9,10},{10,9},{13,14},{14,13},{17,18},{18,... | collective-permute-start | bytes 884744 | tf_op jit(solution)/shard_map/ppermute | solution.py:531
  42.4 13.1 %collective-permute-start.14 = (bf16[64,2304]{1,0:T(8,128)(2,1)S(1)}, bf16[64,2304]{1,0:T(8,128)(2,1)S(1)}, u32[]{:S(2)}, u32[]{:S(2)}) collective-permute-start(bf16[64,2304]{1,0:T(8,128)(2,1)S(1)} %get-tuple-element.103), channel_id=1, source_target_pairs={{0,2},{3,1},{4,6},{7,5},{8,10},{11,9},{12,14},{15,13},{16,18},{19,... | collective-permute-start | bytes 884744 | tf_op jit(solution)/shard_map/ppermute | solution.py:532
  49.7 16.6 %collective-permute-start.15 = (bf16[64,2304]{1,0:T(8,128)(2,1)S(1)}, bf16[64,2304]{1,0:T(8,128)(2,1)S(1)}, u32[]{:S(2)}, u32[]{:S(2)}) collective-permute-start(bf16[64,2304]{1,0:T(8,128)(2,1)S(1)} %fusion.6), channel_id=1, source_target_pairs={{0,1},{3,2},{1,3},{2,0},{4,5},{7,6},{5,7},{6,4},{8,9},{11,10},{9,1... | collective-permute-start | bytes 884744 | tf_op jit(solution)/shard_map/ppermute | solution.py:534

commit v4 on v3

--- a/solution.py
+++ b/solution.py
@@ -60,7 +60,7 @@
     for tap in range(number - 1):
         first = 8 - (number - 1) + tap
         total = total + taps[tap : tap + 1, :].astype(F32) * scratch[first : first + count, :]
-    return total / (1.0 + jnp.exp(-total))
+    return total * lax.logistic(total)
 
 
 def normalize(data):
@@ -253,10 +253,11 @@
         fetch.wait()
 
 
-def scan_kernel(count, where, *refs):
+def scan_kernel(slots, where, *refs):
+    count = len(slots)
     tables, outs, (states, table) = refs[:count], refs[count:-2], refs[-2:]
-    for slot in range(count):
-        table[slot] = tables[slot][...]
+    for slot, ref in zip(slots, tables):
+        table[slot] = ref[...]
     state = jnp.zeros((DK, DK), F32)
     for shard in range(count):
         slot = lax.bitwise_xor(where[0], shard)
@@ -419,11 +420,11 @@
         later_summary, later_decay,
     )
 
+    hops = sorted(range(1, ranks), key=lambda m: (-(m // 2).bit_count(), m))
+
     def exchange(blocks):
-        return [blocks[0]] + [
-            lax.ppermute(blocks[m], "seq", [(i, i ^ m) for i in range(ranks)])
-            for m in range(1, ranks)
-        ]
+        sent = [lax.ppermute(blocks[m], "seq", [(i, i ^ m) for i in range(ranks)]) for m in hops]
+        return [blocks[0]] + sent
 
     def outputs(half, later_solved, fetch):
         half_spec = spec((length, width // 2), lambda p: (0, half))
@@ -450,7 +451,7 @@
         arrived = exchange(send)
         arrived, direct_one, weight_one = lax.optimization_barrier((arrived, direct_one, weight_one))
         states = call(
-            functools.partial(scan_kernel, ranks),
+            functools.partial(scan_kernel, [0] + hops),
             (1,),
             [here] * ranks,
             [here] * (ranks // 2),

time: 67.5 us -> 66.4 us (0.984)
  waiting for transfers between devices: 19.8 us -> 19 us
    ppermute x7, waiting for transfers between devices: 2.16 us -> 1.36 us  [exchange(): lax.ppermute(blocks[m], 'seq', [(i, i ^ m) for i in range(ranks)])]
  transfers between devices with their start and end apart: 16 -> 16, of which waited for: 6 -> 8; matrix products, arithmetic and copies ran while one was open for 0% -> 0% of each run, Pallas kernels for 17% -> 17%
where the time goes in v4:
time: 66.4 us; the launch traced here: 66.1 us
  starting transfers between devices  24.4 us (37%)
  Pallas kernels  21.5 us (32%)
  waiting for transfers between devices  19 us (29%)
  other arithmetic  0.99 us (1%)
    pallas_call x9, Pallas kernels, call(): pl.pallas_call(kernel, grid_spec=pltpu.PrefetchScalarGridSpec(num_scalar_...  21.5 us
    ppermute x1, waiting for transfers between devices, shards(): joined = lax.ppermute(joined, 'head', [(0, 1), (3, 2), (1, 3), (2, 0)])  10.7 us
    ppermute x7, starting transfers between devices, exchange(): lax.ppermute(blocks[m], 'seq', [(i, i ^ m) for i in range(ranks)])  8.57 us
    ppermute x1, starting transfers between devices, shards(): skipped = lax.ppermute(inward, 'head', [(0, 2), (3, 1)])  5.74 us
    ppermute x1, waiting for transfers between devices, shards(): skipped = lax.ppermute(inward, 'head', [(0, 2), (3, 1)])  4.11 us
    ppermute x3, starting transfers between devices, shards(): lax.ppermute(states[d], 'seq', [(i, i ^ 2 * d) for i in range(ranks)])  3.55 us
    ppermute x1, starting transfers between devices, shards(): rims = lax.ppermute(rims, 'seq', [(i, i + 1) for i in range(ranks - 1)])  2.35 us
    ppermute x1, starting transfers between devices, shards(): joined = lax.ppermute(joined, 'head', [(0, 1), (3, 2), (1, 3), (2, 0)])  1.77 us
  transfers between devices with their start and end apart: 16, of which 8 were waited for; matrix products, arithmetic and copies ran while one was open for 0% of the time, Pallas kernels for 17%

profile of v4, /device:TPU:0, one launch (start us, length us, event | category | flops | bytes accessed | tf_op | source)
XLA Modules:
  0.0 66.1 jit_solution(5376566463998362844)
XLA Ops:
  0.0 0.8 %shard_map.91 = bf16[3,16,1024]{2,1,0:T(8,128)(2,1)S(1)} custom-call(bf16[256,1024]{1,0:T(8,128)(2,1)} %query.5, bf16[256,1024]{1,0:T(8,128)(2,1)} %key.5, bf16[256,1024]{1,0:T(8,128)(2,1)} %value.5), custom_call_target="tpu_custom_call" | custom-call | bytes 196608 | tf_op jit(solution)/shard_map/pallas_call | solution.py:340
  0.8 2.4 %collective-permute-start = (bf16[3,16,1024]{2,1,0:T(8,128)(2,1)S(1)}, bf16[3,16,1024]{2,1,0:T(8,128)(2,1)S(1)}, u32[]{:S(2)}, u32[]{:S(2)}) collective-permute-start(bf16[3,16,1024]{2,1,0:T(8,128)(2,1)S(1)} %shard_map.91), channel_id=1, source_target_pairs={{0,4},{4,8},{8,12},{12,16},{16,20},{20,24},{24,28},{1,5},{5,9},{9,... | collective-permute-start | bytes 294920 | tf_op jit(solution)/shard_map/ppermute | solution.py:381
  3.2 5.1 %shard_map.92 = (f32[8,256,128]{2,1,0:T(8,128)S(1)}, f32[8,8,128]{2,1,0:T(8,128)S(1)}, f32[8,128,256]{2,1,0:T(8,128)S(1)}, bf16[128,1024]{1,0:T(8,128)(2,1)S(1)}) custom-call(bf16[256,1024]{1,0:T(8,128)(2,1)} %key.5, bf16[256,1024]{1,0:T(8,128)(2,1)} %value.5, bf16[256,1024]{1,0:T(8,128)(2,1)} %gate.7, f32[8,256]{1,0:T(8,128)} %bitcast.3, ...), custom_call_target="tpu_custom_call" | custom-call | flops 800000000 | bytes 4194304 | tf_op jit(solution)/shard_map/pallas_call | solution.py:340
  8.2 0.0 collective-permute-done.rims
  8.3 5.4 %shard_map.93 = (bf16[8,256,128]{2,1,0:T(8,128)(2,1)S(1)}, f32[8,128,256]{2,1,0:T(8,128)S(1)}, bf16[128,1024]{1,0:T(8,128)(2,1)S(1)}, bf16[272,128]{1,0:T(8,128)...) custom-call(s32[1]{0:T(128)} %bitcast.where, ...), custom_call_target="tpu_custom_call" | custom-call | flops 800000000 | bytes 4194304 | tf_op jit(solution)/shard_map/pallas_call | solution.py:340
  13.6 3.5 %collective-permute-start.1 = (bf16[272,128]{1,0:T(8,128)(2,1)S(1)}, bf16[272,128]{1,0:T(8,128)(2,1)S(1)}, u32[]{:S(2)}, u32[]{:S(2)}) collective-permute-start(bf16[272,128]{1,0:T(8,128)(2,1)S(1)} %get-tuple-element.58), channel_id=1, source_target_pairs={{0,24},{4,28},{8,16},{12,20},{16,8},{20,12},{24,0},{28,4},{1,25},{... | collective-permute-start | bytes 208904 | tf_op jit(solution)/shard_map/ppermute | solution.py:426
  17.2 1.4 %collective-permute-start.2 = (bf16[272,128]{1,0:T(8,128)(2,1)S(1)}, bf16[272,128]{1,0:T(8,128)(2,1)S(1)}, u32[]{:S(2)}, u32[]{:S(2)}) collective-permute-start(bf16[272,128]{1,0:T(8,128)(2,1)S(1)} %get-tuple-element.59), channel_id=1, source_target_pairs={{0,28},{4,24},{8,20},{12,16},{16,12},{20,8},{24,4},{28,0},{1,29},{... | collective-permute-start | bytes 208904 | tf_op jit(solution)/shard_map/ppermute | solution.py:426
  18.6 1.5 %collective-permute-start.3 = (bf16[272,128]{1,0:T(8,128)(2,1)S(1)}, bf16[272,128]{1,0:T(8,128)(2,1)S(1)}, u32[]{:S(2)}, u32[]{:S(2)}) collective-permute-start(bf16[272,128]{1,0:T(8,128)(2,1)S(1)} %get-tuple-element.60), channel_id=1, source_target_pairs={{0,8},{4,12},{8,0},{12,4},{16,24},{20,28},{24,16},{28,20},{1,9},{5... | collective-permute-start | bytes 208904 | tf_op jit(solution)/shard_map/ppermute | solution.py:426
  20.1 0.0 collective-permute-start.4
  20.1 0.6 collective-permute-start.5
  20.6 0.0 collective-permute-done.1.refs_1_
  20.6 1.4 %collective-permute-start.6 = (bf16[272,128]{1,0:T(8,128)(2,1)S(1)}, bf16[272,128]{1,0:T(8,128)(2,1)S(1)}, u32[]{:S(2)}, u32[]{:S(2)}) collective-permute-start(bf16[272,128]{1,0:T(8,128)(2,1)S(1)} %get-tuple-element.63), channel_id=1, source_target_pairs={{0,20},{4,16},{8,28},{12,24},{16,4},{20,0},{24,12},{28,8},{1,21},{... | collective-permute-start | bytes 208904 | tf_op jit(solution)/shard_map/ppermute | solution.py:426
  22.1 0.0 collective-permute-done.2.refs_2_
  22.1 0.2 collective-permute-start.7
  22.2 2.3 %shard_map.94 = (f32[256,512]{1,0:T(8,128)S(1)}, bf16[256,512]{1,0:T(8,128)(2,1)S(1)}) custom-call(bf16[256,1024]{1,0:T(8,128)(2,1)} %query.5, bf16[256,1024]{1,0:T(8,128)(2,1)} %gate.7, bf16[3,16,1024]{2,1,0:T(8,128)(2,1)S(1)} %collective-permute-done.rims, bf16[4,1024]{1,0:T(4,128)(2,1)} %query_taps.3, f32[8,128,256]{2,1,0:T(8,128)S(1)} %get-tuple-element.65.first_solved, ...), custom_call_target="tpu_custom_call" | custom-call | flops 400000000 | bytes 2097152 | tf_op jit(solution)/shard_map/pallas_call | solution.py:340
  24.5 0.0 collective-permute-done.3.refs_3_
  24.5 0.1 collective-permute-done.4.refs_4_
  24.6 0.5 collective-permute-done.5.refs_5_
  25.1 0.8 %collective-permute-done.6.refs_6_ = bf16[272,128]{1,0:T(8,128)(2,1)S(1)} collective-permute-done((bf16[272,128]{1,0:T(8,128)(2,1)S(1)}, bf16[272,128]{1,0:T(8,128)(2,1)S(1)}, u32[]{:S(2)}, u32[]{:S(2)}) %collective-permute-start.6) | collective-permute-done | bytes 69664 | tf_op jit(solution)/shard_map/ppermute | solution.py:426
  25.9 0.0 collective-permute-done.7.refs_7_
  25.9 0.9 %shard_map.95 = (bf16[2,128,128]{2,1,0:T(8,128)(2,1)S(1)}, bf16[2,128,128]{2,1,0:T(8,128)(2,1)S(1)}, bf16[2,128,128]{2,1,0:T(8,128)(2,1)S(1)}, bf16[2,128,128]{2,1,0:T(8,128)(2,1)S(1)}) custom-call(s32[1]{0:T(128)} %bitcast.where, bf16[272,128]{1,0:T(8,128)(2,1)S(1)} %get-tuple-element.73.refs_0_, bf16[272,128]{1,0:T(8,128)(2,1)S(1)} %collective-permute-done.1.refs_1_, ...), custom_call_target="tpu_custom_call" | custom-call | flops 32000000 | bytes 1048576 | tf_op jit(solution)/shard_map/pallas_call | solution.py:340
  26.8 1.2 %collective-permute-start.10 = (bf16[2,128,128]{2,1,0:T(8,128)(2,1)S(1)}, bf16[2,128,128]{2,1,0:T(8,128)(2,1)S(1)}, u32[]{:S(2)}, u32[]{:S(2)}) collective-permute-start(bf16[2,128,128]{2,1,0:T(8,128)(2,1)S(1)} %get-tuple-element.88), channel_id=1, source_target_pairs={{0,24},{4,28},{8,16},{12,20},{16,8},{20,12},{24,0},{28,4},{1,25},{... | collective-permute-start | bytes 196616 | tf_op jit(solution)/shard_map/ppermute | solution.py:468
  28.0 1.9 %collective-permute-start.8 = (bf16[2,128,128]{2,1,0:T(8,128)(2,1)S(1)}, bf16[2,128,128]{2,1,0:T(8,128)(2,1)S(1)}, u32[]{:S(2)}, u32[]{:S(2)}) collective-permute-start(bf16[2,128,128]{2,1,0:T(8,128)(2,1)S(1)} %get-tuple-element.86), channel_id=1, source_target_pairs={{0,8},{4,12},{8,0},{12,4},{16,24},{20,28},{24,16},{28,20},{1,9},{5... | collective-permute-start | bytes 196616 | tf_op jit(solution)/shard_map/ppermute | solution.py:468
  29.9 0.5 collective-permute-start.9
  30.4 2.3 %shard_map.96 = (f32[256,512]{1,0:T(8,128)S(1)}, bf16[256,512]{1,0:T(8,128)(2,1)S(1)}) custom-call(bf16[256,1024]{1,0:T(8,128)(2,1)} %query.5, bf16[256,1024]{1,0:T(8,128)(2,1)} %gate.7, bf16[3,16,1024]{2,1,0:T(8,128)(2,1)S(1)} %collective-permute-done.rims, bf16[4,1024]{1,0:T(4,128)(2,1)} %query_taps.3, f32[8,128,256]{2,1,0:T(8,128)S(1)} %get-tuple-element.65.first_solved, ...), custom_call_target="tpu_custom_call" | custom-call | flops 400000000 | bytes 2097152 | tf_op jit(solution)/shard_map/pallas_call | solution.py:340
  32.6 0.0 collective-permute-done.10.refs_3_.rest_3_
  32.7 0.3 collective-permute-done.8.refs_1_.rest_1_
  33.0 1.1 %collective-permute-done.9.refs_2_.rest_2_ = bf16[2,128,128]{2,1,0:T(8,128)(2,1)S(1)} collective-permute-done((bf16[2,128,128]{2,1,0:T(8,128)(2,1)S(1)}, bf16[2,128,128]{2,1,0:T(8,128)(2,1)S(1)}, u32[]{:S(2)}, u32[]{:S(2)}) %collective-permute-start.9) | collective-permute-done | bytes 65568 | tf_op jit(solution)/shard_map/ppermute | solution.py:468
  34.1 0.1 collective-permute-start.11
  34.2 1.7 %shard_map.98.early = bf16[1024,1152]{1,0:T(8,128)(2,1)S(1)} custom-call(bf16[1024,2304]{1,0:T(8,128)(2,1)} %matrix.4), custom_call_target="tpu_custom_call" | custom-call | bytes 4718592 | tf_op jit(solution)/shard_map/pallas_call | solution.py:340
  35.9 0.0 collective-permute-done.11.rest_4_
  35.9 3.1 %shard_map.99 = (f32[64,2304]{1,0:T(8,128)S(1)}, bf16[64,2304]{1,0:T(8,128)(2,1)S(1)}, bf16[64,2304]{1,0:T(8,128)(2,1)S(1)}, bf16[64,2304]{1,0:T(8,128)(2,1)S(1)}) custom-call(s32[1]{0:T(128)} %bitcast.where, s32[1]{0:T(128)} %bitcast.1.mine, f32[256,512]{1,0:T(8,128)S(1)} %get-tuple-element.72.direct_one, f32[256,512]{1,0:T(8,128)S(1)} %get-tuple-element.92.direct_two, ...), custom_call_target="tpu_custom_call" | custom-call | flops 1207959552 | bytes 4718592 | tf_op jit(solution)/shard_map/pallas_call | solution.py:340
  39.0 1.6 %collective-permute-start.12 = (bf16[64,2304]{1,0:T(8,128)(2,1)S(1)}, bf16[64,2304]{1,0:T(8,128)(2,1)S(1)}, u32[]{:S(2)}, u32[]{:S(2)}) collective-permute-start(bf16[64,2304]{1,0:T(8,128)(2,1)S(1)} %get-tuple-element.102), channel_id=1, source_target_pairs={{0,1},{1,0},{2,3},{3,2},{4,5},{5,4},{6,7},{7,6},{8,9},{9,8},{10,11... | collective-permute-start | bytes 884744 | tf_op jit(solution)/shard_map/ppermute | solution.py:531
  40.7 0.7 %collective-permute-start.13 = (bf16[64,2304]{1,0:T(8,128)(2,1)S(1)}, bf16[64,2304]{1,0:T(8,128)(2,1)S(1)}, u32[]{:S(2)}, u32[]{:S(2)}) collective-permute-start(bf16[64,2304]{1,0:T(8,128)(2,1)S(1)} %get-tuple-element.103), channel_id=1, source_target_pairs={{1,2},{2,1},{5,6},{6,5},{9,10},{10,9},{13,14},{14,13},{17,18},{18,... | collective-permute-start | bytes 884744 | tf_op jit(solution)/shard_map/ppermute | solution.py:532
  41.4 5.7 %collective-permute-start.14 = (bf16[64,2304]{1,0:T(8,128)(2,1)S(1)}, bf16[64,2304]{1,0:T(8,128)(2,1)S(1)}, u32[]{:S(2)}, u32[]{:S(2)}) collective-permute-start(bf16[64,2304]{1,0:T(8,128)(2,1)S(1)} %get-tuple-element.103), channel_id=1, source_target_pairs={{0,2},{3,1},{4,6},{7,5},{8,10},{11,9},{12,14},{15,13},{16,18},{19,... | collective-permute-start | bytes 884744 | tf_op jit(solution)/shard_map/ppermute | solution.py:533
  47.1 1.4 %collective-permute-done.12 = bf16[64,2304]{1,0:T(8,128)(2,1)S(1)} collective-permute-done((bf16[64,2304]{1,0:T(8,128)(2,1)S(1)}, bf16[64,2304]{1,0:T(8,128)(2,1)S(1)}, u32[]{:S(2)}, u32[]{:S(2)}) %collective-permute-start.12) | collective-permute-done | bytes 294944 | tf_op jit(solution)/shard_map/ppermute | solution.py:531
  48.5 0.1 fusion.6
  48.6 1.8 %collective-permute-start.15 = (bf16[64,2304]{1,0:T(8,128)(2,1)S(1)}, bf16[64,2304]{1,0:T(8,128)(2,1)S(1)}, u32[]{:S(2)}, u32[]{:S(2)}) collective-permute-start(bf16[64,2304]{1,0:T(8,128)(2,1)S(1)} %fusion.6), channel_id=1, source_target_pairs={{0,1},{3,2},{1,3},{2,0},{4,5},{7,6},{5,7},{6,4},{8,9},{11,10},{9,1... | collective-permute-start | bytes 884744 | tf_op jit(solution)/shard_map/ppermute | solution.py:535
  50.4 0.0 collective-permute-done.13
  50.4 4.1 %collective-permute-done.14 = bf16[64,2304]{1,0:T(8,128)(2,1)S(1)} collective-permute-done((bf16[64,2304]{1,0:T(8,128)(2,1)S(1)}, bf16[64,2304]{1,0:T(8,128)(2,1)S(1)}, u32[]{:S(2)}, u32[]{:S(2)}) %collective-permute-start.14) | collective-permute-done | bytes 294944 | tf_op jit(solution)/shard_map/ppermute | solution.py:533
  54.5 10.7 %collective-permute-done.15 = bf16[64,2304]{1,0:T(8,128)(2,1)S(1)} collective-permute-done((bf16[64,2304]{1,0:T(8,128)(2,1)S(1)}, bf16[64,2304]{1,0:T(8,128)(2,1)S(1)}, u32[]{:S(2)}, u32[]{:S(2)}) %collective-permute-start.15) | collective-permute-done | bytes 294944 | tf_op jit(solution)/shard_map/ppermute | solution.py:535
  65.2 0.9 %fusion.4 = bf16[64,2304]{1,0:T(8,128)(2,1)} fusion(f32[64,2304]{1,0:T(8,128)S(1)} %get-tuple-element.101, bf16[64,2304]{1,0:T(8,128)(2,1)S(1)} %collective-permute-done.12, bf16[64,2304]{1,0:T(8,128)(2,1)S(1)} %collective-permute-done.15, bf16[64,2304]{1,0:T(8,128)(2,1)S(1)} %collective-permute-done.14, bf16[64,2304]{1,0:T(8,128)(2,1)S(1)} %collective-permute-done.13, ...), kind=kLoop, calls=%fused_computation.6 | loop fusion | flops 1474560 | bytes 2064385 | tf_op jit(solution)/shard_map/convert_element_type | solution.py:545
  (1 shorter events, 0.0 us)
Async XLA Ops:
  0.8 7.4 %collective-permute-start = (bf16[3,16,1024]{2,1,0:T(8,128)(2,1)S(1)}, bf16[3,16,1024]{2,1,0:T(8,128)(2,1)S(1)}, u32[]{:S(2)}, u32[]{:S(2)}) collective-permute-start(bf16[3,16,1024]{2,1,0:T(8,128)(2,1)S(1)} %shard_map.91), channel_id=1, source_target_pairs={{0,4},{4,8},{8,12},{12,16},{16,20},{20,24},{24,28},{1,5},{5,9},{9,... | collective-permute-start | bytes 294920 | tf_op jit(solution)/shard_map/ppermute | solution.py:381
  13.6 7.0 %collective-permute-start.1 = (bf16[272,128]{1,0:T(8,128)(2,1)S(1)}, bf16[272,128]{1,0:T(8,128)(2,1)S(1)}, u32[]{:S(2)}, u32[]{:S(2)}) collective-permute-start(bf16[272,128]{1,0:T(8,128)(2,1)S(1)} %get-tuple-element.58), channel_id=1, source_target_pairs={{0,24},{4,28},{8,16},{12,20},{16,8},{20,12},{24,0},{28,4},{1,25},{... | collective-permute-start | bytes 208904 | tf_op jit(solution)/shard_map/ppermute | solution.py:426
  17.2 4.9 %collective-permute-start.2 = (bf16[272,128]{1,0:T(8,128)(2,1)S(1)}, bf16[272,128]{1,0:T(8,128)(2,1)S(1)}, u32[]{:S(2)}, u32[]{:S(2)}) collective-permute-start(bf16[272,128]{1,0:T(8,128)(2,1)S(1)} %get-tuple-element.59), channel_id=1, source_target_pairs={{0,28},{4,24},{8,20},{12,16},{16,12},{20,8},{24,4},{28,0},{1,29},{... | collective-permute-start | bytes 208904 | tf_op jit(solution)/shard_map/ppermute | solution.py:426
  18.6 6.0 %collective-permute-start.3 = (bf16[272,128]{1,0:T(8,128)(2,1)S(1)}, bf16[272,128]{1,0:T(8,128)(2,1)S(1)}, u32[]{:S(2)}, u32[]{:S(2)}) collective-permute-start(bf16[272,128]{1,0:T(8,128)(2,1)S(1)} %get-tuple-element.60), channel_id=1, source_target_pairs={{0,8},{4,12},{8,0},{12,4},{16,24},{20,28},{24,16},{28,20},{1,9},{5... | collective-permute-start | bytes 208904 | tf_op jit(solution)/shard_map/ppermute | solution.py:426
  20.1 4.5 %collective-permute-start.4 = (bf16[272,128]{1,0:T(8,128)(2,1)S(1)}, bf16[272,128]{1,0:T(8,128)(2,1)S(1)}, u32[]{:S(2)}, u32[]{:S(2)}) collective-permute-start(bf16[272,128]{1,0:T(8,128)(2,1)S(1)} %get-tuple-element.61), channel_id=1, source_target_pairs={{0,12},{4,8},{8,4},{12,0},{16,28},{20,24},{24,20},{28,16},{1,13},{... | collective-permute-start | bytes 208904 | tf_op jit(solution)/shard_map/ppermute | solution.py:426
  20.1 5.1 %collective-permute-start.5 = (bf16[272,128]{1,0:T(8,128)(2,1)S(1)}, bf16[272,128]{1,0:T(8,128)(2,1)S(1)}, u32[]{:S(2)}, u32[]{:S(2)}) collective-permute-start(bf16[272,128]{1,0:T(8,128)(2,1)S(1)} %get-tuple-element.62), channel_id=1, source_target_pairs={{0,16},{4,20},{8,24},{12,28},{16,0},{20,4},{24,8},{28,12},{1,17},{... | collective-permute-start | bytes 208904 | tf_op jit(solution)/shard_map/ppermute | solution.py:426
  20.6 5.2 %collective-permute-start.6 = (bf16[272,128]{1,0:T(8,128)(2,1)S(1)}, bf16[272,128]{1,0:T(8,128)(2,1)S(1)}, u32[]{:S(2)}, u32[]{:S(2)}) collective-permute-start(bf16[272,128]{1,0:T(8,128)(2,1)S(1)} %get-tuple-element.63), channel_id=1, source_target_pairs={{0,20},{4,16},{8,28},{12,24},{16,4},{20,0},{24,12},{28,8},{1,21},{... | collective-permute-start | bytes 208904 | tf_op jit(solution)/shard_map/ppermute | solution.py:426
  22.1 3.8 %collective-permute-start.7 = (bf16[272,128]{1,0:T(8,128)(2,1)S(1)}, bf16[272,128]{1,0:T(8,128)(2,1)S(1)}, u32[]{:S(2)}, u32[]{:S(2)}) collective-permute-start(bf16[272,128]{1,0:T(8,128)(2,1)S(1)} %get-tuple-element.64), channel_id=1, source_target_pairs={{0,4},{4,0},{8,12},{12,8},{16,20},{20,16},{24,28},{28,24},{1,5},{5... | collective-permute-start | bytes 208904 | tf_op jit(solution)/shard_map/ppermute | solution.py:426
  26.8 5.9 %collective-permute-start.10 = (bf16[2,128,128]{2,1,0:T(8,128)(2,1)S(1)}, bf16[2,128,128]{2,1,0:T(8,128)(2,1)S(1)}, u32[]{:S(2)}, u32[]{:S(2)}) collective-permute-start(bf16[2,128,128]{2,1,0:T(8,128)(2,1)S(1)} %get-tuple-element.88), channel_id=1, source_target_pairs={{0,24},{4,28},{8,16},{12,20},{16,8},{20,12},{24,0},{28,4},{1,25},{... | collective-permute-start | bytes 196616 | tf_op jit(solution)/shard_map/ppermute | solution.py:468
  28.0 5.1 %collective-permute-start.8 = (bf16[2,128,128]{2,1,0:T(8,128)(2,1)S(1)}, bf16[2,128,128]{2,1,0:T(8,128)(2,1)S(1)}, u32[]{:S(2)}, u32[]{:S(2)}) collective-permute-start(bf16[2,128,128]{2,1,0:T(8,128)(2,1)S(1)} %get-tuple-element.86), channel_id=1, source_target_pairs={{0,8},{4,12},{8,0},{12,4},{16,24},{20,28},{24,16},{28,20},{1,9},{5... | collective-permute-start | bytes 196616 | tf_op jit(solution)/shard_map/ppermute | solution.py:468
  29.9 4.3 %collective-permute-start.9 = (bf16[2,128,128]{2,1,0:T(8,128)(2,1)S(1)}, bf16[2,128,128]{2,1,0:T(8,128)(2,1)S(1)}, u32[]{:S(2)}, u32[]{:S(2)}) collective-permute-start(bf16[2,128,128]{2,1,0:T(8,128)(2,1)S(1)} %get-tuple-element.87), channel_id=1, source_target_pairs={{0,16},{4,20},{8,24},{12,28},{16,0},{20,4},{24,8},{28,12},{1,17},{... | collective-permute-start | bytes 196616 | tf_op jit(solution)/shard_map/ppermute | solution.py:468
  34.1 1.8 %collective-permute-start.11 = (bf16[4,128,128]{2,1,0:T(8,128)(2,1)S(1)}, bf16[4,128,128]{2,1,0:T(8,128)(2,1)S(1)}, u32[]{:S(2)}, u32[]{:S(2)}) collective-permute-start(bf16[4,128,128]{2,1,0:T(8,128)(2,1)S(1)} %shard_map.97), channel_id=1, source_target_pairs={{0,4},{4,0},{8,12},{12,8},{16,20},{20,16},{24,28},{28,24},{1,5},{5... | collective-permute-start | bytes 393224 | tf_op jit(solution)/shard_map/ppermute | solution.py:477
  39.0 9.5 %collective-permute-start.12 = (bf16[64,2304]{1,0:T(8,128)(2,1)S(1)}, bf16[64,2304]{1,0:T(8,128)(2,1)S(1)}, u32[]{:S(2)}, u32[]{:S(2)}) collective-permute-start(bf16[64,2304]{1,0:T(8,128)(2,1)S(1)} %get-tuple-element.102), channel_id=1, source_target_pairs={{0,1},{1,0},{2,3},{3,2},{4,5},{5,4},{6,7},{7,6},{8,9},{9,8},{10,11... | collective-permute-start | bytes 884744 | tf_op jit(solution)/shard_map/ppermute | solution.py:531
  40.7 9.7 %collective-permute-start.13 = (bf16[64,2304]{1,0:T(8,128)(2,1)S(1)}, bf16[64,2304]{1,0:T(8,128)(2,1)S(1)}, u32[]{:S(2)}, u32[]{:S(2)}) collective-permute-start(bf16[64,2304]{1,0:T(8,128)(2,1)S(1)} %get-tuple-element.103), channel_id=1, source_target_pairs={{1,2},{2,1},{5,6},{6,5},{9,10},{10,9},{13,14},{14,13},{17,18},{18,... | collective-permute-start | bytes 884744 | tf_op jit(solution)/shard_map/ppermute | solution.py:532
  41.4 13.1 %collective-permute-start.14 = (bf16[64,2304]{1,0:T(8,128)(2,1)S(1)}, bf16[64,2304]{1,0:T(8,128)(2,1)S(1)}, u32[]{:S(2)}, u32[]{:S(2)}) collective-permute-start(bf16[64,2304]{1,0:T(8,128)(2,1)S(1)} %get-tuple-element.103), channel_id=1, source_target_pairs={{0,2},{3,1},{4,6},{7,5},{8,10},{11,9},{12,14},{15,13},{16,18},{19,... | collective-permute-start | bytes 884744 | tf_op jit(solution)/shard_map/ppermute | solution.py:533
  48.6 16.6 %collective-permute-start.15 = (bf16[64,2304]{1,0:T(8,128)(2,1)S(1)}, bf16[64,2304]{1,0:T(8,128)(2,1)S(1)}, u32[]{:S(2)}, u32[]{:S(2)}) collective-permute-start(bf16[64,2304]{1,0:T(8,128)(2,1)S(1)} %fusion.6), channel_id=1, source_target_pairs={{0,1},{3,2},{1,3},{2,0},{4,5},{7,6},{5,7},{6,4},{8,9},{11,10},{9,1... | collective-permute-start | bytes 884744 | tf_op jit(solution)/shard_map/ppermute | solution.py:535

commit v5 on v4

--- a/solution.py
+++ b/solution.py
@@ -503,7 +503,7 @@
         )
     else:
         owners = [lambda z, d=d: lax.rem(z + d, parts) for d in range(parts)]
-    half = model // 2
+    half = 2 * (model // 3)
     early = call(
         fetch_kernel, (1,), [anywhere], here, kept((width, half), BF16),
         [pltpu.SemaphoreType.DMA], (0, width * model * 2), LIMIT, 0, source,

time: 66.4 us -> 66.2 us (level)
  transfers between devices with their start and end apart: 16 -> 16, of which waited for: 8 -> 8; matrix products, arithmetic and copies ran while one was open for 0% -> 0% of each run, Pallas kernels for 17% -> 18%
where the time goes in v5:
time: 66.2 us; the launch traced here: 65.8 us
  starting transfers between devices  24.4 us (37%)
  Pallas kernels  21.2 us (32%)
  waiting for transfers between devices  19 us (29%)
  other arithmetic  0.99 us (1%)
    pallas_call x9, Pallas kernels, call(): pl.pallas_call(kernel, grid_spec=pltpu.PrefetchScalarGridSpec(num_scalar_...  21.2 us
    ppermute x1, waiting for transfers between devices, shards(): joined = lax.ppermute(joined, 'head', [(0, 1), (3, 2), (1, 3), (2, 0)])  10.7 us
    ppermute x7, starting transfers between devices, exchange(): lax.ppermute(blocks[m], 'seq', [(i, i ^ m) for i in range(ranks)])  8.57 us
    ppermute x1, starting transfers between devices, shards(): skipped = lax.ppermute(inward, 'head', [(0, 2), (3, 1)])  5.75 us
    ppermute x1, waiting for transfers between devices, shards(): skipped = lax.ppermute(inward, 'head', [(0, 2), (3, 1)])  4.1 us
    ppermute x3, starting transfers between devices, shards(): lax.ppermute(states[d], 'seq', [(i, i ^ 2 * d) for i in range(ranks)])  3.55 us
    ppermute x1, starting transfers between devices, shards(): rims = lax.ppermute(rims, 'seq', [(i, i + 1) for i in range(ranks - 1)])  2.35 us
    ppermute x1, starting transfers between devices, shards(): joined = lax.ppermute(joined, 'head', [(0, 1), (3, 2), (1, 3), (2, 0)])  1.77 us
  transfers between devices with their start and end apart: 16, of which 8 were waited for; matrix products, arithmetic and copies ran while one was open for 0% of the time, Pallas kernels for 18%

profile of v5, /device:TPU:0, one launch (start us, length us, event | category | flops | bytes accessed | tf_op | source)
XLA Modules:
  0.0 65.8 jit_solution(16850670631235677864)
XLA Ops:
  0.0 0.8 %shard_map.91 = bf16[3,16,1024]{2,1,0:T(8,128)(2,1)S(1)} custom-call(bf16[256,1024]{1,0:T(8,128)(2,1)} %query.5, bf16[256,1024]{1,0:T(8,128)(2,1)} %key.5, bf16[256,1024]{1,0:T(8,128)(2,1)} %value.5), custom_call_target="tpu_custom_call" | custom-call | bytes 196608 | tf_op jit(solution)/shard_map/pallas_call | solution.py:340
  0.8 2.4 %collective-permute-start = (bf16[3,16,1024]{2,1,0:T(8,128)(2,1)S(1)}, bf16[3,16,1024]{2,1,0:T(8,128)(2,1)S(1)}, u32[]{:S(2)}, u32[]{:S(2)}) collective-permute-start(bf16[3,16,1024]{2,1,0:T(8,128)(2,1)S(1)} %shard_map.91), channel_id=1, source_target_pairs={{0,4},{4,8},{8,12},{12,16},{16,20},{20,24},{24,28},{1,5},{5,9},{9,... | collective-permute-start | bytes 294920 | tf_op jit(solution)/shard_map/ppermute | solution.py:381
  3.2 5.1 %shard_map.92 = (f32[8,256,128]{2,1,0:T(8,128)S(1)}, f32[8,8,128]{2,1,0:T(8,128)S(1)}, f32[8,128,256]{2,1,0:T(8,128)S(1)}, bf16[128,1024]{1,0:T(8,128)(2,1)S(1)}) custom-call(bf16[256,1024]{1,0:T(8,128)(2,1)} %key.5, bf16[256,1024]{1,0:T(8,128)(2,1)} %value.5, bf16[256,1024]{1,0:T(8,128)(2,1)} %gate.7, f32[8,256]{1,0:T(8,128)} %bitcast.3, ...), custom_call_target="tpu_custom_call" | custom-call | flops 800000000 | bytes 4194304 | tf_op jit(solution)/shard_map/pallas_call | solution.py:340
  8.2 0.0 collective-permute-done.rims
  8.3 5.4 %shard_map.93 = (bf16[8,256,128]{2,1,0:T(8,128)(2,1)S(1)}, f32[8,128,256]{2,1,0:T(8,128)S(1)}, bf16[128,1024]{1,0:T(8,128)(2,1)S(1)}, bf16[272,128]{1,0:T(8,128)...) custom-call(s32[1]{0:T(128)} %bitcast.where, ...), custom_call_target="tpu_custom_call" | custom-call | flops 800000000 | bytes 4194304 | tf_op jit(solution)/shard_map/pallas_call | solution.py:340
  13.6 3.5 %collective-permute-start.1 = (bf16[272,128]{1,0:T(8,128)(2,1)S(1)}, bf16[272,128]{1,0:T(8,128)(2,1)S(1)}, u32[]{:S(2)}, u32[]{:S(2)}) collective-permute-start(bf16[272,128]{1,0:T(8,128)(2,1)S(1)} %get-tuple-element.58), channel_id=1, source_target_pairs={{0,24},{4,28},{8,16},{12,20},{16,8},{20,12},{24,0},{28,4},{1,25},{... | collective-permute-start | bytes 208904 | tf_op jit(solution)/shard_map/ppermute | solution.py:426
  17.2 1.4 %collective-permute-start.2 = (bf16[272,128]{1,0:T(8,128)(2,1)S(1)}, bf16[272,128]{1,0:T(8,128)(2,1)S(1)}, u32[]{:S(2)}, u32[]{:S(2)}) collective-permute-start(bf16[272,128]{1,0:T(8,128)(2,1)S(1)} %get-tuple-element.59), channel_id=1, source_target_pairs={{0,28},{4,24},{8,20},{12,16},{16,12},{20,8},{24,4},{28,0},{1,29},{... | collective-permute-start | bytes 208904 | tf_op jit(solution)/shard_map/ppermute | solution.py:426
  18.6 1.5 %collective-permute-start.3 = (bf16[272,128]{1,0:T(8,128)(2,1)S(1)}, bf16[272,128]{1,0:T(8,128)(2,1)S(1)}, u32[]{:S(2)}, u32[]{:S(2)}) collective-permute-start(bf16[272,128]{1,0:T(8,128)(2,1)S(1)} %get-tuple-element.60), channel_id=1, source_target_pairs={{0,8},{4,12},{8,0},{12,4},{16,24},{20,28},{24,16},{28,20},{1,9},{5... | collective-permute-start | bytes 208904 | tf_op jit(solution)/shard_map/ppermute | solution.py:426
  20.1 0.0 collective-permute-start.4
  20.1 0.6 collective-permute-start.5
  20.6 0.0 collective-permute-done.1.refs_1_
  20.6 1.4 %collective-permute-start.6 = (bf16[272,128]{1,0:T(8,128)(2,1)S(1)}, bf16[272,128]{1,0:T(8,128)(2,1)S(1)}, u32[]{:S(2)}, u32[]{:S(2)}) collective-permute-start(bf16[272,128]{1,0:T(8,128)(2,1)S(1)} %get-tuple-element.63), channel_id=1, source_target_pairs={{0,20},{4,16},{8,28},{12,24},{16,4},{20,0},{24,12},{28,8},{1,21},{... | collective-permute-start | bytes 208904 | tf_op jit(solution)/shard_map/ppermute | solution.py:426
  22.1 0.0 collective-permute-done.2.refs_2_
  22.1 0.2 collective-permute-start.7
  22.2 2.3 %shard_map.94 = (f32[256,512]{1,0:T(8,128)S(1)}, bf16[256,512]{1,0:T(8,128)(2,1)S(1)}) custom-call(bf16[256,1024]{1,0:T(8,128)(2,1)} %query.5, bf16[256,1024]{1,0:T(8,128)(2,1)} %gate.7, bf16[3,16,1024]{2,1,0:T(8,128)(2,1)S(1)} %collective-permute-done.rims, bf16[4,1024]{1,0:T(4,128)(2,1)} %query_taps.3, f32[8,128,256]{2,1,0:T(8,128)S(1)} %get-tuple-element.65.first_solved, ...), custom_call_target="tpu_custom_call" | custom-call | flops 400000000 | bytes 2097152 | tf_op jit(solution)/shard_map/pallas_call | solution.py:340
  24.5 0.0 collective-permute-done.3.refs_3_
  24.5 0.1 collective-permute-done.4.refs_4_
  24.6 0.5 collective-permute-done.5.refs_5_
  25.1 0.8 %collective-permute-done.6.refs_6_ = bf16[272,128]{1,0:T(8,128)(2,1)S(1)} collective-permute-done((bf16[272,128]{1,0:T(8,128)(2,1)S(1)}, bf16[272,128]{1,0:T(8,128)(2,1)S(1)}, u32[]{:S(2)}, u32[]{:S(2)}) %collective-permute-start.6) | collective-permute-done | bytes 69664 | tf_op jit(solution)/shard_map/ppermute | solution.py:426
  25.9 0.0 collective-permute-done.7.refs_7_
  25.9 0.9 %shard_map.95 = (bf16[2,128,128]{2,1,0:T(8,128)(2,1)S(1)}, bf16[2,128,128]{2,1,0:T(8,128)(2,1)S(1)}, bf16[2,128,128]{2,1,0:T(8,128)(2,1)S(1)}, bf16[2,128,128]{2,1,0:T(8,128)(2,1)S(1)}) custom-call(s32[1]{0:T(128)} %bitcast.where, bf16[272,128]{1,0:T(8,128)(2,1)S(1)} %get-tuple-element.73.refs_0_, bf16[272,128]{1,0:T(8,128)(2,1)S(1)} %collective-permute-done.1.refs_1_, ...), custom_call_target="tpu_custom_call" | custom-call | flops 32000000 | bytes 1048576 | tf_op jit(solution)/shard_map/pallas_call | solution.py:340
  26.8 1.2 %collective-permute-start.10 = (bf16[2,128,128]{2,1,0:T(8,128)(2,1)S(1)}, bf16[2,128,128]{2,1,0:T(8,128)(2,1)S(1)}, u32[]{:S(2)}, u32[]{:S(2)}) collective-permute-start(bf16[2,128,128]{2,1,0:T(8,128)(2,1)S(1)} %get-tuple-element.88), channel_id=1, source_target_pairs={{0,24},{4,28},{8,16},{12,20},{16,8},{20,12},{24,0},{28,4},{1,25},{... | collective-permute-start | bytes 196616 | tf_op jit(solution)/shard_map/ppermute | solution.py:468
  28.0 1.9 %collective-permute-start.8 = (bf16[2,128,128]{2,1,0:T(8,128)(2,1)S(1)}, bf16[2,128,128]{2,1,0:T(8,128)(2,1)S(1)}, u32[]{:S(2)}, u32[]{:S(2)}) collective-permute-start(bf16[2,128,128]{2,1,0:T(8,128)(2,1)S(1)} %get-tuple-element.86), channel_id=1, source_target_pairs={{0,8},{4,12},{8,0},{12,4},{16,24},{20,28},{24,16},{28,20},{1,9},{5... | collective-permute-start | bytes 196616 | tf_op jit(solution)/shard_map/ppermute | solution.py:468
  29.9 0.5 collective-permute-start.9
  30.4 2.3 %shard_map.96 = (f32[256,512]{1,0:T(8,128)S(1)}, bf16[256,512]{1,0:T(8,128)(2,1)S(1)}) custom-call(bf16[256,1024]{1,0:T(8,128)(2,1)} %query.5, bf16[256,1024]{1,0:T(8,128)(2,1)} %gate.7, bf16[3,16,1024]{2,1,0:T(8,128)(2,1)S(1)} %collective-permute-done.rims, bf16[4,1024]{1,0:T(4,128)(2,1)} %query_taps.3, f32[8,128,256]{2,1,0:T(8,128)S(1)} %get-tuple-element.65.first_solved, ...), custom_call_target="tpu_custom_call" | custom-call | flops 400000000 | bytes 2097152 | tf_op jit(solution)/shard_map/pallas_call | solution.py:340
  32.6 0.0 collective-permute-done.10.refs_3_.rest_3_
  32.7 0.3 collective-permute-done.8.refs_1_.rest_1_
  33.0 1.1 %collective-permute-done.9.refs_2_.rest_2_ = bf16[2,128,128]{2,1,0:T(8,128)(2,1)S(1)} collective-permute-done((bf16[2,128,128]{2,1,0:T(8,128)(2,1)S(1)}, bf16[2,128,128]{2,1,0:T(8,128)(2,1)S(1)}, u32[]{:S(2)}, u32[]{:S(2)}) %collective-permute-start.9) | collective-permute-done | bytes 65568 | tf_op jit(solution)/shard_map/ppermute | solution.py:468
  34.1 0.1 collective-permute-start.11
  34.2 1.9 %shard_map.98.early = bf16[1024,1536]{1,0:T(8,128)(2,1)S(1)} custom-call(bf16[1024,2304]{1,0:T(8,128)(2,1)} %matrix.4), custom_call_target="tpu_custom_call" | custom-call | bytes 4718592 | tf_op jit(solution)/shard_map/pallas_call | solution.py:340
  36.1 0.0 collective-permute-done.11.rest_4_
  36.1 2.6 %shard_map.99 = (f32[64,2304]{1,0:T(8,128)S(1)}, bf16[64,2304]{1,0:T(8,128)(2,1)S(1)}, bf16[64,2304]{1,0:T(8,128)(2,1)S(1)}, bf16[64,2304]{1,0:T(8,128)(2,1)S(1)}) custom-call(s32[1]{0:T(128)} %bitcast.where, s32[1]{0:T(128)} %bitcast.1.mine, f32[256,512]{1,0:T(8,128)S(1)} %get-tuple-element.72.direct_one, f32[256,512]{1,0:T(8,128)S(1)} %get-tuple-element.92.direct_two, ...), custom_call_target="tpu_custom_call" | custom-call | flops 1207959552 | bytes 4718592 | tf_op jit(solution)/shard_map/pallas_call | solution.py:340
  38.7 1.6 %collective-permute-start.12 = (bf16[64,2304]{1,0:T(8,128)(2,1)S(1)}, bf16[64,2304]{1,0:T(8,128)(2,1)S(1)}, u32[]{:S(2)}, u32[]{:S(2)}) collective-permute-start(bf16[64,2304]{1,0:T(8,128)(2,1)S(1)} %get-tuple-element.102), channel_id=1, source_target_pairs={{0,1},{1,0},{2,3},{3,2},{4,5},{5,4},{6,7},{7,6},{8,9},{9,8},{10,11... | collective-permute-start | bytes 884744 | tf_op jit(solution)/shard_map/ppermute | solution.py:531
  40.4 0.7 %collective-permute-start.13 = (bf16[64,2304]{1,0:T(8,128)(2,1)S(1)}, bf16[64,2304]{1,0:T(8,128)(2,1)S(1)}, u32[]{:S(2)}, u32[]{:S(2)}) collective-permute-start(bf16[64,2304]{1,0:T(8,128)(2,1)S(1)} %get-tuple-element.103), channel_id=1, source_target_pairs={{1,2},{2,1},{5,6},{6,5},{9,10},{10,9},{13,14},{14,13},{17,18},{18,... | collective-permute-start | bytes 884744 | tf_op jit(solution)/shard_map/ppermute | solution.py:532
  41.1 5.7 %collective-permute-start.14 = (bf16[64,2304]{1,0:T(8,128)(2,1)S(1)}, bf16[64,2304]{1,0:T(8,128)(2,1)S(1)}, u32[]{:S(2)}, u32[]{:S(2)}) collective-permute-start(bf16[64,2304]{1,0:T(8,128)(2,1)S(1)} %get-tuple-element.103), channel_id=1, source_target_pairs={{0,2},{3,1},{4,6},{7,5},{8,10},{11,9},{12,14},{15,13},{16,18},{19,... | collective-permute-start | bytes 884744 | tf_op jit(solution)/shard_map/ppermute | solution.py:533
  46.8 1.4 %collective-permute-done.12 = bf16[64,2304]{1,0:T(8,128)(2,1)S(1)} collective-permute-done((bf16[64,2304]{1,0:T(8,128)(2,1)S(1)}, bf16[64,2304]{1,0:T(8,128)(2,1)S(1)}, u32[]{:S(2)}, u32[]{:S(2)}) %collective-permute-start.12) | collective-permute-done | bytes 294944 | tf_op jit(solution)/shard_map/ppermute | solution.py:531
  48.2 0.1 fusion.6
  48.3 1.8 %collective-permute-start.15 = (bf16[64,2304]{1,0:T(8,128)(2,1)S(1)}, bf16[64,2304]{1,0:T(8,128)(2,1)S(1)}, u32[]{:S(2)}, u32[]{:S(2)}) collective-permute-start(bf16[64,2304]{1,0:T(8,128)(2,1)S(1)} %fusion.6), channel_id=1, source_target_pairs={{0,1},{3,2},{1,3},{2,0},{4,5},{7,6},{5,7},{6,4},{8,9},{11,10},{9,1... | collective-permute-start | bytes 884744 | tf_op jit(solution)/shard_map/ppermute | solution.py:535
  50.1 0.0 collective-permute-done.13
  50.1 4.1 %collective-permute-done.14 = bf16[64,2304]{1,0:T(8,128)(2,1)S(1)} collective-permute-done((bf16[64,2304]{1,0:T(8,128)(2,1)S(1)}, bf16[64,2304]{1,0:T(8,128)(2,1)S(1)}, u32[]{:S(2)}, u32[]{:S(2)}) %collective-permute-start.14) | collective-permute-done | bytes 294944 | tf_op jit(solution)/shard_map/ppermute | solution.py:533
  54.2 10.7 %collective-permute-done.15 = bf16[64,2304]{1,0:T(8,128)(2,1)S(1)} collective-permute-done((bf16[64,2304]{1,0:T(8,128)(2,1)S(1)}, bf16[64,2304]{1,0:T(8,128)(2,1)S(1)}, u32[]{:S(2)}, u32[]{:S(2)}) %collective-permute-start.15) | collective-permute-done | bytes 294944 | tf_op jit(solution)/shard_map/ppermute | solution.py:535
  64.9 0.9 %fusion.4 = bf16[64,2304]{1,0:T(8,128)(2,1)} fusion(f32[64,2304]{1,0:T(8,128)S(1)} %get-tuple-element.101, bf16[64,2304]{1,0:T(8,128)(2,1)S(1)} %collective-permute-done.12, bf16[64,2304]{1,0:T(8,128)(2,1)S(1)} %collective-permute-done.15, bf16[64,2304]{1,0:T(8,128)(2,1)S(1)} %collective-permute-done.14, bf16[64,2304]{1,0:T(8,128)(2,1)S(1)} %collective-permute-done.13, ...), kind=kLoop, calls=%fused_computation.6 | loop fusion | flops 1474560 | bytes 2064385 | tf_op jit(solution)/shard_map/convert_element_type | solution.py:545
  (1 shorter events, 0.0 us)
Async XLA Ops:
  0.8 7.4 %collective-permute-start = (bf16[3,16,1024]{2,1,0:T(8,128)(2,1)S(1)}, bf16[3,16,1024]{2,1,0:T(8,128)(2,1)S(1)}, u32[]{:S(2)}, u32[]{:S(2)}) collective-permute-start(bf16[3,16,1024]{2,1,0:T(8,128)(2,1)S(1)} %shard_map.91), channel_id=1, source_target_pairs={{0,4},{4,8},{8,12},{12,16},{16,20},{20,24},{24,28},{1,5},{5,9},{9,... | collective-permute-start | bytes 294920 | tf_op jit(solution)/shard_map/ppermute | solution.py:381
  13.6 7.0 %collective-permute-start.1 = (bf16[272,128]{1,0:T(8,128)(2,1)S(1)}, bf16[272,128]{1,0:T(8,128)(2,1)S(1)}, u32[]{:S(2)}, u32[]{:S(2)}) collective-permute-start(bf16[272,128]{1,0:T(8,128)(2,1)S(1)} %get-tuple-element.58), channel_id=1, source_target_pairs={{0,24},{4,28},{8,16},{12,20},{16,8},{20,12},{24,0},{28,4},{1,25},{... | collective-permute-start | bytes 208904 | tf_op jit(solution)/shard_map/ppermute | solution.py:426
  17.2 4.9 %collective-permute-start.2 = (bf16[272,128]{1,0:T(8,128)(2,1)S(1)}, bf16[272,128]{1,0:T(8,128)(2,1)S(1)}, u32[]{:S(2)}, u32[]{:S(2)}) collective-permute-start(bf16[272,128]{1,0:T(8,128)(2,1)S(1)} %get-tuple-element.59), channel_id=1, source_target_pairs={{0,28},{4,24},{8,20},{12,16},{16,12},{20,8},{24,4},{28,0},{1,29},{... | collective-permute-start | bytes 208904 | tf_op jit(solution)/shard_map/ppermute | solution.py:426
  18.6 6.0 %collective-permute-start.3 = (bf16[272,128]{1,0:T(8,128)(2,1)S(1)}, bf16[272,128]{1,0:T(8,128)(2,1)S(1)}, u32[]{:S(2)}, u32[]{:S(2)}) collective-permute-start(bf16[272,128]{1,0:T(8,128)(2,1)S(1)} %get-tuple-element.60), channel_id=1, source_target_pairs={{0,8},{4,12},{8,0},{12,4},{16,24},{20,28},{24,16},{28,20},{1,9},{5... | collective-permute-start | bytes 208904 | tf_op jit(solution)/shard_map/ppermute | solution.py:426
  20.1 4.5 %collective-permute-start.4 = (bf16[272,128]{1,0:T(8,128)(2,1)S(1)}, bf16[272,128]{1,0:T(8,128)(2,1)S(1)}, u32[]{:S(2)}, u32[]{:S(2)}) collective-permute-start(bf16[272,128]{1,0:T(8,128)(2,1)S(1)} %get-tuple-element.61), channel_id=1, source_target_pairs={{0,12},{4,8},{8,4},{12,0},{16,28},{20,24},{24,20},{28,16},{1,13},{... | collective-permute-start | bytes 208904 | tf_op jit(solution)/shard_map/ppermute | solution.py:426
  20.1 5.1 %collective-permute-start.5 = (bf16[272,128]{1,0:T(8,128)(2,1)S(1)}, bf16[272,128]{1,0:T(8,128)(2,1)S(1)}, u32[]{:S(2)}, u32[]{:S(2)}) collective-permute-start(bf16[272,128]{1,0:T(8,128)(2,1)S(1)} %get-tuple-element.62), channel_id=1, source_target_pairs={{0,16},{4,20},{8,24},{12,28},{16,0},{20,4},{24,8},{28,12},{1,17},{... | collective-permute-start | bytes 208904 | tf_op jit(solution)/shard_map/ppermute | solution.py:426
  20.6 5.2 %collective-permute-start.6 = (bf16[272,128]{1,0:T(8,128)(2,1)S(1)}, bf16[272,128]{1,0:T(8,128)(2,1)S(1)}, u32[]{:S(2)}, u32[]{:S(2)}) collective-permute-start(bf16[272,128]{1,0:T(8,128)(2,1)S(1)} %get-tuple-element.63), channel_id=1, source_target_pairs={{0,20},{4,16},{8,28},{12,24},{16,4},{20,0},{24,12},{28,8},{1,21},{... | collective-permute-start | bytes 208904 | tf_op jit(solution)/shard_map/ppermute | solution.py:426
  22.1 3.8 %collective-permute-start.7 = (bf16[272,128]{1,0:T(8,128)(2,1)S(1)}, bf16[272,128]{1,0:T(8,128)(2,1)S(1)}, u32[]{:S(2)}, u32[]{:S(2)}) collective-permute-start(bf16[272,128]{1,0:T(8,128)(2,1)S(1)} %get-tuple-element.64), channel_id=1, source_target_pairs={{0,4},{4,0},{8,12},{12,8},{16,20},{20,16},{24,28},{28,24},{1,5},{5... | collective-permute-start | bytes 208904 | tf_op jit(solution)/shard_map/ppermute | solution.py:426
  26.8 5.9 %collective-permute-start.10 = (bf16[2,128,128]{2,1,0:T(8,128)(2,1)S(1)}, bf16[2,128,128]{2,1,0:T(8,128)(2,1)S(1)}, u32[]{:S(2)}, u32[]{:S(2)}) collective-permute-start(bf16[2,128,128]{2,1,0:T(8,128)(2,1)S(1)} %get-tuple-element.88), channel_id=1, source_target_pairs={{0,24},{4,28},{8,16},{12,20},{16,8},{20,12},{24,0},{28,4},{1,25},{... | collective-permute-start | bytes 196616 | tf_op jit(solution)/shard_map/ppermute | solution.py:468
  28.0 5.1 %collective-permute-start.8 = (bf16[2,128,128]{2,1,0:T(8,128)(2,1)S(1)}, bf16[2,128,128]{2,1,0:T(8,128)(2,1)S(1)}, u32[]{:S(2)}, u32[]{:S(2)}) collective-permute-start(bf16[2,128,128]{2,1,0:T(8,128)(2,1)S(1)} %get-tuple-element.86), channel_id=1, source_target_pairs={{0,8},{4,12},{8,0},{12,4},{16,24},{20,28},{24,16},{28,20},{1,9},{5... | collective-permute-start | bytes 196616 | tf_op jit(solution)/shard_map/ppermute | solution.py:468
  29.9 4.3 %collective-permute-start.9 = (bf16[2,128,128]{2,1,0:T(8,128)(2,1)S(1)}, bf16[2,128,128]{2,1,0:T(8,128)(2,1)S(1)}, u32[]{:S(2)}, u32[]{:S(2)}) collective-permute-start(bf16[2,128,128]{2,1,0:T(8,128)(2,1)S(1)} %get-tuple-element.87), channel_id=1, source_target_pairs={{0,16},{4,20},{8,24},{12,28},{16,0},{20,4},{24,8},{28,12},{1,17},{... | collective-permute-start | bytes 196616 | tf_op jit(solution)/shard_map/ppermute | solution.py:468
  34.1 2.0 %collective-permute-start.11 = (bf16[4,128,128]{2,1,0:T(8,128)(2,1)S(1)}, bf16[4,128,128]{2,1,0:T(8,128)(2,1)S(1)}, u32[]{:S(2)}, u32[]{:S(2)}) collective-permute-start(bf16[4,128,128]{2,1,0:T(8,128)(2,1)S(1)} %shard_map.97), channel_id=1, source_target_pairs={{0,4},{4,0},{8,12},{12,8},{16,20},{20,16},{24,28},{28,24},{1,5},{5... | collective-permute-start | bytes 393224 | tf_op jit(solution)/shard_map/ppermute | solution.py:477
  38.7 9.5 %collective-permute-start.12 = (bf16[64,2304]{1,0:T(8,128)(2,1)S(1)}, bf16[64,2304]{1,0:T(8,128)(2,1)S(1)}, u32[]{:S(2)}, u32[]{:S(2)}) collective-permute-start(bf16[64,2304]{1,0:T(8,128)(2,1)S(1)} %get-tuple-element.102), channel_id=1, source_target_pairs={{0,1},{1,0},{2,3},{3,2},{4,5},{5,4},{6,7},{7,6},{8,9},{9,8},{10,11... | collective-permute-start | bytes 884744 | tf_op jit(solution)/shard_map/ppermute | solution.py:531
  40.4 9.7 %collective-permute-start.13 = (bf16[64,2304]{1,0:T(8,128)(2,1)S(1)}, bf16[64,2304]{1,0:T(8,128)(2,1)S(1)}, u32[]{:S(2)}, u32[]{:S(2)}) collective-permute-start(bf16[64,2304]{1,0:T(8,128)(2,1)S(1)} %get-tuple-element.103), channel_id=1, source_target_pairs={{1,2},{2,1},{5,6},{6,5},{9,10},{10,9},{13,14},{14,13},{17,18},{18,... | collective-permute-start | bytes 884744 | tf_op jit(solution)/shard_map/ppermute | solution.py:532
  41.1 13.1 %collective-permute-start.14 = (bf16[64,2304]{1,0:T(8,128)(2,1)S(1)}, bf16[64,2304]{1,0:T(8,128)(2,1)S(1)}, u32[]{:S(2)}, u32[]{:S(2)}) collective-permute-start(bf16[64,2304]{1,0:T(8,128)(2,1)S(1)} %get-tuple-element.103), channel_id=1, source_target_pairs={{0,2},{3,1},{4,6},{7,5},{8,10},{11,9},{12,14},{15,13},{16,18},{19,... | collective-permute-start | bytes 884744 | tf_op jit(solution)/shard_map/ppermute | solution.py:533
  48.3 16.6 %collective-permute-start.15 = (bf16[64,2304]{1,0:T(8,128)(2,1)S(1)}, bf16[64,2304]{1,0:T(8,128)(2,1)S(1)}, u32[]{:S(2)}, u32[]{:S(2)}) collective-permute-start(bf16[64,2304]{1,0:T(8,128)(2,1)S(1)} %fusion.6), channel_id=1, source_target_pairs={{0,1},{3,2},{1,3},{2,0},{4,5},{7,6},{5,7},{6,4},{8,9},{11,10},{9,1... | collective-permute-start | bytes 884744 | tf_op jit(solution)/shard_map/ppermute | solution.py:535

commit v6 on v5

--- a/solution.py
+++ b/solution.py
@@ -503,7 +503,7 @@
         )
     else:
         owners = [lambda z, d=d: lax.rem(z + d, parts) for d in range(parts)]
-    half = 2 * (model // 3)
+    half = 8 * (model // 9)
     early = call(
         fetch_kernel, (1,), [anywhere], here, kept((width, half), BF16),
         [pltpu.SemaphoreType.DMA], (0, width * model * 2), LIMIT, 0, source,

time: 66.2 us -> 66 us (level)
  no operation moved by 1% of the time
where the time goes in v6:
time: 66 us; the launch traced here: 65.6 us
  starting transfers between devices  24.4 us (37%)
  Pallas kernels  21.1 us (32%)
  waiting for transfers between devices  19 us (29%)
  other arithmetic  0.99 us (2%)
    pallas_call x9, Pallas kernels, call(): pl.pallas_call(kernel, grid_spec=pltpu.PrefetchScalarGridSpec(num_scalar_...  21.1 us
    ppermute x1, waiting for transfers between devices, shards(): joined = lax.ppermute(joined, 'head', [(0, 1), (3, 2), (1, 3), (2, 0)])  10.7 us
    ppermute x7, starting transfers between devices, exchange(): lax.ppermute(blocks[m], 'seq', [(i, i ^ m) for i in range(ranks)])  8.57 us
    ppermute x1, starting transfers between devices, shards(): skipped = lax.ppermute(inward, 'head', [(0, 2), (3, 1)])  5.74 us
    ppermute x1, waiting for transfers between devices, shards(): skipped = lax.ppermute(inward, 'head', [(0, 2), (3, 1)])  4.12 us
    ppermute x3, starting transfers between devices, shards(): lax.ppermute(states[d], 'seq', [(i, i ^ 2 * d) for i in range(ranks)])  3.55 us
    ppermute x1, starting transfers between devices, shards(): rims = lax.ppermute(rims, 'seq', [(i, i + 1) for i in range(ranks - 1)])  2.35 us
    ppermute x1, starting transfers between devices, shards(): joined = lax.ppermute(joined, 'head', [(0, 1), (3, 2), (1, 3), (2, 0)])  1.77 us
  transfers between devices with their start and end apart: 16, of which 8 were waited for; matrix products, arithmetic and copies ran while one was open for 0% of the time, Pallas kernels for 18%

profile of v6, /device:TPU:0, one launch (start us, length us, event | category | flops | bytes accessed | tf_op | source)
XLA Modules:
  0.0 65.6 jit_solution(14340700248600227685)
XLA Ops:
  0.0 0.8 %shard_map.91 = bf16[3,16,1024]{2,1,0:T(8,128)(2,1)S(1)} custom-call(bf16[256,1024]{1,0:T(8,128)(2,1)} %query.5, bf16[256,1024]{1,0:T(8,128)(2,1)} %key.5, bf16[256,1024]{1,0:T(8,128)(2,1)} %value.5), custom_call_target="tpu_custom_call" | custom-call | bytes 196608 | tf_op jit(solution)/shard_map/pallas_call | solution.py:340
  0.8 2.4 %collective-permute-start = (bf16[3,16,1024]{2,1,0:T(8,128)(2,1)S(1)}, bf16[3,16,1024]{2,1,0:T(8,128)(2,1)S(1)}, u32[]{:S(2)}, u32[]{:S(2)}) collective-permute-start(bf16[3,16,1024]{2,1,0:T(8,128)(2,1)S(1)} %shard_map.91), channel_id=1, source_target_pairs={{0,4},{4,8},{8,12},{12,16},{16,20},{20,24},{24,28},{1,5},{5,9},{9,... | collective-permute-start | bytes 294920 | tf_op jit(solution)/shard_map/ppermute | solution.py:381
  3.2 5.1 %shard_map.92 = (f32[8,256,128]{2,1,0:T(8,128)S(1)}, f32[8,8,128]{2,1,0:T(8,128)S(1)}, f32[8,128,256]{2,1,0:T(8,128)S(1)}, bf16[128,1024]{1,0:T(8,128)(2,1)S(1)}) custom-call(bf16[256,1024]{1,0:T(8,128)(2,1)} %key.5, bf16[256,1024]{1,0:T(8,128)(2,1)} %value.5, bf16[256,1024]{1,0:T(8,128)(2,1)} %gate.7, f32[8,256]{1,0:T(8,128)} %bitcast.3, ...), custom_call_target="tpu_custom_call" | custom-call | flops 800000000 | bytes 4194304 | tf_op jit(solution)/shard_map/pallas_call | solution.py:340
  8.2 0.0 collective-permute-done.rims
  8.3 5.4 %shard_map.93 = (bf16[8,256,128]{2,1,0:T(8,128)(2,1)S(1)}, f32[8,128,256]{2,1,0:T(8,128)S(1)}, bf16[128,1024]{1,0:T(8,128)(2,1)S(1)}, bf16[272,128]{1,0:T(8,128)...) custom-call(s32[1]{0:T(128)} %bitcast.where, ...), custom_call_target="tpu_custom_call" | custom-call | flops 800000000 | bytes 4194304 | tf_op jit(solution)/shard_map/pallas_call | solution.py:340
  13.6 3.5 %collective-permute-start.1 = (bf16[272,128]{1,0:T(8,128)(2,1)S(1)}, bf16[272,128]{1,0:T(8,128)(2,1)S(1)}, u32[]{:S(2)}, u32[]{:S(2)}) collective-permute-start(bf16[272,128]{1,0:T(8,128)(2,1)S(1)} %get-tuple-element.58), channel_id=1, source_target_pairs={{0,24},{4,28},{8,16},{12,20},{16,8},{20,12},{24,0},{28,4},{1,25},{... | collective-permute-start | bytes 208904 | tf_op jit(solution)/shard_map/ppermute | solution.py:426
  17.2 1.4 %collective-permute-start.2 = (bf16[272,128]{1,0:T(8,128)(2,1)S(1)}, bf16[272,128]{1,0:T(8,128)(2,1)S(1)}, u32[]{:S(2)}, u32[]{:S(2)}) collective-permute-start(bf16[272,128]{1,0:T(8,128)(2,1)S(1)} %get-tuple-element.59), channel_id=1, source_target_pairs={{0,28},{4,24},{8,20},{12,16},{16,12},{20,8},{24,4},{28,0},{1,29},{... | collective-permute-start | bytes 208904 | tf_op jit(solution)/shard_map/ppermute | solution.py:426
  18.6 1.5 %collective-permute-start.3 = (bf16[272,128]{1,0:T(8,128)(2,1)S(1)}, bf16[272,128]{1,0:T(8,128)(2,1)S(1)}, u32[]{:S(2)}, u32[]{:S(2)}) collective-permute-start(bf16[272,128]{1,0:T(8,128)(2,1)S(1)} %get-tuple-element.60), channel_id=1, source_target_pairs={{0,8},{4,12},{8,0},{12,4},{16,24},{20,28},{24,16},{28,20},{1,9},{5... | collective-permute-start | bytes 208904 | tf_op jit(solution)/shard_map/ppermute | solution.py:426
  20.1 0.0 collective-permute-start.4
  20.1 0.6 collective-permute-start.5
  20.6 0.0 collective-permute-done.1.refs_1_
  20.6 1.4 %collective-permute-start.6 = (bf16[272,128]{1,0:T(8,128)(2,1)S(1)}, bf16[272,128]{1,0:T(8,128)(2,1)S(1)}, u32[]{:S(2)}, u32[]{:S(2)}) collective-permute-start(bf16[272,128]{1,0:T(8,128)(2,1)S(1)} %get-tuple-element.63), channel_id=1, source_target_pairs={{0,20},{4,16},{8,28},{12,24},{16,4},{20,0},{24,12},{28,8},{1,21},{... | collective-permute-start | bytes 208904 | tf_op jit(solution)/shard_map/ppermute | solution.py:426
  22.1 0.0 collective-permute-done.2.refs_2_
  22.1 0.2 collective-permute-start.7
  22.2 2.3 %shard_map.94 = (f32[256,512]{1,0:T(8,128)S(1)}, bf16[256,512]{1,0:T(8,128)(2,1)S(1)}) custom-call(bf16[256,1024]{1,0:T(8,128)(2,1)} %query.5, bf16[256,1024]{1,0:T(8,128)(2,1)} %gate.7, bf16[3,16,1024]{2,1,0:T(8,128)(2,1)S(1)} %collective-permute-done.rims, bf16[4,1024]{1,0:T(4,128)(2,1)} %query_taps.3, f32[8,128,256]{2,1,0:T(8,128)S(1)} %get-tuple-element.65.first_solved, ...), custom_call_target="tpu_custom_call" | custom-call | flops 400000000 | bytes 2097152 | tf_op jit(solution)/shard_map/pallas_call | solution.py:340
  24.5 0.0 collective-permute-done.3.refs_3_
  24.5 0.1 collective-permute-done.4.refs_4_
  24.6 0.5 collective-permute-done.5.refs_5_
  25.1 0.8 %collective-permute-done.6.refs_6_ = bf16[272,128]{1,0:T(8,128)(2,1)S(1)} collective-permute-done((bf16[272,128]{1,0:T(8,128)(2,1)S(1)}, bf16[272,128]{1,0:T(8,128)(2,1)S(1)}, u32[]{:S(2)}, u32[]{:S(2)}) %collective-permute-start.6) | collective-permute-done | bytes 69664 | tf_op jit(solution)/shard_map/ppermute | solution.py:426
  25.9 0.0 collective-permute-done.7.refs_7_
  25.9 0.9 %shard_map.95 = (bf16[2,128,128]{2,1,0:T(8,128)(2,1)S(1)}, bf16[2,128,128]{2,1,0:T(8,128)(2,1)S(1)}, bf16[2,128,128]{2,1,0:T(8,128)(2,1)S(1)}, bf16[2,128,128]{2,1,0:T(8,128)(2,1)S(1)}) custom-call(s32[1]{0:T(128)} %bitcast.where, bf16[272,128]{1,0:T(8,128)(2,1)S(1)} %get-tuple-element.73.refs_0_, bf16[272,128]{1,0:T(8,128)(2,1)S(1)} %collective-permute-done.1.refs_1_, ...), custom_call_target="tpu_custom_call" | custom-call | flops 32000000 | bytes 1048576 | tf_op jit(solution)/shard_map/pallas_call | solution.py:340
  26.8 1.2 %collective-permute-start.10 = (bf16[2,128,128]{2,1,0:T(8,128)(2,1)S(1)}, bf16[2,128,128]{2,1,0:T(8,128)(2,1)S(1)}, u32[]{:S(2)}, u32[]{:S(2)}) collective-permute-start(bf16[2,128,128]{2,1,0:T(8,128)(2,1)S(1)} %get-tuple-element.88), channel_id=1, source_target_pairs={{0,24},{4,28},{8,16},{12,20},{16,8},{20,12},{24,0},{28,4},{1,25},{... | collective-permute-start | bytes 196616 | tf_op jit(solution)/shard_map/ppermute | solution.py:468
  28.0 1.9 %collective-permute-start.8 = (bf16[2,128,128]{2,1,0:T(8,128)(2,1)S(1)}, bf16[2,128,128]{2,1,0:T(8,128)(2,1)S(1)}, u32[]{:S(2)}, u32[]{:S(2)}) collective-permute-start(bf16[2,128,128]{2,1,0:T(8,128)(2,1)S(1)} %get-tuple-element.86), channel_id=1, source_target_pairs={{0,8},{4,12},{8,0},{12,4},{16,24},{20,28},{24,16},{28,20},{1,9},{5... | collective-permute-start | bytes 196616 | tf_op jit(solution)/shard_map/ppermute | solution.py:468
  29.9 0.5 collective-permute-start.9
  30.4 2.3 %shard_map.96 = (f32[256,512]{1,0:T(8,128)S(1)}, bf16[256,512]{1,0:T(8,128)(2,1)S(1)}) custom-call(bf16[256,1024]{1,0:T(8,128)(2,1)} %query.5, bf16[256,1024]{1,0:T(8,128)(2,1)} %gate.7, bf16[3,16,1024]{2,1,0:T(8,128)(2,1)S(1)} %collective-permute-done.rims, bf16[4,1024]{1,0:T(4,128)(2,1)} %query_taps.3, f32[8,128,256]{2,1,0:T(8,128)S(1)} %get-tuple-element.65.first_solved, ...), custom_call_target="tpu_custom_call" | custom-call | flops 400000000 | bytes 2097152 | tf_op jit(solution)/shard_map/pallas_call | solution.py:340
  32.6 0.0 collective-permute-done.10.refs_3_.rest_3_
  32.7 0.3 collective-permute-done.8.refs_1_.rest_1_
  33.0 1.1 %collective-permute-done.9.refs_2_.rest_2_ = bf16[2,128,128]{2,1,0:T(8,128)(2,1)S(1)} collective-permute-done((bf16[2,128,128]{2,1,0:T(8,128)(2,1)S(1)}, bf16[2,128,128]{2,1,0:T(8,128)(2,1)S(1)}, u32[]{:S(2)}, u32[]{:S(2)}) %collective-permute-start.9) | collective-permute-done | bytes 65568 | tf_op jit(solution)/shard_map/ppermute | solution.py:468
  34.1 0.1 collective-permute-start.11
  34.2 2.2 %shard_map.98.early = bf16[1024,2048]{1,0:T(8,128)(2,1)S(1)} custom-call(bf16[1024,2304]{1,0:T(8,128)(2,1)} %matrix.4), custom_call_target="tpu_custom_call" | custom-call | bytes 4718592 | tf_op jit(solution)/shard_map/pallas_call | solution.py:340
  36.4 0.0 collective-permute-done.11.rest_4_
  36.4 2.2 %shard_map.99 = (f32[64,2304]{1,0:T(8,128)S(1)}, bf16[64,2304]{1,0:T(8,128)(2,1)S(1)}, bf16[64,2304]{1,0:T(8,128)(2,1)S(1)}, bf16[64,2304]{1,0:T(8,128)(2,1)S(1)}) custom-call(s32[1]{0:T(128)} %bitcast.where, s32[1]{0:T(128)} %bitcast.1.mine, f32[256,512]{1,0:T(8,128)S(1)} %get-tuple-element.72.direct_one, f32[256,512]{1,0:T(8,128)S(1)} %get-tuple-element.92.direct_two, ...), custom_call_target="tpu_custom_call" | custom-call | flops 1207959552 | bytes 4718592 | tf_op jit(solution)/shard_map/pallas_call | solution.py:340
  38.6 1.6 %collective-permute-start.12 = (bf16[64,2304]{1,0:T(8,128)(2,1)S(1)}, bf16[64,2304]{1,0:T(8,128)(2,1)S(1)}, u32[]{:S(2)}, u32[]{:S(2)}) collective-permute-start(bf16[64,2304]{1,0:T(8,128)(2,1)S(1)} %get-tuple-element.102), channel_id=1, source_target_pairs={{0,1},{1,0},{2,3},{3,2},{4,5},{5,4},{6,7},{7,6},{8,9},{9,8},{10,11... | collective-permute-start | bytes 884744 | tf_op jit(solution)/shard_map/ppermute | solution.py:531
  40.2 0.7 %collective-permute-start.13 = (bf16[64,2304]{1,0:T(8,128)(2,1)S(1)}, bf16[64,2304]{1,0:T(8,128)(2,1)S(1)}, u32[]{:S(2)}, u32[]{:S(2)}) collective-permute-start(bf16[64,2304]{1,0:T(8,128)(2,1)S(1)} %get-tuple-element.103), channel_id=1, source_target_pairs={{1,2},{2,1},{5,6},{6,5},{9,10},{10,9},{13,14},{14,13},{17,18},{18,... | collective-permute-start | bytes 884744 | tf_op jit(solution)/shard_map/ppermute | solution.py:532
  40.9 5.7 %collective-permute-start.14 = (bf16[64,2304]{1,0:T(8,128)(2,1)S(1)}, bf16[64,2304]{1,0:T(8,128)(2,1)S(1)}, u32[]{:S(2)}, u32[]{:S(2)}) collective-permute-start(bf16[64,2304]{1,0:T(8,128)(2,1)S(1)} %get-tuple-element.103), channel_id=1, source_target_pairs={{0,2},{3,1},{4,6},{7,5},{8,10},{11,9},{12,14},{15,13},{16,18},{19,... | collective-permute-start | bytes 884744 | tf_op jit(solution)/shard_map/ppermute | solution.py:533
  46.7 1.4 %collective-permute-done.12 = bf16[64,2304]{1,0:T(8,128)(2,1)S(1)} collective-permute-done((bf16[64,2304]{1,0:T(8,128)(2,1)S(1)}, bf16[64,2304]{1,0:T(8,128)(2,1)S(1)}, u32[]{:S(2)}, u32[]{:S(2)}) %collective-permute-start.12) | collective-permute-done | bytes 294944 | tf_op jit(solution)/shard_map/ppermute | solution.py:531
  48.1 0.1 fusion.6
  48.2 1.8 %collective-permute-start.15 = (bf16[64,2304]{1,0:T(8,128)(2,1)S(1)}, bf16[64,2304]{1,0:T(8,128)(2,1)S(1)}, u32[]{:S(2)}, u32[]{:S(2)}) collective-permute-start(bf16[64,2304]{1,0:T(8,128)(2,1)S(1)} %fusion.6), channel_id=1, source_target_pairs={{0,1},{3,2},{1,3},{2,0},{4,5},{7,6},{5,7},{6,4},{8,9},{11,10},{9,1... | collective-permute-start | bytes 884744 | tf_op jit(solution)/shard_map/ppermute | solution.py:535
  49.9 0.0 collective-permute-done.13
  49.9 4.1 %collective-permute-done.14 = bf16[64,2304]{1,0:T(8,128)(2,1)S(1)} collective-permute-done((bf16[64,2304]{1,0:T(8,128)(2,1)S(1)}, bf16[64,2304]{1,0:T(8,128)(2,1)S(1)}, u32[]{:S(2)}, u32[]{:S(2)}) %collective-permute-start.14) | collective-permute-done | bytes 294944 | tf_op jit(solution)/shard_map/ppermute | solution.py:533
  54.0 10.7 %collective-permute-done.15 = bf16[64,2304]{1,0:T(8,128)(2,1)S(1)} collective-permute-done((bf16[64,2304]{1,0:T(8,128)(2,1)S(1)}, bf16[64,2304]{1,0:T(8,128)(2,1)S(1)}, u32[]{:S(2)}, u32[]{:S(2)}) %collective-permute-start.15) | collective-permute-done | bytes 294944 | tf_op jit(solution)/shard_map/ppermute | solution.py:535
  64.7 0.9 %fusion.4 = bf16[64,2304]{1,0:T(8,128)(2,1)} fusion(f32[64,2304]{1,0:T(8,128)S(1)} %get-tuple-element.101, bf16[64,2304]{1,0:T(8,128)(2,1)S(1)} %collective-permute-done.12, bf16[64,2304]{1,0:T(8,128)(2,1)S(1)} %collective-permute-done.15, bf16[64,2304]{1,0:T(8,128)(2,1)S(1)} %collective-permute-done.14, bf16[64,2304]{1,0:T(8,128)(2,1)S(1)} %collective-permute-done.13, ...), kind=kLoop, calls=%fused_computation.6 | loop fusion | flops 1474560 | bytes 2064385 | tf_op jit(solution)/shard_map/convert_element_type | solution.py:545
  (1 shorter events, 0.0 us)
Async XLA Ops:
  0.8 7.4 %collective-permute-start = (bf16[3,16,1024]{2,1,0:T(8,128)(2,1)S(1)}, bf16[3,16,1024]{2,1,0:T(8,128)(2,1)S(1)}, u32[]{:S(2)}, u32[]{:S(2)}) collective-permute-start(bf16[3,16,1024]{2,1,0:T(8,128)(2,1)S(1)} %shard_map.91), channel_id=1, source_target_pairs={{0,4},{4,8},{8,12},{12,16},{16,20},{20,24},{24,28},{1,5},{5,9},{9,... | collective-permute-start | bytes 294920 | tf_op jit(solution)/shard_map/ppermute | solution.py:381
  13.6 7.0 %collective-permute-start.1 = (bf16[272,128]{1,0:T(8,128)(2,1)S(1)}, bf16[272,128]{1,0:T(8,128)(2,1)S(1)}, u32[]{:S(2)}, u32[]{:S(2)}) collective-permute-start(bf16[272,128]{1,0:T(8,128)(2,1)S(1)} %get-tuple-element.58), channel_id=1, source_target_pairs={{0,24},{4,28},{8,16},{12,20},{16,8},{20,12},{24,0},{28,4},{1,25},{... | collective-permute-start | bytes 208904 | tf_op jit(solution)/shard_map/ppermute | solution.py:426
  17.2 4.9 %collective-permute-start.2 = (bf16[272,128]{1,0:T(8,128)(2,1)S(1)}, bf16[272,128]{1,0:T(8,128)(2,1)S(1)}, u32[]{:S(2)}, u32[]{:S(2)}) collective-permute-start(bf16[272,128]{1,0:T(8,128)(2,1)S(1)} %get-tuple-element.59), channel_id=1, source_target_pairs={{0,28},{4,24},{8,20},{12,16},{16,12},{20,8},{24,4},{28,0},{1,29},{... | collective-permute-start | bytes 208904 | tf_op jit(solution)/shard_map/ppermute | solution.py:426
  18.6 6.0 %collective-permute-start.3 = (bf16[272,128]{1,0:T(8,128)(2,1)S(1)}, bf16[272,128]{1,0:T(8,128)(2,1)S(1)}, u32[]{:S(2)}, u32[]{:S(2)}) collective-permute-start(bf16[272,128]{1,0:T(8,128)(2,1)S(1)} %get-tuple-element.60), channel_id=1, source_target_pairs={{0,8},{4,12},{8,0},{12,4},{16,24},{20,28},{24,16},{28,20},{1,9},{5... | collective-permute-start | bytes 208904 | tf_op jit(solution)/shard_map/ppermute | solution.py:426
  20.1 4.5 %collective-permute-start.4 = (bf16[272,128]{1,0:T(8,128)(2,1)S(1)}, bf16[272,128]{1,0:T(8,128)(2,1)S(1)}, u32[]{:S(2)}, u32[]{:S(2)}) collective-permute-start(bf16[272,128]{1,0:T(8,128)(2,1)S(1)} %get-tuple-element.61), channel_id=1, source_target_pairs={{0,12},{4,8},{8,4},{12,0},{16,28},{20,24},{24,20},{28,16},{1,13},{... | collective-permute-start | bytes 208904 | tf_op jit(solution)/shard_map/ppermute | solution.py:426
  20.1 5.1 %collective-permute-start.5 = (bf16[272,128]{1,0:T(8,128)(2,1)S(1)}, bf16[272,128]{1,0:T(8,128)(2,1)S(1)}, u32[]{:S(2)}, u32[]{:S(2)}) collective-permute-start(bf16[272,128]{1,0:T(8,128)(2,1)S(1)} %get-tuple-element.62), channel_id=1, source_target_pairs={{0,16},{4,20},{8,24},{12,28},{16,0},{20,4},{24,8},{28,12},{1,17},{... | collective-permute-start | bytes 208904 | tf_op jit(solution)/shard_map/ppermute | solution.py:426
  20.6 5.2 %collective-permute-start.6 = (bf16[272,128]{1,0:T(8,128)(2,1)S(1)}, bf16[272,128]{1,0:T(8,128)(2,1)S(1)}, u32[]{:S(2)}, u32[]{:S(2)}) collective-permute-start(bf16[272,128]{1,0:T(8,128)(2,1)S(1)} %get-tuple-element.63), channel_id=1, source_target_pairs={{0,20},{4,16},{8,28},{12,24},{16,4},{20,0},{24,12},{28,8},{1,21},{... | collective-permute-start | bytes 208904 | tf_op jit(solution)/shard_map/ppermute | solution.py:426
  22.1 3.8 %collective-permute-start.7 = (bf16[272,128]{1,0:T(8,128)(2,1)S(1)}, bf16[272,128]{1,0:T(8,128)(2,1)S(1)}, u32[]{:S(2)}, u32[]{:S(2)}) collective-permute-start(bf16[272,128]{1,0:T(8,128)(2,1)S(1)} %get-tuple-element.64), channel_id=1, source_target_pairs={{0,4},{4,0},{8,12},{12,8},{16,20},{20,16},{24,28},{28,24},{1,5},{5... | collective-permute-start | bytes 208904 | tf_op jit(solution)/shard_map/ppermute | solution.py:426
  26.8 5.9 %collective-permute-start.10 = (bf16[2,128,128]{2,1,0:T(8,128)(2,1)S(1)}, bf16[2,128,128]{2,1,0:T(8,128)(2,1)S(1)}, u32[]{:S(2)}, u32[]{:S(2)}) collective-permute-start(bf16[2,128,128]{2,1,0:T(8,128)(2,1)S(1)} %get-tuple-element.88), channel_id=1, source_target_pairs={{0,24},{4,28},{8,16},{12,20},{16,8},{20,12},{24,0},{28,4},{1,25},{... | collective-permute-start | bytes 196616 | tf_op jit(solution)/shard_map/ppermute | solution.py:468
  28.0 5.1 %collective-permute-start.8 = (bf16[2,128,128]{2,1,0:T(8,128)(2,1)S(1)}, bf16[2,128,128]{2,1,0:T(8,128)(2,1)S(1)}, u32[]{:S(2)}, u32[]{:S(2)}) collective-permute-start(bf16[2,128,128]{2,1,0:T(8,128)(2,1)S(1)} %get-tuple-element.86), channel_id=1, source_target_pairs={{0,8},{4,12},{8,0},{12,4},{16,24},{20,28},{24,16},{28,20},{1,9},{5... | collective-permute-start | bytes 196616 | tf_op jit(solution)/shard_map/ppermute | solution.py:468
  29.9 4.3 %collective-permute-start.9 = (bf16[2,128,128]{2,1,0:T(8,128)(2,1)S(1)}, bf16[2,128,128]{2,1,0:T(8,128)(2,1)S(1)}, u32[]{:S(2)}, u32[]{:S(2)}) collective-permute-start(bf16[2,128,128]{2,1,0:T(8,128)(2,1)S(1)} %get-tuple-element.87), channel_id=1, source_target_pairs={{0,16},{4,20},{8,24},{12,28},{16,0},{20,4},{24,8},{28,12},{1,17},{... | collective-permute-start | bytes 196616 | tf_op jit(solution)/shard_map/ppermute | solution.py:468
  34.1 2.3 %collective-permute-start.11 = (bf16[4,128,128]{2,1,0:T(8,128)(2,1)S(1)}, bf16[4,128,128]{2,1,0:T(8,128)(2,1)S(1)}, u32[]{:S(2)}, u32[]{:S(2)}) collective-permute-start(bf16[4,128,128]{2,1,0:T(8,128)(2,1)S(1)} %shard_map.97), channel_id=1, source_target_pairs={{0,4},{4,0},{8,12},{12,8},{16,20},{20,16},{24,28},{28,24},{1,5},{5... | collective-permute-start | bytes 393224 | tf_op jit(solution)/shard_map/ppermute | solution.py:477
  38.6 9.5 %collective-permute-start.12 = (bf16[64,2304]{1,0:T(8,128)(2,1)S(1)}, bf16[64,2304]{1,0:T(8,128)(2,1)S(1)}, u32[]{:S(2)}, u32[]{:S(2)}) collective-permute-start(bf16[64,2304]{1,0:T(8,128)(2,1)S(1)} %get-tuple-element.102), channel_id=1, source_target_pairs={{0,1},{1,0},{2,3},{3,2},{4,5},{5,4},{6,7},{7,6},{8,9},{9,8},{10,11... | collective-permute-start | bytes 884744 | tf_op jit(solution)/shard_map/ppermute | solution.py:531
  40.2 9.7 %collective-permute-start.13 = (bf16[64,2304]{1,0:T(8,128)(2,1)S(1)}, bf16[64,2304]{1,0:T(8,128)(2,1)S(1)}, u32[]{:S(2)}, u32[]{:S(2)}) collective-permute-start(bf16[64,2304]{1,0:T(8,128)(2,1)S(1)} %get-tuple-element.103), channel_id=1, source_target_pairs={{1,2},{2,1},{5,6},{6,5},{9,10},{10,9},{13,14},{14,13},{17,18},{18,... | collective-permute-start | bytes 884744 | tf_op jit(solution)/shard_map/ppermute | solution.py:532
  40.9 13.1 %collective-permute-start.14 = (bf16[64,2304]{1,0:T(8,128)(2,1)S(1)}, bf16[64,2304]{1,0:T(8,128)(2,1)S(1)}, u32[]{:S(2)}, u32[]{:S(2)}) collective-permute-start(bf16[64,2304]{1,0:T(8,128)(2,1)S(1)} %get-tuple-element.103), channel_id=1, source_target_pairs={{0,2},{3,1},{4,6},{7,5},{8,10},{11,9},{12,14},{15,13},{16,18},{19,... | collective-permute-start | bytes 884744 | tf_op jit(solution)/shard_map/ppermute | solution.py:533
  48.2 16.6 %collective-permute-start.15 = (bf16[64,2304]{1,0:T(8,128)(2,1)S(1)}, bf16[64,2304]{1,0:T(8,128)(2,1)S(1)}, u32[]{:S(2)}, u32[]{:S(2)}) collective-permute-start(bf16[64,2304]{1,0:T(8,128)(2,1)S(1)} %fusion.6), channel_id=1, source_target_pairs={{0,1},{3,2},{1,3},{2,0},{4,5},{7,6},{5,7},{6,4},{8,9},{11,10},{9,1... | collective-permute-start | bytes 884744 | tf_op jit(solution)/shard_map/ppermute | solution.py:535
